TPU v7x, 32 devices: a whole 2x2x4 slice. The times are simulated.
32 devices in a mesh: sector: 8 (over y, x, core), term: 4 (over z).
Axes of the slice: x: 2, y: 2, z: 4, core: 2. Of those that a mesh axis runs over, the one named last changes fastest.
Arguments:
- x_start: float32 [8, 384, 384], P('sector', 'term'), may hold values from -6 to 6
- x_prev: float32 [8, 384, 384], P('sector', 'term'), may hold values from -6 to 6
- precond: float32 [8, 384, 384], P('sector', 'term'), may hold values from 0.5 to 6
- left_env: bfloat16 [256, 384, 384], P(('sector', 'term')), may hold values from -0.20412415 to 1.2041241
- right_env: bfloat16 [256, 384, 384], P(('sector', 'term')), may hold values from -0.20412415 to 1.2041241
- triples: int32 [640, 4], P(('sector', 'term')), may hold values from 0 to 63, as said below
- trip_count: int32 [8, 4], P('sector', 'term'), may hold values from 5 to 20, as said below
- term_coef: float32 [64], replicated, may hold values from 0.25 to 1
- lanczos_beta: float32 [3], replicated, may hold values from 0.3 to 1.2
- block_owner: int32 [8], replicated, may hold values from 0 to 7, each once
Outputs:
- final_vector: float32 [8, 384, 384], P('sector', 'term')
- rayleigh: float32 [3], replicated
Inputs may be any that keep to these rules, and one draw needn't show every extreme that they name: `triples`: Columns: a left slot below 8, a wavefunction block id below 8, a right slot below 8, an operator term below 64. `trip_count`: some device has exactly 20 live triples in every draw. `block_owner`: each sector index holds exactly one block.
All inputs are finite; a program needn't handle non-finite values.
Results may differ from a plain program's by a relative error of at most 0.006.
Values may be sent and summed in bfloat16 or wider, within the bound.
No kernel may reach another device: no remote copies, remote signals or barrier semaphores. Data moves between devices by JAX's collectives and lax.ppermute only.
A program may use at most 64 MiB of HBM per device.

v0:
```python
import functools
import math

import jax
import jax.numpy as jnp
from jax import lax
from jax.experimental import pallas as pl
from jax.experimental.pallas import tpu as pltpu
from jax.sharding import PartitionSpec as P


APPS = 3
EPSILON = 1e-06

F32 = jnp.float32
BF16 = jnp.bfloat16
SUBLANES = 8
HEAD = 16
LANES = 128

SCALARS = pl.BlockSpec(memory_space=pltpu.SMEM)
NEAR = pl.BlockSpec(memory_space=pltpu.VMEM)
FAR = pl.BlockSpec(memory_space=pltpu.HBM)
SMALL_CALL = pltpu.CompilerParams(vmem_limit_bytes=4 << 20)


def exchange(array, axis, flip):
    count = lax.axis_size(axis)
    return lax.ppermute(array, axis, [(i, i ^ flip) for i in range(count)])


def tree(parts):
    while len(parts) > 1:
        parts = [parts[i] + parts[i + 1] for i in range(0, len(parts), 2)]
    return parts[0]


def sum_term(values, term_count):
    flip = 1
    while flip < term_count:
        values = values + exchange(values, "term", flip)
        flip *= 2
    return values


def gather_ordered(rows, term_count):
    parts = [rows]
    for flip in range(1, term_count):
        parts.append(exchange(rows, "term", flip))
    me = lax.axis_index("term")
    ordered = []
    for index in range(term_count):
        chosen = parts[0]
        for flip in range(1, term_count):
            chosen = jnp.where((me ^ flip) == index, parts[flip], chosen)
        ordered.append(chosen)
    return jnp.concatenate(ordered, axis=0)


def over_term(array, term_count):
    parts = [array]
    for flip in range(1, term_count):
        parts.append(exchange(array, "term", flip))
    return parts


def over_chips(array, sectors):
    parts = [array]
    for flip in range(2, sectors, 2):
        parts.append(exchange(array, "sector", flip))
    return parts


def gather(pieces, sectors, term_count):
    if len(pieces) == 1:
        groups = [over_chips(gather_ordered(pieces[0], term_count), sectors)]
    else:
        main = jnp.concatenate(over_term(pieces[0], term_count))
        rest = jnp.concatenate(over_chips(pieces[1], sectors))
        groups = [over_chips(main, sectors), over_term(rest, term_count)]
    arrays = []
    for group in groups:
        arrays += group
        arrays += [exchange(array, "sector", 1) for array in group]
    return arrays


def main_rows(share):
    return share - share // 3 if share % (3 * HEAD) == 0 else share


def place_waves(wave, arrays, place, sectors, term_count):
    size = wave.shape[1]
    share = size // term_count
    cut = main_rows(share)
    chips = sectors // 2
    mains = arrays[:sectors]
    if len(arrays) == sectors:
        cut = share
    for core in range(2):
        for chip in range(chips):
            source = mains[core * chips + chip]
            slot = 2 * chip + core
            if cut == share:
                wave[slot] = source[...]
                continue
            for flip in range(term_count):
                start = pl.multiple_of((place[1] ^ flip) * share, HEAD)
                wave[slot, pl.ds(start, cut), :] = source[flip * cut : (flip + 1) * cut, :]
    left_over = share - cut
    for i, source in enumerate(arrays[sectors:]):
        core, flip = divmod(i, term_count)
        start = pl.multiple_of((place[1] ^ flip) * share + cut, HEAD)
        for chip in range(chips):
            rows = source[chip * left_over : (chip + 1) * left_over, :]
            wave[2 * chip + core, pl.ds(start, left_over), :] = rows


def fold(values):
    rows, columns = values.shape
    down = jnp.sum(values.reshape(rows // SUBLANES, SUBLANES, columns), axis=0)
    return tree_any([down[:, i : i + LANES] for i in range(0, columns, LANES)])


def tree_any(parts):
    total = parts[0]
    for part in parts[1:]:
        total = total + part
    return total


def plan_kernel(normaliser, triples, owner, live, coef, place, table, weights):
    for k in range(triples.shape[1]):
        table[0, k] = triples[0, k]
        table[1, k] = owner[triples[1, k]] ^ place[0]
        table[2, k] = triples[2, k]
        weights[k] = jnp.where(k < live[0, 0], coef[triples[3, k]], 0.0) * normaliser


def plan(normaliser, triples, owner, live, coef, place):
    slots = triples.shape[1]
    return pl.pallas_call(
        functools.partial(plan_kernel, normaliser),
        out_shape=[
            jax.ShapeDtypeStruct((3, slots), jnp.int32),
            jax.ShapeDtypeStruct((slots,), F32),
        ],
        in_specs=[SCALARS] * 5,
        out_specs=[SCALARS] * 2,
        name="plan",
        compiler_params=SMALL_CALL,
    )(triples, owner, live, coef, place)


def load_kernel(left, right, left_near, right_near, sems):
    copies = []
    for i, (far, near) in enumerate(((left, left_near), (right, right_near))):
        copies += [
            pltpu.make_async_copy(far.at[j], near.at[j], sems.at[i, j])
            for j in range(far.shape[0])
        ]
    for copy in copies:
        copy.start()
    for copy in copies:
        copy.wait()


def load(left, right):
    like = jax.ShapeDtypeStruct(left.shape, left.dtype)
    return pl.pallas_call(
        load_kernel,
        out_shape=[like, like],
        in_specs=[FAR] * 2,
        out_specs=[NEAR] * 2,
        scratch_shapes=[pltpu.SemaphoreType.DMA((2, left.shape[0]))],
        name="load",
        compiler_params=pltpu.CompilerParams(vmem_limit_bytes=12 << 20),
    )(left, right)


STATS = 3
PARTS = 3


def spread(values, columns):
    rows = lax.broadcasted_iota(jnp.int32, (HEAD, columns), 0)
    tile = jnp.zeros((HEAD, columns), F32)
    for i, value in enumerate(values):
        rest = value
        for part in range(PARTS):
            high = rest.astype(BF16).astype(F32)
            tile = jnp.where(rows == PARTS * i + part, high, tile)
            rest = rest - high
    return tile


def joined(head, i):
    row = PARTS * i
    return (head[row : row + 1] + head[row + 1 : row + 2]) + head[row + 2 : row + 3]


def apply_kernel(
    sectors,
    term_count,
    count,
    unroll,
    table,
    weights,
    place,
    left,
    right,
    overlap,
    square,
    *rest,
):
    arrays = rest[:count]
    chunks = rest[count : count + term_count]
    wave, total, halves, image = rest[count + term_count :]
    slots = weights.shape[0]
    size = left.shape[1]
    envs = right.shape[0]
    share = size // term_count
    for env in range(envs):
        total[env] = jnp.zeros((size, size), F32)
    place_waves(wave, arrays, place, sectors, term_count)

    def one(k):
        slot = table[2, k]
        total[slot] += weights[k] * jnp.dot(
            left[table[0, k]], wave[table[1, k]], preferred_element_type=F32
        )

    def step(i, carry):
        for u in range(unroll):
            one(i * unroll + u)
        return carry

    lax.fori_loop(0, slots // unroll, step, 0)
    for env in range(envs):
        columns = slice(env * size, (env + 1) * size)
        high = total[env].astype(BF16)
        halves[:size, columns] = high
        halves[size:, columns] = (total[env] - high.astype(F32)).astype(BF16)
    flat = right[...].reshape(envs * size, size)
    both = jnp.dot(halves[...], flat, preferred_element_type=F32)
    image[...] = both[:size] + both[size:]
    inner = jnp.sum(fold(wave[0].astype(F32) * image[...]), keepdims=True)
    head = spread(
        (
            inner,
            jnp.sum(overlap[...], keepdims=True),
            jnp.sum(square[...], keepdims=True),
        ),
        LANES,
    )
    for flip in range(term_count):
        start = pl.multiple_of((place[1] ^ flip) * share, SUBLANES)
        kind = chunks[flip].dtype
        chunks[flip][:HEAD] = head.astype(kind)
        for i in range(size // LANES):
            slab = image[pl.ds(start, share), i * LANES : (i + 1) * LANES]
            chunks[flip][HEAD + i * share : HEAD + (i + 1) * share] = slab.astype(kind)


def apply_local(
    table, weights, place, left, right, overlap, square, arrays, sectors, term_count
):
    slots = weights.shape[0]
    envs, size, _ = left.shape
    share = size // term_count
    unroll = next(u for u in (4, 2, 1) if slots % u == 0)
    kinds = [F32] + [BF16] * (term_count - 1)
    return pl.pallas_call(
        functools.partial(apply_kernel, sectors, term_count, len(arrays), unroll),
        out_shape=[jax.ShapeDtypeStruct((HEAD + size // LANES * share, LANES), kind) for kind in kinds],
        in_specs=[SCALARS] * 3 + [NEAR] * (4 + len(arrays)),
        out_specs=[NEAR] * term_count,
        scratch_shapes=[
            pltpu.VMEM((sectors, size, size), BF16),
            pltpu.VMEM((envs, size, size), F32),
            pltpu.VMEM((2 * size, envs * size), BF16),
            pltpu.VMEM((size, size), F32),
        ],
        name="apply_triples",
        cost_estimate=pl.CostEstimate(
            flops=2 * size**3 * (slots + 2 * envs),
            bytes_accessed=2 * size * size * (2 * envs + sectors + 1),
            transcendentals=0,
        ),
        compiler_params=pltpu.CompilerParams(vmem_limit_bytes=18 << 20),
    )(table, weights, place, left, right, overlap, square, *arrays)


def add_chunks(chunks, applied):
    share = applied.shape[0]
    for i in range(applied.shape[1] // LANES):
        rows = slice(HEAD + i * share, HEAD + (i + 1) * share)
        slab = tree_any([chunk[rows, :].astype(F32) for chunk in chunks])
        applied[:, i * LANES : (i + 1) * LANES] = slab


def collect_kernel(count, *rest):
    chunks, (applied, stats) = rest[:count], rest[count:]
    add_chunks(chunks, applied)
    heads = [chunk[:HEAD, :].astype(F32) for chunk in chunks]
    rows = lax.broadcasted_iota(jnp.int32, (SUBLANES, LANES), 0)
    tile = jnp.zeros((SUBLANES, LANES), F32)
    for i in range(STATS):
        tile = jnp.where(rows == i, tree([joined(head, i) for head in heads]), tile)
    stats[...] = tile


def collect(chunks, shape):
    return pl.pallas_call(
        functools.partial(collect_kernel, len(chunks)),
        out_shape=[
            jax.ShapeDtypeStruct(shape, F32),
            jax.ShapeDtypeStruct((SUBLANES, LANES), F32),
        ],
        in_specs=[NEAR] * len(chunks),
        out_specs=[NEAR] * 2,
        name="collect",
        compiler_params=SMALL_CALL,
    )(*chunks)


def summed(sums):
    rows = sums.shape[0]
    return tree_any([sums[i : i + SUBLANES] for i in range(0, rows, SUBLANES)])


def first_kernel(rows, *out):
    *pieces, overlap, square = out
    held = rows[...]
    rounded = held.astype(BF16)
    store_pieces(pieces, rounded)
    overlap[...] = fold(held * rounded.astype(F32))
    square[...] = fold(held * held)


def store_pieces(pieces, rows):
    start = 0
    for piece in pieces:
        stop = start + piece.shape[0]
        piece[...] = rows[start:stop]
        start = stop


def piece_shapes(share, size):
    cut = main_rows(share)
    counts = (cut, share - cut) if cut < share else (share,)
    return [jax.ShapeDtypeStruct((count, size), BF16) for count in counts]


def first(rows):
    pieces = [jax.ShapeDtypeStruct(rows.shape, BF16)]
    tile = jax.ShapeDtypeStruct((SUBLANES, LANES), F32)
    *pieces, overlap, square = pl.pallas_call(
        first_kernel,
        out_shape=pieces + [tile, tile],
        in_specs=[NEAR],
        out_specs=[NEAR] * (len(pieces) + 2),
        name="first_wave",
        compiler_params=SMALL_CALL,
    )(rows)
    return pieces, overlap, square


def advance_kernel(
    cell_count,
    position,
    beta,
    scale,
    sums,
    applied,
    current,
    previous,
    diagonal,
    following,
    *rest,
):
    *pieces, overlap, square, quotient, scale_out = rest
    stats = summed(sums)
    ratio = stats[:1, :1] / stats[1:2, :1]
    if position > 0:
        mean = stats[2:3, :1] / cell_count
        inverse = 1.0 / jnp.sqrt(mean + EPSILON)
    else:
        inverse = jnp.ones((1, 1), F32)
    held = current[...]
    residual = (applied[...] - ratio * held) * inverse - (beta[position] * scale[:1, :1]) * previous[...]
    scaled = diagonal[...] * residual
    rounded = scaled.astype(BF16)
    following[...] = scaled
    store_pieces(pieces, rounded)
    overlap[...] = fold(scaled * rounded.astype(F32))
    square[...] = fold(scaled * scaled)
    quotient[...] = jnp.broadcast_to(ratio, quotient.shape)
    scale_out[...] = jnp.broadcast_to(inverse, scale_out.shape)


def advance(cell_count, position, beta, scale, sums, applied, current, previous, diagonal):
    tile = jax.ShapeDtypeStruct((SUBLANES, LANES), F32)
    pieces = piece_shapes(*current.shape)
    following, *pieces, overlap, square, quotient, scale = pl.pallas_call(
        functools.partial(advance_kernel, cell_count, position),
        out_shape=[jax.ShapeDtypeStruct(current.shape, F32)] + pieces + [tile] * 4,
        in_specs=[SCALARS] + [NEAR] * 6,
        out_specs=[NEAR] * (5 + len(pieces)),
        name="advance",
        compiler_params=SMALL_CALL,
    )(beta, scale, sums, applied, current, previous, diagonal)
    return following, pieces, overlap, square, quotient, scale


def closing_kernel(
    position, count, beta, scale, current, previous, diagonal, *rest
):
    chunks = rest[:count]
    applied_out, products = rest[count:]
    add_chunks(chunks, applied_out)
    applied = applied_out[...]
    held = current[...]
    weight = diagonal[...]
    direct = weight * applied
    turned = weight * held
    older = weight * ((beta[position] * scale[:1, :1]) * previous[...])
    pairs = (
        (held, applied),
        (held, held),
        (direct, direct),
        (direct, turned),
        (turned, turned),
        (direct, older),
        (turned, older),
        (older, older),
    )
    rows = lax.broadcasted_iota(jnp.int32, (SUBLANES, LANES), 0)
    tile = jnp.zeros((SUBLANES, LANES), F32)
    for i, (a, b) in enumerate(pairs):
        tile = jnp.where(rows == i, jnp.sum(fold(a * b), keepdims=True), tile)
    products[...] = tile


def closing(position, beta, scale, current, previous, diagonal, chunks):
    return pl.pallas_call(
        functools.partial(closing_kernel, position, len(chunks)),
        out_shape=[
            jax.ShapeDtypeStruct(current.shape, F32),
            jax.ShapeDtypeStruct((SUBLANES, LANES), F32),
        ],
        in_specs=[SCALARS] + [NEAR] * (4 + len(chunks)),
        out_specs=[NEAR] * 2,
        name="closing_products",
        compiler_params=SMALL_CALL,
    )(beta, scale, current, previous, diagonal, *chunks)


def final_kernel(
    cell_count,
    position,
    beta,
    scale,
    sums,
    applied,
    current,
    previous,
    diagonal,
    *rest,
):
    earlier, (out, quotients) = rest[:position], rest[position:]

    stats = summed(sums)

    def total(i):
        return stats[i : i + 1, :1]

    ratio = total(0) / total(1)
    inverse = 1.0 / jnp.sqrt(total(1) / cell_count + EPSILON)
    for i, tile in enumerate(earlier):
        quotients[i] = jnp.max(tile[...])
    quotients[position] = jnp.max(ratio)
    inner = total(2) - 2.0 * ratio * total(3) + ratio * ratio * total(4)
    mixed = total(5) - ratio * total(6)
    squares = inverse * inverse * inner - 2.0 * inverse * mixed + total(7)
    norm = 1.0 / jnp.sqrt(squares / cell_count + EPSILON)
    residual = (applied[...] - ratio * current[...]) * inverse
    residual = residual - (beta[position] * scale[:1, :1]) * previous[...]
    out[...] = diagonal[...] * residual * norm


def final(cell_count, position, beta, scale, sums, applied, current, previous, diagonal, earlier):
    return pl.pallas_call(
        functools.partial(final_kernel, cell_count, position),
        out_shape=[
            jax.ShapeDtypeStruct(current.shape, F32),
            jax.ShapeDtypeStruct((position + 1,), F32),
        ],
        in_specs=[SCALARS] + [NEAR] * (6 + position),
        out_specs=[NEAR, SCALARS],
        name="final_vector",
        compiler_params=SMALL_CALL,
    )(beta, scale, sums, applied, current, previous, diagonal, *earlier)


def local(
    x_start,
    x_prev,
    precond,
    left_env,
    right_env,
    triples,
    trip_count,
    term_coef,
    lanczos_beta,
    block_owner,
):
    sectors = lax.axis_size("sector")
    term_count = lax.axis_size("term")
    size = left_env.shape[1]
    cell_count = sectors * size * size
    place = jnp.stack([lax.axis_index("sector"), lax.axis_index("term")]).astype(jnp.int32)

    normaliser = 1.0 / math.sqrt(term_count * triples.shape[0])
    current, previous, diagonal = x_start[0], x_prev[0], precond[0]
    pieces, overlap, square = first(current)
    table, weights = plan(
        normaliser, triples.T, block_owner, trip_count, term_coef, place
    )
    left, right = load(left_env, right_env)
    scale = jnp.ones((SUBLANES, LANES), F32)
    quotients = []
    for position in range(APPS):
        arrays = gather(pieces, sectors, term_count)
        chunks = apply_local(
            table,
            weights,
            place,
            left,
            right,
            overlap,
            square,
            arrays,
            sectors,
            term_count,
        )
        arrived = [chunks[0]]
        for flip in range(1, term_count):
            arrived.append(exchange(chunks[flip], "term", flip))
        if position < APPS - 1:
            applied, stats = collect(arrived, current.shape)
            sums = lax.all_gather(stats, "sector", axis=0, tiled=True)
            following, pieces, overlap, square, quotient, scale_new = advance(
                cell_count,
                position,
                lanczos_beta,
                scale,
                sums,
                applied,
                current,
                previous,
                diagonal,
            )
            previous, current, scale = current, following, scale_new
            quotients.append(quotient)
        else:
            applied, products = closing(
                position, lanczos_beta, scale, current, previous, diagonal, arrived
            )
            products = sum_term(products, term_count)
            sums = lax.all_gather(products, "sector", axis=0, tiled=True)
            current, quotients = final(
                cell_count,
                position,
                lanczos_beta,
                scale,
                sums,
                applied,
                current,
                previous,
                diagonal,
                quotients,
            )
    return current[None], quotients


def solution(mesh):
    placed = (
        P("sector", "term", None),
        P("sector", "term", None),
        P("sector", "term", None),
        P(("sector", "term"), None, None),
        P(("sector", "term"), None, None),
        P(("sector", "term"), None),
        P("sector", "term"),
        P(),
        P(),
        P(),
    )
    return jax.shard_map(
        local,
        mesh=mesh,
        in_specs=placed,
        out_specs=(P("sector", "term", None), P()),
        check_vma=False,
    )
```

profile of v0, /device:TPU:0, one launch (start us, length us, event | category | flops | bytes accessed | tf_op | source)
XLA Modules:
  0.0 180.7 jit_solution(14746793298732765467)
XLA Ops:
  1.6 3.1 %collective-permute-start.2 = (bf16[96,384]{1,0:T(8,128)(2,1)S(1)}, bf16[96,384]{1,0:T(8,128)(2,1)S(1)}, u32[]{:S(2)}, u32[]{:S(2)}) collective-permute-start(bf16[96,384]{1,0:T(8,128)(2,1)S(1)} %get-tuple-element.49), channel_id=1, source_target_pairs={{0,1},{1,0},{2,3},{3,2},{4,5},{5,4},{6,7},{7,6},{8,9},{9,8},{10,11... | collective-permute-start | bytes 221192 | tf_op jit(solution)/shard_map/ppermute | solution.py:29
  4.7 2.6 %collective-permute-start.1 = (bf16[96,384]{1,0:T(8,128)(2,1)S(1)}, bf16[96,384]{1,0:T(8,128)(2,1)S(1)}, u32[]{:S(2)}, u32[]{:S(2)}) collective-permute-start(bf16[96,384]{1,0:T(8,128)(2,1)S(1)} %get-tuple-element.49), channel_id=1, source_target_pairs={{0,2},{1,3},{2,0},{3,1},{4,6},{5,7},{6,4},{7,5},{8,10},{9,11},{10,... | collective-permute-start | bytes 221192 | tf_op jit(solution)/shard_map/ppermute | solution.py:29
  7.3 5.2 %collective-permute-done.1 = bf16[96,384]{1,0:T(8,128)(2,1)S(1)} collective-permute-done((bf16[96,384]{1,0:T(8,128)(2,1)S(1)}, bf16[96,384]{1,0:T(8,128)(2,1)S(1)}, u32[]{:S(2)}, u32[]{:S(2)}) %collective-permute-start.1) | collective-permute-done | bytes 73760 | tf_op jit(solution)/shard_map/ppermute | solution.py:29
  13.6 2.5 %collective-permute-start.5 = (bf16[384,384]{1,0:T(8,128)(2,1)S(1)}, bf16[384,384]{1,0:T(8,128)(2,1)S(1)}, u32[]{:S(2)}, u32[]{:S(2)}) collective-permute-start(bf16[384,384]{1,0:T(8,128)(2,1)S(1)} %pad_maximum_fusion.rest_0_), channel_id=1, source_target_pairs={{0,24},{4,28},{8,16},{12,20},{16,8},{20,12},{24,0},{28,4},{1,25},{... | collective-permute-start | bytes 884744 | tf_op jit(solution)/shard_map/ppermute | solution.py:29
  17.2 7.3 %collective-permute-done.5.rest_3_ = bf16[384,384]{1,0:T(8,128)(2,1)S(1)} collective-permute-done((bf16[384,384]{1,0:T(8,128)(2,1)S(1)}, bf16[384,384]{1,0:T(8,128)(2,1)S(1)}, u32[]{:S(2)}, u32[]{:S(2)}) %collective-permute-start.5) | collective-permute-done | bytes 294944 | tf_op jit(solution)/shard_map/ppermute | solution.py:29
  24.5 3.4 %collective-permute-done.4.rest_2_ = bf16[384,384]{1,0:T(8,128)(2,1)S(1)} collective-permute-done((bf16[384,384]{1,0:T(8,128)(2,1)S(1)}, bf16[384,384]{1,0:T(8,128)(2,1)S(1)}, u32[]{:S(2)}, u32[]{:S(2)}) %collective-permute-start.4) | collective-permute-done | bytes 294944 | tf_op jit(solution)/shard_map/ppermute | solution.py:29
  29.0 1.7 copy-done
  30.7 1.7 copy-done.1
  34.9 8.4 %apply_triples.3 = (f32[304,128]{1,0:T(8,128)S(1)}, bf16[304,128]{1,0:T(8,128)(2,1)S(1)}, bf16[304,128]{1,0:T(8,128)(2,1)S(1)}, bf16[304,128]{1,0:T(8,128)(2,1)S(1)}) custom-call(s32[3,20]{1,0:T(4,128)S(1)} %get-tuple-element.43.table, f32[20]{0:T(128)S(1)} %get-tuple-element.44.weights, s32[2]{0:T(128)S(1)} %pad_add_fusion.place, ...), custom_call_target="tpu_custom_call" | custom-call | flops 4076863488 | bytes 7372800 | tf_op jit(solution)/shard_map/apply_triples/pallas_call | solution.py:273
  43.4 1.3 collective-permute-start.10
  44.7 1.6 collective-permute-start.11
  46.3 1.5 collective-permute-start.12
  47.8 6.0 %collective-permute-done.11.rest_2_ = bf16[304,128]{1,0:T(8,128)(2,1)S(1)} collective-permute-done((bf16[304,128]{1,0:T(8,128)(2,1)S(1)}, bf16[304,128]{1,0:T(8,128)(2,1)S(1)}, u32[]{:S(2)}, u32[]{:S(2)}) %collective-permute-start.11) | collective-permute-done | bytes 77856 | tf_op jit(solution)/shard_map/ppermute | solution.py:29
  53.9 9.2 %all_gather.9.sums = f32[64,128]{1,0:T(8,128)S(1)} all-gather(f32[8,128]{1,0:T(8,128)S(1)} %get-tuple-element.54), channel_id=1, replica_groups=mesh['sector'=8,'term'=4] {'sector'}, dimensions={0}, use_global_device_ids=true | all-gather | bytes 36864 | tf_op jit(solution)/shard_map/all_gather | solution.py:552
  63.7 1.5 collective-permute-start.25
  67.3 2.1 %collective-permute-start.15 = (bf16[64,384]{1,0:T(8,128)(2,1)S(1)}, bf16[64,384]{1,0:T(8,128)(2,1)S(1)}, u32[]{:S(2)}, u32[]{:S(2)}) collective-permute-start(bf16[64,384]{1,0:T(8,128)(2,1)S(1)} %get-tuple-element.59), channel_id=1, source_target_pairs={{0,3},{1,2},{2,1},{3,0},{4,7},{5,6},{6,5},{7,4},{8,11},{9,10},{10,... | collective-permute-start | bytes 147464 | tf_op jit(solution)/shard_map/ppermute | solution.py:29
  70.4 1.3 collective-permute-start.13
  71.9 2.4 %collective-permute-start.28 = (bf16[128,384]{1,0:T(8,128)(2,1)S(1)}, bf16[128,384]{1,0:T(8,128)(2,1)S(1)}, u32[]{:S(2)}, u32[]{:S(2)}) collective-permute-start(bf16[128,384]{1,0:T(8,128)(2,1)S(1)} %constant_dynamic-update-slice_fusion.4.rest_8_), channel_id=1, source_target_pairs={{0,3},{1,2},{2,1},{3,0},{4,7},{5,6},{6,5},{7,4},{8,11},{9,10},{10,... | collective-permute-start | bytes 294920 | tf_op jit(solution)/shard_map/ppermute | solution.py:29
  75.1 1.6 collective-permute-start.27
  76.8 1.5 collective-permute-start.18
  78.3 1.3 collective-permute-start.17
  80.3 2.2 %collective-permute-start.26 = (bf16[128,384]{1,0:T(8,128)(2,1)S(1)}, bf16[128,384]{1,0:T(8,128)(2,1)S(1)}, u32[]{:S(2)}, u32[]{:S(2)}) collective-permute-start(bf16[128,384]{1,0:T(8,128)(2,1)S(1)} %constant_dynamic-update-slice_fusion.4.rest_8_), channel_id=1, source_target_pairs={{0,1},{1,0},{2,3},{3,2},{4,5},{5,4},{6,7},{7,6},{8,9},{9,8},{10,11... | collective-permute-start | bytes 294920 | tf_op jit(solution)/shard_map/ppermute | solution.py:29
  83.7 1.6 collective-permute-done.26.rest_9_
  87.3 1.3 collective-permute-done.30.rest_13_
  88.6 8.4 %apply_triples.4 = (f32[304,128]{1,0:T(8,128)S(1)}, bf16[304,128]{1,0:T(8,128)(2,1)S(1)}, bf16[304,128]{1,0:T(8,128)(2,1)S(1)}, bf16[304,128]{1,0:T(8,128)(2,1)S(1)}) custom-call(s32[3,20]{1,0:T(4,128)S(1)} %get-tuple-element.43.table, f32[20]{0:T(128)S(1)} %get-tuple-element.44.weights, s32[2]{0:T(128)S(1)} %pad_add_fusion.place, ...), custom_call_target="tpu_custom_call" | custom-call | flops 4076863488 | bytes 7372800 | tf_op jit(solution)/shard_map/apply_triples/pallas_call | solution.py:273
  97.1 1.6 collective-permute-start.33
  98.7 1.6 collective-permute-start.34
  101.6 6.2 %collective-permute-done.34.rest_2_ = bf16[304,128]{1,0:T(8,128)(2,1)S(1)} collective-permute-done((bf16[304,128]{1,0:T(8,128)(2,1)S(1)}, bf16[304,128]{1,0:T(8,128)(2,1)S(1)}, u32[]{:S(2)}, u32[]{:S(2)}) %collective-permute-start.34) | collective-permute-done | bytes 77856 | tf_op jit(solution)/shard_map/ppermute | solution.py:29
  107.9 8.8 %all_gather.10.sums = f32[64,128]{1,0:T(8,128)S(1)} all-gather(f32[8,128]{1,0:T(8,128)S(1)} %get-tuple-element.65), channel_id=1, replica_groups=mesh['sector'=8,'term'=4] {'sector'}, dimensions={0}, use_global_device_ids=true | all-gather | bytes 36864 | tf_op jit(solution)/shard_map/all_gather | solution.py:552
  117.4 1.5 collective-permute-start.48
  121.0 2.2 %collective-permute-start.38 = (bf16[64,384]{1,0:T(8,128)(2,1)S(1)}, bf16[64,384]{1,0:T(8,128)(2,1)S(1)}, u32[]{:S(2)}, u32[]{:S(2)}) collective-permute-start(bf16[64,384]{1,0:T(8,128)(2,1)S(1)} %get-tuple-element.72), channel_id=1, source_target_pairs={{0,3},{1,2},{2,1},{3,0},{4,7},{5,6},{6,5},{7,4},{8,11},{9,10},{10,... | collective-permute-start | bytes 147464 | tf_op jit(solution)/shard_map/ppermute | solution.py:29
  124.0 1.4 collective-permute-start.36
  125.6 2.4 %collective-permute-start.51 = (bf16[128,384]{1,0:T(8,128)(2,1)S(1)}, bf16[128,384]{1,0:T(8,128)(2,1)S(1)}, u32[]{:S(2)}, u32[]{:S(2)}) collective-permute-start(bf16[128,384]{1,0:T(8,128)(2,1)S(1)} %constant_dynamic-update-slice_fusion.12.rest_8_), channel_id=1, source_target_pairs={{0,3},{1,2},{2,1},{3,0},{4,7},{5,6},{6,5},{7,4},{8,11},{9,10},{10,... | collective-permute-start | bytes 294920 | tf_op jit(solution)/shard_map/ppermute | solution.py:29
  128.5 1.9 %collective-permute-start.50 = (bf16[128,384]{1,0:T(8,128)(2,1)S(1)}, bf16[128,384]{1,0:T(8,128)(2,1)S(1)}, u32[]{:S(2)}, u32[]{:S(2)}) collective-permute-start(bf16[128,384]{1,0:T(8,128)(2,1)S(1)} %constant_dynamic-update-slice_fusion.12.rest_8_), channel_id=1, source_target_pairs={{0,2},{1,3},{2,0},{3,1},{4,6},{5,7},{6,4},{7,5},{8,10},{9,11},{10,... | collective-permute-start | bytes 294920 | tf_op jit(solution)/shard_map/ppermute | solution.py:29
  130.5 1.5 collective-permute-start.41
  134.0 1.9 %collective-permute-start.49 = (bf16[128,384]{1,0:T(8,128)(2,1)S(1)}, bf16[128,384]{1,0:T(8,128)(2,1)S(1)}, u32[]{:S(2)}, u32[]{:S(2)}) collective-permute-start(bf16[128,384]{1,0:T(8,128)(2,1)S(1)} %constant_dynamic-update-slice_fusion.12.rest_8_), channel_id=1, source_target_pairs={{0,1},{1,0},{2,3},{3,2},{4,5},{5,4},{6,7},{7,6},{8,9},{9,8},{10,11... | collective-permute-start | bytes 294920 | tf_op jit(solution)/shard_map/ppermute | solution.py:29
  136.0 1.3 collective-permute-done.50.rest_10_
  137.3 1.7 collective-permute-done.49.rest_9_
  142.1 8.4 %apply_triples.5 = (f32[304,128]{1,0:T(8,128)S(1)}, bf16[304,128]{1,0:T(8,128)(2,1)S(1)}, bf16[304,128]{1,0:T(8,128)(2,1)S(1)}, bf16[304,128]{1,0:T(8,128)(2,1)S(1)}) custom-call(s32[3,20]{1,0:T(4,128)S(1)} %get-tuple-element.43.table, f32[20]{0:T(128)S(1)} %get-tuple-element.44.weights, s32[2]{0:T(128)S(1)} %pad_add_fusion.place, ...), custom_call_target="tpu_custom_call" | custom-call | flops 4076863488 | bytes 7372800 | tf_op jit(solution)/shard_map/apply_triples/pallas_call | solution.py:273
  150.6 1.8 collective-permute-start.56
  153.3 1.7 collective-permute-start.58
  155.1 6.5 %collective-permute-done.57.rest_2_ = bf16[304,128]{1,0:T(8,128)(2,1)S(1)} collective-permute-done((bf16[304,128]{1,0:T(8,128)(2,1)S(1)}, bf16[304,128]{1,0:T(8,128)(2,1)S(1)}, u32[]{:S(2)}, u32[]{:S(2)}) %collective-permute-start.57) | collective-permute-done | bytes 77856 | tf_op jit(solution)/shard_map/ppermute | solution.py:29
  162.4 1.5 collective-permute-start.59
  163.9 2.2 %collective-permute-done.59 = f32[8,128]{1,0:T(8,128)S(1)} collective-permute-done((f32[8,128]{1,0:T(8,128)S(1)}, f32[8,128]{1,0:T(8,128)S(1)}, u32[]{:S(2)}, u32[]{:S(2)}) %collective-permute-start.59) | collective-permute-done | bytes 4128 | tf_op jit(solution)/shard_map/ppermute | solution.py:29
  166.1 2.2 %collective-permute-start.60 = (f32[8,128]{1,0:T(8,128)S(1)}, f32[8,128]{1,0:T(8,128)S(1)}, u32[]{:S(2)}, u32[]{:S(2)}) collective-permute-start(f32[8,128]{1,0:T(8,128)S(1)} %add.6), channel_id=1, source_target_pairs={{0,2},{1,3},{2,0},{3,1},{4,6},{5,7},{6,4},{7,5},{8,10},{9,11},{10,... | collective-permute-start | bytes 12296 | tf_op jit(solution)/shard_map/ppermute | solution.py:29
  168.3 2.3 %collective-permute-done.60 = f32[8,128]{1,0:T(8,128)S(1)} collective-permute-done((f32[8,128]{1,0:T(8,128)S(1)}, f32[8,128]{1,0:T(8,128)S(1)}, u32[]{:S(2)}, u32[]{:S(2)}) %collective-permute-start.60) | collective-permute-done | bytes 4128 | tf_op jit(solution)/shard_map/ppermute | solution.py:29
  170.6 8.6 %all_gather.11.sums = f32[64,128]{1,0:T(8,128)S(1)} all-gather(f32[8,128]{1,0:T(8,128)S(1)} %add.7), channel_id=1, replica_groups=mesh['sector'=8,'term'=4] {'sector'}, dimensions={0}, use_global_device_ids=true | all-gather | bytes 36864 | tf_op jit(solution)/shard_map/all_gather | solution.py:571
  179.2 1.4 final_vector.1
  (131 shorter events, 27.6 us)
Async XLA Ops:
  1.6 5.7 %collective-permute-start.2 = (bf16[96,384]{1,0:T(8,128)(2,1)S(1)}, bf16[96,384]{1,0:T(8,128)(2,1)S(1)}, u32[]{:S(2)}, u32[]{:S(2)}) collective-permute-start(bf16[96,384]{1,0:T(8,128)(2,1)S(1)} %get-tuple-element.49), channel_id=1, source_target_pairs={{0,1},{1,0},{2,3},{3,2},{4,5},{5,4},{6,7},{7,6},{8,9},{9,8},{10,11... | collective-permute-start | bytes 221192 | tf_op jit(solution)/shard_map/ppermute | solution.py:29
  4.7 7.8 %collective-permute-start.1 = (bf16[96,384]{1,0:T(8,128)(2,1)S(1)}, bf16[96,384]{1,0:T(8,128)(2,1)S(1)}, u32[]{:S(2)}, u32[]{:S(2)}) collective-permute-start(bf16[96,384]{1,0:T(8,128)(2,1)S(1)} %get-tuple-element.49), channel_id=1, source_target_pairs={{0,2},{1,3},{2,0},{3,1},{4,6},{5,7},{6,4},{7,5},{8,10},{9,11},{10,... | collective-permute-start | bytes 221192 | tf_op jit(solution)/shard_map/ppermute | solution.py:29
  7.3 6.3 %collective-permute-start = (bf16[96,384]{1,0:T(8,128)(2,1)S(1)}, bf16[96,384]{1,0:T(8,128)(2,1)S(1)}, u32[]{:S(2)}, u32[]{:S(2)}) collective-permute-start(bf16[96,384]{1,0:T(8,128)(2,1)S(1)} %get-tuple-element.49), channel_id=1, source_target_pairs={{0,3},{1,2},{2,1},{3,0},{4,7},{5,6},{6,5},{7,4},{8,11},{9,10},{10,... | collective-permute-start | bytes 221192 | tf_op jit(solution)/shard_map/ppermute | solution.py:29
  13.6 10.9 %collective-permute-start.5 = (bf16[384,384]{1,0:T(8,128)(2,1)S(1)}, bf16[384,384]{1,0:T(8,128)(2,1)S(1)}, u32[]{:S(2)}, u32[]{:S(2)}) collective-permute-start(bf16[384,384]{1,0:T(8,128)(2,1)S(1)} %pad_maximum_fusion.rest_0_), channel_id=1, source_target_pairs={{0,24},{4,28},{8,16},{12,20},{16,8},{20,12},{24,0},{28,4},{1,25},{... | collective-permute-start | bytes 884744 | tf_op jit(solution)/shard_map/ppermute | solution.py:29
  16.2 11.7 %collective-permute-start.4 = (bf16[384,384]{1,0:T(8,128)(2,1)S(1)}, bf16[384,384]{1,0:T(8,128)(2,1)S(1)}, u32[]{:S(2)}, u32[]{:S(2)}) collective-permute-start(bf16[384,384]{1,0:T(8,128)(2,1)S(1)} %pad_maximum_fusion.rest_0_), channel_id=1, source_target_pairs={{0,16},{4,20},{8,24},{12,28},{16,0},{20,4},{24,8},{28,12},{1,17},{... | collective-permute-start | bytes 884744 | tf_op jit(solution)/shard_map/ppermute | solution.py:29
  16.7 11.3 %collective-permute-start.3 = (bf16[384,384]{1,0:T(8,128)(2,1)S(1)}, bf16[384,384]{1,0:T(8,128)(2,1)S(1)}, u32[]{:S(2)}, u32[]{:S(2)}) collective-permute-start(bf16[384,384]{1,0:T(8,128)(2,1)S(1)} %pad_maximum_fusion.rest_0_), channel_id=1, source_target_pairs={{0,8},{4,12},{8,0},{12,4},{16,24},{20,28},{24,16},{28,20},{1,9},{5... | collective-permute-start | bytes 884744 | tf_op jit(solution)/shard_map/ppermute | solution.py:29
  17.2 17.7 %collective-permute-start.6 = (bf16[384,384]{1,0:T(8,128)(2,1)S(1)}, bf16[384,384]{1,0:T(8,128)(2,1)S(1)}, u32[]{:S(2)}, u32[]{:S(2)}) collective-permute-start(bf16[384,384]{1,0:T(8,128)(2,1)S(1)} %pad_maximum_fusion.rest_0_), channel_id=1, source_target_pairs={{0,4},{4,0},{8,12},{12,8},{16,20},{20,16},{24,28},{28,24},{1,5},{5... | collective-permute-start | bytes 884744 | tf_op jit(solution)/shard_map/ppermute | solution.py:29
  24.5 10.4 %collective-permute-start.9 = (bf16[384,384]{1,0:T(8,128)(2,1)S(1)}, bf16[384,384]{1,0:T(8,128)(2,1)S(1)}, u32[]{:S(2)}, u32[]{:S(2)}) collective-permute-start(bf16[384,384]{1,0:T(8,128)(2,1)S(1)} %collective-permute-done.5.rest_3_), channel_id=1, source_target_pairs={{0,4},{4,0},{8,12},{12,8},{16,20},{20,16},{24,28},{28,24},{1,5},{5... | collective-permute-start | bytes 884744 | tf_op jit(solution)/shard_map/ppermute | solution.py:29
  27.9 7.0 %collective-permute-start.8 = (bf16[384,384]{1,0:T(8,128)(2,1)S(1)}, bf16[384,384]{1,0:T(8,128)(2,1)S(1)}, u32[]{:S(2)}, u32[]{:S(2)}) collective-permute-start(bf16[384,384]{1,0:T(8,128)(2,1)S(1)} %collective-permute-done.4.rest_2_), channel_id=1, source_target_pairs={{0,4},{4,0},{8,12},{12,8},{16,20},{20,16},{24,28},{28,24},{1,5},{5... | collective-permute-start | bytes 884744 | tf_op jit(solution)/shard_map/ppermute | solution.py:29
  28.0 6.9 %collective-permute-start.7 = (bf16[384,384]{1,0:T(8,128)(2,1)S(1)}, bf16[384,384]{1,0:T(8,128)(2,1)S(1)}, u32[]{:S(2)}, u32[]{:S(2)}) collective-permute-start(bf16[384,384]{1,0:T(8,128)(2,1)S(1)} %collective-permute-done.3.rest_1_), channel_id=1, source_target_pairs={{0,4},{4,0},{8,12},{12,8},{16,20},{20,16},{24,28},{28,24},{1,5},{5... | collective-permute-start | bytes 884744 | tf_op jit(solution)/shard_map/ppermute | solution.py:29
  43.4 4.5 %collective-permute-start.10 = (bf16[304,128]{1,0:T(8,128)(2,1)S(1)}, bf16[304,128]{1,0:T(8,128)(2,1)S(1)}, u32[]{:S(2)}, u32[]{:S(2)}) collective-permute-start(bf16[304,128]{1,0:T(8,128)(2,1)S(1)} %get-tuple-element.51), channel_id=1, source_target_pairs={{0,1},{1,0},{2,3},{3,2},{4,5},{5,4},{6,7},{7,6},{8,9},{9,8},{10,11... | collective-permute-start | bytes 233480 | tf_op jit(solution)/shard_map/ppermute | solution.py:29
  44.7 9.1 %collective-permute-start.11 = (bf16[304,128]{1,0:T(8,128)(2,1)S(1)}, bf16[304,128]{1,0:T(8,128)(2,1)S(1)}, u32[]{:S(2)}, u32[]{:S(2)}) collective-permute-start(bf16[304,128]{1,0:T(8,128)(2,1)S(1)} %get-tuple-element.52), channel_id=1, source_target_pairs={{0,2},{1,3},{2,0},{3,1},{4,6},{5,7},{6,4},{7,5},{8,10},{9,11},{10,... | collective-permute-start | bytes 233480 | tf_op jit(solution)/shard_map/ppermute | solution.py:29
  46.3 7.5 %collective-permute-start.12 = (bf16[304,128]{1,0:T(8,128)(2,1)S(1)}, bf16[304,128]{1,0:T(8,128)(2,1)S(1)}, u32[]{:S(2)}, u32[]{:S(2)}) collective-permute-start(bf16[304,128]{1,0:T(8,128)(2,1)S(1)} %get-tuple-element.53), channel_id=1, source_target_pairs={{0,3},{1,2},{2,1},{3,0},{4,7},{5,6},{6,5},{7,4},{8,11},{9,10},{10,... | collective-permute-start | bytes 233480 | tf_op jit(solution)/shard_map/ppermute | solution.py:29
  63.7 8.1 %collective-permute-start.25 = (bf16[32,384]{1,0:T(8,128)(2,1)S(1)}, bf16[32,384]{1,0:T(8,128)(2,1)S(1)}, u32[]{:S(2)}, u32[]{:S(2)}) collective-permute-start(bf16[32,384]{1,0:T(8,128)(2,1)S(1)} %get-tuple-element.60), channel_id=1, source_target_pairs={{0,24},{4,28},{8,16},{12,20},{16,8},{20,12},{24,0},{28,4},{1,25},{... | collective-permute-start | bytes 73736 | tf_op jit(solution)/shard_map/ppermute | solution.py:29
  65.3 6.5 %collective-permute-start.24 = (bf16[32,384]{1,0:T(8,128)(2,1)S(1)}, bf16[32,384]{1,0:T(8,128)(2,1)S(1)}, u32[]{:S(2)}, u32[]{:S(2)}) collective-permute-start(bf16[32,384]{1,0:T(8,128)(2,1)S(1)} %get-tuple-element.60), channel_id=1, source_target_pairs={{0,16},{4,20},{8,24},{12,28},{16,0},{20,4},{24,8},{28,12},{1,17},{... | collective-permute-start | bytes 73736 | tf_op jit(solution)/shard_map/ppermute | solution.py:29
  66.0 4.4 %collective-permute-start.23 = (bf16[32,384]{1,0:T(8,128)(2,1)S(1)}, bf16[32,384]{1,0:T(8,128)(2,1)S(1)}, u32[]{:S(2)}, u32[]{:S(2)}) collective-permute-start(bf16[32,384]{1,0:T(8,128)(2,1)S(1)} %get-tuple-element.60), channel_id=1, source_target_pairs={{0,8},{4,12},{8,0},{12,4},{16,24},{20,28},{24,16},{28,20},{1,9},{5... | collective-permute-start | bytes 73736 | tf_op jit(solution)/shard_map/ppermute | solution.py:29
  67.3 9.4 %collective-permute-start.15 = (bf16[64,384]{1,0:T(8,128)(2,1)S(1)}, bf16[64,384]{1,0:T(8,128)(2,1)S(1)}, u32[]{:S(2)}, u32[]{:S(2)}) collective-permute-start(bf16[64,384]{1,0:T(8,128)(2,1)S(1)} %get-tuple-element.59), channel_id=1, source_target_pairs={{0,3},{1,2},{2,1},{3,0},{4,7},{5,6},{6,5},{7,4},{8,11},{9,10},{10,... | collective-permute-start | bytes 147464 | tf_op jit(solution)/shard_map/ppermute | solution.py:29
  69.4 7.3 %collective-permute-start.14 = (bf16[64,384]{1,0:T(8,128)(2,1)S(1)}, bf16[64,384]{1,0:T(8,128)(2,1)S(1)}, u32[]{:S(2)}, u32[]{:S(2)}) collective-permute-start(bf16[64,384]{1,0:T(8,128)(2,1)S(1)} %get-tuple-element.59), channel_id=1, source_target_pairs={{0,2},{1,3},{2,0},{3,1},{4,6},{5,7},{6,4},{7,5},{8,10},{9,11},{10,... | collective-permute-start | bytes 147464 | tf_op jit(solution)/shard_map/ppermute | solution.py:29
  70.4 4.7 %collective-permute-start.13 = (bf16[64,384]{1,0:T(8,128)(2,1)S(1)}, bf16[64,384]{1,0:T(8,128)(2,1)S(1)}, u32[]{:S(2)}, u32[]{:S(2)}) collective-permute-start(bf16[64,384]{1,0:T(8,128)(2,1)S(1)} %get-tuple-element.59), channel_id=1, source_target_pairs={{0,1},{1,0},{2,3},{3,2},{4,5},{5,4},{6,7},{7,6},{8,9},{9,8},{10,11... | collective-permute-start | bytes 147464 | tf_op jit(solution)/shard_map/ppermute | solution.py:29
  71.8 7.8 %collective-permute-start.29 = (bf16[128,384]{1,0:T(8,128)(2,1)S(1)}, bf16[128,384]{1,0:T(8,128)(2,1)S(1)}, u32[]{:S(2)}, u32[]{:S(2)}) collective-permute-start(bf16[128,384]{1,0:T(8,128)(2,1)S(1)} %constant_dynamic-update-slice_fusion.4.rest_8_), channel_id=1, source_target_pairs={{0,4},{4,0},{8,12},{12,8},{16,20},{20,16},{24,28},{28,24},{1,5},{5... | collective-permute-start | bytes 294920 | tf_op jit(solution)/shard_map/ppermute | solution.py:29
  71.9 8.4 %collective-permute-start.28 = (bf16[128,384]{1,0:T(8,128)(2,1)S(1)}, bf16[128,384]{1,0:T(8,128)(2,1)S(1)}, u32[]{:S(2)}, u32[]{:S(2)}) collective-permute-start(bf16[128,384]{1,0:T(8,128)(2,1)S(1)} %constant_dynamic-update-slice_fusion.4.rest_8_), channel_id=1, source_target_pairs={{0,3},{1,2},{2,1},{3,0},{4,7},{5,6},{6,5},{7,4},{8,11},{9,10},{10,... | collective-permute-start | bytes 294920 | tf_op jit(solution)/shard_map/ppermute | solution.py:29
  75.1 8.6 %collective-permute-start.27 = (bf16[128,384]{1,0:T(8,128)(2,1)S(1)}, bf16[128,384]{1,0:T(8,128)(2,1)S(1)}, u32[]{:S(2)}, u32[]{:S(2)}) collective-permute-start(bf16[128,384]{1,0:T(8,128)(2,1)S(1)} %constant_dynamic-update-slice_fusion.4.rest_8_), channel_id=1, source_target_pairs={{0,2},{1,3},{2,0},{3,1},{4,6},{5,7},{6,4},{7,5},{8,10},{9,11},{10,... | collective-permute-start | bytes 294920 | tf_op jit(solution)/shard_map/ppermute | solution.py:29
  76.8 9.1 %collective-permute-start.18 = (bf16[256,384]{1,0:T(8,128)(2,1)S(1)}, bf16[256,384]{1,0:T(8,128)(2,1)S(1)}, u32[]{:S(2)}, u32[]{:S(2)}) collective-permute-start(bf16[256,384]{1,0:T(8,128)(2,1)S(1)} %constant_dynamic-update-slice_fusion.rest_0_), channel_id=1, source_target_pairs={{0,24},{4,28},{8,16},{12,20},{16,8},{20,12},{24,0},{28,4},{1,25},{... | collective-permute-start | bytes 589832 | tf_op jit(solution)/shard_map/ppermute | solution.py:29
  78.3 8.4 %collective-permute-start.17 = (bf16[256,384]{1,0:T(8,128)(2,1)S(1)}, bf16[256,384]{1,0:T(8,128)(2,1)S(1)}, u32[]{:S(2)}, u32[]{:S(2)}) collective-permute-start(bf16[256,384]{1,0:T(8,128)(2,1)S(1)} %constant_dynamic-update-slice_fusion.rest_0_), channel_id=1, source_target_pairs={{0,16},{4,20},{8,24},{12,28},{16,0},{20,4},{24,8},{28,12},{1,17},{... | collective-permute-start | bytes 589832 | tf_op jit(solution)/shard_map/ppermute | solution.py:29
  79.6 7.2 %collective-permute-start.16 = (bf16[256,384]{1,0:T(8,128)(2,1)S(1)}, bf16[256,384]{1,0:T(8,128)(2,1)S(1)}, u32[]{:S(2)}, u32[]{:S(2)}) collective-permute-start(bf16[256,384]{1,0:T(8,128)(2,1)S(1)} %constant_dynamic-update-slice_fusion.rest_0_), channel_id=1, source_target_pairs={{0,8},{4,12},{8,0},{12,4},{16,24},{20,28},{24,16},{28,20},{1,9},{5... | collective-permute-start | bytes 589832 | tf_op jit(solution)/shard_map/ppermute | solution.py:29
  80.3 5.0 %collective-permute-start.26 = (bf16[128,384]{1,0:T(8,128)(2,1)S(1)}, bf16[128,384]{1,0:T(8,128)(2,1)S(1)}, u32[]{:S(2)}, u32[]{:S(2)}) collective-permute-start(bf16[128,384]{1,0:T(8,128)(2,1)S(1)} %constant_dynamic-update-slice_fusion.4.rest_8_), channel_id=1, source_target_pairs={{0,1},{1,0},{2,3},{3,2},{4,5},{5,4},{6,7},{7,6},{8,9},{9,8},{10,11... | collective-permute-start | bytes 294920 | tf_op jit(solution)/shard_map/ppermute | solution.py:29
  85.3 3.3 %collective-permute-start.19 = (bf16[256,384]{1,0:T(8,128)(2,1)S(1)}, bf16[256,384]{1,0:T(8,128)(2,1)S(1)}, u32[]{:S(2)}, u32[]{:S(2)}) collective-permute-start(bf16[256,384]{1,0:T(8,128)(2,1)S(1)} %constant_dynamic-update-slice_fusion.rest_0_), channel_id=1, source_target_pairs={{0,4},{4,0},{8,12},{12,8},{16,20},{20,16},{24,28},{28,24},{1,5},{5... | collective-permute-start | bytes 589832 | tf_op jit(solution)/shard_map/ppermute | solution.py:29
  97.1 4.6 %collective-permute-start.33 = (bf16[304,128]{1,0:T(8,128)(2,1)S(1)}, bf16[304,128]{1,0:T(8,128)(2,1)S(1)}, u32[]{:S(2)}, u32[]{:S(2)}) collective-permute-start(bf16[304,128]{1,0:T(8,128)(2,1)S(1)} %get-tuple-element.62), channel_id=1, source_target_pairs={{0,1},{1,0},{2,3},{3,2},{4,5},{5,4},{6,7},{7,6},{8,9},{9,8},{10,11... | collective-permute-start | bytes 233480 | tf_op jit(solution)/shard_map/ppermute | solution.py:29
  98.7 9.2 %collective-permute-start.34 = (bf16[304,128]{1,0:T(8,128)(2,1)S(1)}, bf16[304,128]{1,0:T(8,128)(2,1)S(1)}, u32[]{:S(2)}, u32[]{:S(2)}) collective-permute-start(bf16[304,128]{1,0:T(8,128)(2,1)S(1)} %get-tuple-element.63), channel_id=1, source_target_pairs={{0,2},{1,3},{2,0},{3,1},{4,6},{5,7},{6,4},{7,5},{8,10},{9,11},{10,... | collective-permute-start | bytes 233480 | tf_op jit(solution)/shard_map/ppermute | solution.py:29
  100.3 7.6 %collective-permute-start.35 = (bf16[304,128]{1,0:T(8,128)(2,1)S(1)}, bf16[304,128]{1,0:T(8,128)(2,1)S(1)}, u32[]{:S(2)}, u32[]{:S(2)}) collective-permute-start(bf16[304,128]{1,0:T(8,128)(2,1)S(1)} %get-tuple-element.64), channel_id=1, source_target_pairs={{0,3},{1,2},{2,1},{3,0},{4,7},{5,6},{6,5},{7,4},{8,11},{9,10},{10,... | collective-permute-start | bytes 233480 | tf_op jit(solution)/shard_map/ppermute | solution.py:29
  117.4 8.1 %collective-permute-start.48 = (bf16[32,384]{1,0:T(8,128)(2,1)S(1)}, bf16[32,384]{1,0:T(8,128)(2,1)S(1)}, u32[]{:S(2)}, u32[]{:S(2)}) collective-permute-start(bf16[32,384]{1,0:T(8,128)(2,1)S(1)} %get-tuple-element.73), channel_id=1, source_target_pairs={{0,24},{4,28},{8,16},{12,20},{16,8},{20,12},{24,0},{28,4},{1,25},{... | collective-permute-start | bytes 73736 | tf_op jit(solution)/shard_map/ppermute | solution.py:29
  118.9 6.5 %collective-permute-start.47 = (bf16[32,384]{1,0:T(8,128)(2,1)S(1)}, bf16[32,384]{1,0:T(8,128)(2,1)S(1)}, u32[]{:S(2)}, u32[]{:S(2)}) collective-permute-start(bf16[32,384]{1,0:T(8,128)(2,1)S(1)} %get-tuple-element.73), channel_id=1, source_target_pairs={{0,16},{4,20},{8,24},{12,28},{16,0},{20,4},{24,8},{28,12},{1,17},{... | collective-permute-start | bytes 73736 | tf_op jit(solution)/shard_map/ppermute | solution.py:29
  119.9 4.1 %collective-permute-start.46 = (bf16[32,384]{1,0:T(8,128)(2,1)S(1)}, bf16[32,384]{1,0:T(8,128)(2,1)S(1)}, u32[]{:S(2)}, u32[]{:S(2)}) collective-permute-start(bf16[32,384]{1,0:T(8,128)(2,1)S(1)} %get-tuple-element.73), channel_id=1, source_target_pairs={{0,8},{4,12},{8,0},{12,4},{16,24},{20,28},{24,16},{28,20},{1,9},{5... | collective-permute-start | bytes 73736 | tf_op jit(solution)/shard_map/ppermute | solution.py:29
  121.0 9.5 %collective-permute-start.38 = (bf16[64,384]{1,0:T(8,128)(2,1)S(1)}, bf16[64,384]{1,0:T(8,128)(2,1)S(1)}, u32[]{:S(2)}, u32[]{:S(2)}) collective-permute-start(bf16[64,384]{1,0:T(8,128)(2,1)S(1)} %get-tuple-element.72), channel_id=1, source_target_pairs={{0,3},{1,2},{2,1},{3,0},{4,7},{5,6},{6,5},{7,4},{8,11},{9,10},{10,... | collective-permute-start | bytes 147464 | tf_op jit(solution)/shard_map/ppermute | solution.py:29
  123.2 7.3 %collective-permute-start.37 = (bf16[64,384]{1,0:T(8,128)(2,1)S(1)}, bf16[64,384]{1,0:T(8,128)(2,1)S(1)}, u32[]{:S(2)}, u32[]{:S(2)}) collective-permute-start(bf16[64,384]{1,0:T(8,128)(2,1)S(1)} %get-tuple-element.72), channel_id=1, source_target_pairs={{0,2},{1,3},{2,0},{3,1},{4,6},{5,7},{6,4},{7,5},{8,10},{9,11},{10,... | collective-permute-start | bytes 147464 | tf_op jit(solution)/shard_map/ppermute | solution.py:29
  124.0 4.5 %collective-permute-start.36 = (bf16[64,384]{1,0:T(8,128)(2,1)S(1)}, bf16[64,384]{1,0:T(8,128)(2,1)S(1)}, u32[]{:S(2)}, u32[]{:S(2)}) collective-permute-start(bf16[64,384]{1,0:T(8,128)(2,1)S(1)} %get-tuple-element.72), channel_id=1, source_target_pairs={{0,1},{1,0},{2,3},{3,2},{4,5},{5,4},{6,7},{7,6},{8,9},{9,8},{10,11... | collective-permute-start | bytes 147464 | tf_op jit(solution)/shard_map/ppermute | solution.py:29
  125.5 7.5 %collective-permute-start.52 = (bf16[128,384]{1,0:T(8,128)(2,1)S(1)}, bf16[128,384]{1,0:T(8,128)(2,1)S(1)}, u32[]{:S(2)}, u32[]{:S(2)}) collective-permute-start(bf16[128,384]{1,0:T(8,128)(2,1)S(1)} %constant_dynamic-update-slice_fusion.12.rest_8_), channel_id=1, source_target_pairs={{0,4},{4,0},{8,12},{12,8},{16,20},{20,16},{24,28},{28,24},{1,5},{5... | collective-permute-start | bytes 294920 | tf_op jit(solution)/shard_map/ppermute | solution.py:29
  125.6 8.5 %collective-permute-start.51 = (bf16[128,384]{1,0:T(8,128)(2,1)S(1)}, bf16[128,384]{1,0:T(8,128)(2,1)S(1)}, u32[]{:S(2)}, u32[]{:S(2)}) collective-permute-start(bf16[128,384]{1,0:T(8,128)(2,1)S(1)} %constant_dynamic-update-slice_fusion.12.rest_8_), channel_id=1, source_target_pairs={{0,3},{1,2},{2,1},{3,0},{4,7},{5,6},{6,5},{7,4},{8,11},{9,10},{10,... | collective-permute-start | bytes 294920 | tf_op jit(solution)/shard_map/ppermute | solution.py:29
  128.5 8.8 %collective-permute-start.50 = (bf16[128,384]{1,0:T(8,128)(2,1)S(1)}, bf16[128,384]{1,0:T(8,128)(2,1)S(1)}, u32[]{:S(2)}, u32[]{:S(2)}) collective-permute-start(bf16[128,384]{1,0:T(8,128)(2,1)S(1)} %constant_dynamic-update-slice_fusion.12.rest_8_), channel_id=1, source_target_pairs={{0,2},{1,3},{2,0},{3,1},{4,6},{5,7},{6,4},{7,5},{8,10},{9,11},{10,... | collective-permute-start | bytes 294920 | tf_op jit(solution)/shard_map/ppermute | solution.py:29
  130.5 9.0 %collective-permute-start.41 = (bf16[256,384]{1,0:T(8,128)(2,1)S(1)}, bf16[256,384]{1,0:T(8,128)(2,1)S(1)}, u32[]{:S(2)}, u32[]{:S(2)}) collective-permute-start(bf16[256,384]{1,0:T(8,128)(2,1)S(1)} %constant_dynamic-update-slice_fusion.8.rest_0_), channel_id=1, source_target_pairs={{0,24},{4,28},{8,16},{12,20},{16,8},{20,12},{24,0},{28,4},{1,25},{... | collective-permute-start | bytes 589832 | tf_op jit(solution)/shard_map/ppermute | solution.py:29
  132.0 8.3 %collective-permute-start.40 = (bf16[256,384]{1,0:T(8,128)(2,1)S(1)}, bf16[256,384]{1,0:T(8,128)(2,1)S(1)}, u32[]{:S(2)}, u32[]{:S(2)}) collective-permute-start(bf16[256,384]{1,0:T(8,128)(2,1)S(1)} %constant_dynamic-update-slice_fusion.8.rest_0_), channel_id=1, source_target_pairs={{0,16},{4,20},{8,24},{12,28},{16,0},{20,4},{24,8},{28,12},{1,17},{... | collective-permute-start | bytes 589832 | tf_op jit(solution)/shard_map/ppermute | solution.py:29
  133.0 7.3 %collective-permute-start.39 = (bf16[256,384]{1,0:T(8,128)(2,1)S(1)}, bf16[256,384]{1,0:T(8,128)(2,1)S(1)}, u32[]{:S(2)}, u32[]{:S(2)}) collective-permute-start(bf16[256,384]{1,0:T(8,128)(2,1)S(1)} %constant_dynamic-update-slice_fusion.8.rest_0_), channel_id=1, source_target_pairs={{0,8},{4,12},{8,0},{12,4},{16,24},{20,28},{24,16},{28,20},{1,9},{5... | collective-permute-start | bytes 589832 | tf_op jit(solution)/shard_map/ppermute | solution.py:29
  134.0 5.0 %collective-permute-start.49 = (bf16[128,384]{1,0:T(8,128)(2,1)S(1)}, bf16[128,384]{1,0:T(8,128)(2,1)S(1)}, u32[]{:S(2)}, u32[]{:S(2)}) collective-permute-start(bf16[128,384]{1,0:T(8,128)(2,1)S(1)} %constant_dynamic-update-slice_fusion.12.rest_8_), channel_id=1, source_target_pairs={{0,1},{1,0},{2,3},{3,2},{4,5},{5,4},{6,7},{7,6},{8,9},{9,8},{10,11... | collective-permute-start | bytes 294920 | tf_op jit(solution)/shard_map/ppermute | solution.py:29
  150.6 4.6 %collective-permute-start.56 = (bf16[304,128]{1,0:T(8,128)(2,1)S(1)}, bf16[304,128]{1,0:T(8,128)(2,1)S(1)}, u32[]{:S(2)}, u32[]{:S(2)}) collective-permute-start(bf16[304,128]{1,0:T(8,128)(2,1)S(1)} %get-tuple-element.75), channel_id=1, source_target_pairs={{0,1},{1,0},{2,3},{3,2},{4,5},{5,4},{6,7},{7,6},{8,9},{9,8},{10,11... | collective-permute-start | bytes 233480 | tf_op jit(solution)/shard_map/ppermute | solution.py:29
  152.3 9.2 %collective-permute-start.57 = (bf16[304,128]{1,0:T(8,128)(2,1)S(1)}, bf16[304,128]{1,0:T(8,128)(2,1)S(1)}, u32[]{:S(2)}, u32[]{:S(2)}) collective-permute-start(bf16[304,128]{1,0:T(8,128)(2,1)S(1)} %get-tuple-element.76), channel_id=1, source_target_pairs={{0,2},{1,3},{2,0},{3,1},{4,6},{5,7},{6,4},{7,5},{8,10},{9,11},{10,... | collective-permute-start | bytes 233480 | tf_op jit(solution)/shard_map/ppermute | solution.py:29
  153.3 8.3 %collective-permute-start.58 = (bf16[304,128]{1,0:T(8,128)(2,1)S(1)}, bf16[304,128]{1,0:T(8,128)(2,1)S(1)}, u32[]{:S(2)}, u32[]{:S(2)}) collective-permute-start(bf16[304,128]{1,0:T(8,128)(2,1)S(1)} %get-tuple-element.77), channel_id=1, source_target_pairs={{0,3},{1,2},{2,1},{3,0},{4,7},{5,6},{6,5},{7,4},{8,11},{9,10},{10,... | collective-permute-start | bytes 233480 | tf_op jit(solution)/shard_map/ppermute | solution.py:29
  162.4 3.7 %collective-permute-start.59 = (f32[8,128]{1,0:T(8,128)S(1)}, f32[8,128]{1,0:T(8,128)S(1)}, u32[]{:S(2)}, u32[]{:S(2)}) collective-permute-start(f32[8,128]{1,0:T(8,128)S(1)} %get-tuple-element.78), channel_id=1, source_target_pairs={{0,1},{1,0},{2,3},{3,2},{4,5},{5,4},{6,7},{7,6},{8,9},{9,8},{10,11... | collective-permute-start | bytes 12296 | tf_op jit(solution)/shard_map/ppermute | solution.py:29
  166.1 4.5 %collective-permute-start.60 = (f32[8,128]{1,0:T(8,128)S(1)}, f32[8,128]{1,0:T(8,128)S(1)}, u32[]{:S(2)}, u32[]{:S(2)}) collective-permute-start(f32[8,128]{1,0:T(8,128)S(1)} %add.6), channel_id=1, source_target_pairs={{0,2},{1,3},{2,0},{3,1},{4,6},{5,7},{6,4},{7,5},{8,10},{9,11},{10,... | collective-permute-start | bytes 12296 | tf_op jit(solution)/shard_map/ppermute | solution.py:29
  (23 other events, 146.1 us)
where the time goes:
time: 181 us
  starting transfers between devices  64.6 us (36%)
  waiting for transfers between devices  51.8 us (29%)
  Pallas kernels  31.3 us (17%)
  blocking collectives  26.5 us (15%)
  local copies, waits for them, and re-layouts  4.42 us (2%)
  between operations  1.82 us (1%)
    ppermute x61, starting transfers between devices, exchange(): return lax.ppermute(array, axis, [(i, i ^ flip) for i in range(count)])  64.6 us
    ppermute x61, waiting for transfers between devices, exchange(): return lax.ppermute(array, axis, [(i, i ^ flip) for i in range(count)])  51.8 us
    pallas_call x3, Pallas kernels, apply_local(): pl.pallas_call(functools.partial(apply_kernel, sectors, term_count, len(a...  25.3 us
    all_gather x2, blocking collectives, local(): sums = lax.all_gather(stats, 'sector', axis=0, tiled=True)  18 us
    all_gather x1, blocking collectives, local(): sums = lax.all_gather(products, 'sector', axis=0, tiled=True)  8.58 us
    unnamed x32, local copies, waits for them, and re-layouts  4.37 us
  transfers between devices with their start and end apart: 61, of which 22 were waited for; matrix products, arithmetic and copies ran while one was open for 0% of the time, Pallas kernels for 1%

commit v1 on v0

--- a/solution.py
+++ b/solution.py
@@ -35,12 +35,31 @@
     return parts[0]
 
 
-def sum_term(values, term_count):
-    flip = 1
-    while flip < term_count:
-        values = values + exchange(values, "term", flip)
-        flip *= 2
-    return values
+def exchange_by_core(array, axis, flips):
+    sectors, term_count = lax.axis_size("sector"), lax.axis_size("term")
+    pairs = []
+    for sector in range(sectors):
+        for term in range(term_count):
+            flip = flips[sector % 2]
+            there = (sector ^ flip, term) if axis == "sector" else (sector, term ^ flip)
+            pairs.append((sector * term_count + term, there[0] * term_count + there[1]))
+    return lax.ppermute(array, ("sector", "term"), pairs)
+
+
+def sum_over(values, axis, count, unit):
+    if count == 1:
+        return values
+    widest = count - 1
+    sums = [values + exchange(values, axis, unit * widest)]
+    for flip in range(1, count // 2):
+        one = exchange_by_core(values, axis, (unit * flip, unit * (flip ^ widest)))
+        sums.append(one + exchange(one, "sector", 1))
+    return tree(sums)
+
+
+def sum_sector(values, sectors):
+    values = values + exchange(values, "sector", 1)
+    return sum_over(values, "sector", sectors // 2, 2)
 
 
 def gather_ordered(rows, term_count):
@@ -268,7 +287,7 @@
     slots = weights.shape[0]
     envs, size, _ = left.shape
     share = size // term_count
-    unroll = next(u for u in (4, 2, 1) if slots % u == 0)
+    unroll = next(u for u in (5, 4, 2, 1) if slots % u == 0)
     kinds = [F32] + [BF16] * (term_count - 1)
     return pl.pallas_call(
         functools.partial(apply_kernel, sectors, term_count, len(arrays), unroll),
@@ -324,11 +343,6 @@
     )(*chunks)
 
 
-def summed(sums):
-    rows = sums.shape[0]
-    return tree_any([sums[i : i + SUBLANES] for i in range(0, rows, SUBLANES)])
-
-
 def first_kernel(rows, *out):
     *pieces, overlap, square = out
     held = rows[...]
@@ -380,7 +394,7 @@
     *rest,
 ):
     *pieces, overlap, square, quotient, scale_out = rest
-    stats = summed(sums)
+    stats = sums[...]
     ratio = stats[:1, :1] / stats[1:2, :1]
     if position > 0:
         mean = stats[2:3, :1] / cell_count
@@ -470,7 +484,7 @@
 ):
     earlier, (out, quotients) = rest[:position], rest[position:]
 
-    stats = summed(sums)
+    stats = sums[...]
 
     def total(i):
         return stats[i : i + 1, :1]
@@ -549,7 +563,7 @@
             arrived.append(exchange(chunks[flip], "term", flip))
         if position < APPS - 1:
             applied, stats = collect(arrived, current.shape)
-            sums = lax.all_gather(stats, "sector", axis=0, tiled=True)
+            sums = sum_sector(stats, sectors)
             following, pieces, overlap, square, quotient, scale_new = advance(
                 cell_count,
                 position,
@@ -567,8 +581,7 @@
             applied, products = closing(
                 position, lanczos_beta, scale, current, previous, diagonal, arrived
             )
-            products = sum_term(products, term_count)
-            sums = lax.all_gather(products, "sector", axis=0, tiled=True)
+            sums = sum_over(sum_sector(products, sectors), "term", term_count, 1)
             current, quotients = final(
                 cell_count,
                 position,

time: 181 us -> 174 us (0.961)
  blocking collectives: 26.5 us -> 0 us
  waiting for transfers between devices: 51.8 us -> 62.5 us
  starting transfers between devices: 64.6 us -> 73.4 us
    all_gather x3 -> x0, blocking collectives: 26.5 us -> none  [the longest x2 18 us: local(): sums = lax.all_gather(stats, 'sector', axis=0, tiled=True)]
    ppermute x61 -> x70, waiting for transfers between devices: 51.8 us -> 59.7 us  [exchange(): return lax.ppermute(array, axis, [(i, i ^ flip) for i in range(count)])]
    ppermute x0 -> x4, starting transfers between devices: none -> 5.02 us  [exchange_by_core(): return lax.ppermute(array, ('sector', 'term'), pairs)]
    ppermute x61 -> x70, starting transfers between devices: 64.6 us -> 68.3 us  [exchange(): return lax.ppermute(array, axis, [(i, i ^ flip) for i in range(count)])]
    ppermute x0 -> x4, waiting for transfers between devices: none -> 2.83 us  [exchange_by_core(): return lax.ppermute(array, ('sector', 'term'), pairs)]
  transfers between devices with their start and end apart: 61 -> 74, of which waited for: 22 -> 30; matrix products, arithmetic and copies ran while one was open for 0% -> 0% of each run, Pallas kernels for 1% -> 1%
where the time goes in v1:
time: 174 us; the launch traced here: 173 us
  starting transfers between devices  73.4 us (42%)
  waiting for transfers between devices  62.5 us (36%)
  Pallas kernels  30.9 us (18%)
  local copies, waits for them, and re-layouts  4.42 us (3%)
  between operations  1.89 us (1%)
    ppermute x70, starting transfers between devices, exchange(): return lax.ppermute(array, axis, [(i, i ^ flip) for i in range(count)])  68.3 us
    ppermute x70, waiting for transfers between devices, exchange(): return lax.ppermute(array, axis, [(i, i ^ flip) for i in range(count)])  59.7 us
    pallas_call x3, Pallas kernels, apply_local(): pl.pallas_call(functools.partial(apply_kernel, sectors, term_count, len(a...  24.9 us
    ppermute x4, starting transfers between devices, exchange_by_core(): return lax.ppermute(array, ('sector', 'term'), pairs)  5.02 us
    unnamed x32, local copies, waits for them, and re-layouts  4.37 us
  transfers between devices with their start and end apart: 74, of which 30 were waited for; matrix products, arithmetic and copies ran while one was open for 0% of the time, Pallas kernels for 1%

profile of v1, /device:TPU:0, one launch (start us, length us, event | category | flops | bytes accessed | tf_op | source)
XLA Modules:
  0.0 173.3 jit_solution(8092499247882316510)
XLA Ops:
  1.6 3.1 %collective-permute-start.2 = (bf16[96,384]{1,0:T(8,128)(2,1)S(1)}, bf16[96,384]{1,0:T(8,128)(2,1)S(1)}, u32[]{:S(2)}, u32[]{:S(2)}) collective-permute-start(bf16[96,384]{1,0:T(8,128)(2,1)S(1)} %get-tuple-element.49), channel_id=1, source_target_pairs={{0,1},{1,0},{2,3},{3,2},{4,5},{5,4},{6,7},{7,6},{8,9},{9,8},{10,11... | collective-permute-start | bytes 221192 | tf_op jit(solution)/shard_map/ppermute | solution.py:29
  4.7 2.6 %collective-permute-start.1 = (bf16[96,384]{1,0:T(8,128)(2,1)S(1)}, bf16[96,384]{1,0:T(8,128)(2,1)S(1)}, u32[]{:S(2)}, u32[]{:S(2)}) collective-permute-start(bf16[96,384]{1,0:T(8,128)(2,1)S(1)} %get-tuple-element.49), channel_id=1, source_target_pairs={{0,2},{1,3},{2,0},{3,1},{4,6},{5,7},{6,4},{7,5},{8,10},{9,11},{10,... | collective-permute-start | bytes 221192 | tf_op jit(solution)/shard_map/ppermute | solution.py:29
  7.3 5.2 %collective-permute-done.1 = bf16[96,384]{1,0:T(8,128)(2,1)S(1)} collective-permute-done((bf16[96,384]{1,0:T(8,128)(2,1)S(1)}, bf16[96,384]{1,0:T(8,128)(2,1)S(1)}, u32[]{:S(2)}, u32[]{:S(2)}) %collective-permute-start.1) | collective-permute-done | bytes 73760 | tf_op jit(solution)/shard_map/ppermute | solution.py:29
  13.6 2.5 %collective-permute-start.5 = (bf16[384,384]{1,0:T(8,128)(2,1)S(1)}, bf16[384,384]{1,0:T(8,128)(2,1)S(1)}, u32[]{:S(2)}, u32[]{:S(2)}) collective-permute-start(bf16[384,384]{1,0:T(8,128)(2,1)S(1)} %pad_maximum_fusion.rest_0_), channel_id=1, source_target_pairs={{0,24},{4,28},{8,16},{12,20},{16,8},{20,12},{24,0},{28,4},{1,25},{... | collective-permute-start | bytes 884744 | tf_op jit(solution)/shard_map/ppermute | solution.py:29
  17.2 7.3 %collective-permute-done.5.rest_3_ = bf16[384,384]{1,0:T(8,128)(2,1)S(1)} collective-permute-done((bf16[384,384]{1,0:T(8,128)(2,1)S(1)}, bf16[384,384]{1,0:T(8,128)(2,1)S(1)}, u32[]{:S(2)}, u32[]{:S(2)}) %collective-permute-start.5) | collective-permute-done | bytes 294944 | tf_op jit(solution)/shard_map/ppermute | solution.py:29
  24.5 3.4 %collective-permute-done.4.rest_2_ = bf16[384,384]{1,0:T(8,128)(2,1)S(1)} collective-permute-done((bf16[384,384]{1,0:T(8,128)(2,1)S(1)}, bf16[384,384]{1,0:T(8,128)(2,1)S(1)}, u32[]{:S(2)}, u32[]{:S(2)}) %collective-permute-start.4) | collective-permute-done | bytes 294944 | tf_op jit(solution)/shard_map/ppermute | solution.py:29
  29.0 1.7 copy-done
  30.7 1.7 copy-done.1
  34.9 8.2 %apply_triples.3 = (f32[304,128]{1,0:T(8,128)S(1)}, bf16[304,128]{1,0:T(8,128)(2,1)S(1)}, bf16[304,128]{1,0:T(8,128)(2,1)S(1)}, bf16[304,128]{1,0:T(8,128)(2,1)S(1)}) custom-call(s32[3,20]{1,0:T(4,128)S(1)} %get-tuple-element.43.table, f32[20]{0:T(128)S(1)} %get-tuple-element.44.weights, s32[2]{0:T(128)S(1)} %pad_add_fusion.place, ...), custom_call_target="tpu_custom_call" | custom-call | flops 4076863488 | bytes 7372800 | tf_op jit(solution)/shard_map/apply_triples/pallas_call | solution.py:292
  43.2 1.3 collective-permute-start.10
  44.5 1.6 collective-permute-start.11
  46.1 1.5 collective-permute-start.12
  47.6 6.0 %collective-permute-done.11.rest_2_ = bf16[304,128]{1,0:T(8,128)(2,1)S(1)} collective-permute-done((bf16[304,128]{1,0:T(8,128)(2,1)S(1)}, bf16[304,128]{1,0:T(8,128)(2,1)S(1)}, u32[]{:S(2)}, u32[]{:S(2)}) %collective-permute-start.11) | collective-permute-done | bytes 77856 | tf_op jit(solution)/shard_map/ppermute | solution.py:29
  54.9 1.5 collective-permute-start.15
  56.4 1.5 collective-permute-start.14
  58.5 2.4 %collective-permute-done.14 = f32[8,128]{1,0:T(8,128)S(1)} collective-permute-done((f32[8,128]{1,0:T(8,128)S(1)}, f32[8,128]{1,0:T(8,128)S(1)}, u32[]{:S(2)}, u32[]{:S(2)}) %collective-permute-start.14) | collective-permute-done | bytes 4128 | tf_op jit(solution)/shard_map/ppermute | solution.py:29
  61.7 1.6 collective-permute-start.29
  63.7 1.5 collective-permute-start.27
  65.2 2.2 %collective-permute-start.19 = (bf16[64,384]{1,0:T(8,128)(2,1)S(1)}, bf16[64,384]{1,0:T(8,128)(2,1)S(1)}, u32[]{:S(2)}, u32[]{:S(2)}) collective-permute-start(bf16[64,384]{1,0:T(8,128)(2,1)S(1)} %get-tuple-element.59), channel_id=1, source_target_pairs={{0,3},{1,2},{2,1},{3,0},{4,7},{5,6},{6,5},{7,4},{8,11},{9,10},{10,... | collective-permute-start | bytes 147464 | tf_op jit(solution)/shard_map/ppermute | solution.py:29
  69.8 2.2 %collective-permute-start.32 = (bf16[128,384]{1,0:T(8,128)(2,1)S(1)}, bf16[128,384]{1,0:T(8,128)(2,1)S(1)}, u32[]{:S(2)}, u32[]{:S(2)}) collective-permute-start(bf16[128,384]{1,0:T(8,128)(2,1)S(1)} %constant_dynamic-update-slice_fusion.4.rest_8_), channel_id=1, source_target_pairs={{0,3},{1,2},{2,1},{3,0},{4,7},{5,6},{6,5},{7,4},{8,11},{9,10},{10,... | collective-permute-start | bytes 294920 | tf_op jit(solution)/shard_map/ppermute | solution.py:29
  72.9 1.6 collective-permute-start.31
  74.5 1.7 collective-permute-start.22
  78.1 2.4 %collective-permute-start.30 = (bf16[128,384]{1,0:T(8,128)(2,1)S(1)}, bf16[128,384]{1,0:T(8,128)(2,1)S(1)}, u32[]{:S(2)}, u32[]{:S(2)}) collective-permute-start(bf16[128,384]{1,0:T(8,128)(2,1)S(1)} %constant_dynamic-update-slice_fusion.4.rest_8_), channel_id=1, source_target_pairs={{0,1},{1,0},{2,3},{3,2},{4,5},{5,4},{6,7},{7,6},{8,9},{9,8},{10,11... | collective-permute-start | bytes 294920 | tf_op jit(solution)/shard_map/ppermute | solution.py:29
  81.7 1.5 collective-permute-done.30.rest_9_
  86.1 8.4 %apply_triples.4 = (f32[304,128]{1,0:T(8,128)S(1)}, bf16[304,128]{1,0:T(8,128)(2,1)S(1)}, bf16[304,128]{1,0:T(8,128)(2,1)S(1)}, bf16[304,128]{1,0:T(8,128)(2,1)S(1)}) custom-call(s32[3,20]{1,0:T(4,128)S(1)} %get-tuple-element.43.table, f32[20]{0:T(128)S(1)} %get-tuple-element.44.weights, s32[2]{0:T(128)S(1)} %pad_add_fusion.place, ...), custom_call_target="tpu_custom_call" | custom-call | flops 4076863488 | bytes 7372800 | tf_op jit(solution)/shard_map/apply_triples/pallas_call | solution.py:292
  94.6 2.0 %collective-permute-start.37 = (bf16[304,128]{1,0:T(8,128)(2,1)S(1)}, bf16[304,128]{1,0:T(8,128)(2,1)S(1)}, u32[]{:S(2)}, u32[]{:S(2)}) collective-permute-start(bf16[304,128]{1,0:T(8,128)(2,1)S(1)} %get-tuple-element.62), channel_id=1, source_target_pairs={{0,1},{1,0},{2,3},{3,2},{4,5},{5,4},{6,7},{7,6},{8,9},{9,8},{10,11... | collective-permute-start | bytes 233480 | tf_op jit(solution)/shard_map/ppermute | solution.py:29
  96.6 1.7 collective-permute-start.38
  99.3 6.4 %collective-permute-done.38.rest_2_ = bf16[304,128]{1,0:T(8,128)(2,1)S(1)} collective-permute-done((bf16[304,128]{1,0:T(8,128)(2,1)S(1)}, bf16[304,128]{1,0:T(8,128)(2,1)S(1)}, u32[]{:S(2)}, u32[]{:S(2)}) %collective-permute-start.38) | collective-permute-done | bytes 77856 | tf_op jit(solution)/shard_map/ppermute | solution.py:29
  108.1 1.5 collective-permute-start.41
  110.7 2.0 %collective-permute-done.41 = f32[8,128]{1,0:T(8,128)S(1)} collective-permute-done((f32[8,128]{1,0:T(8,128)S(1)}, f32[8,128]{1,0:T(8,128)S(1)}, u32[]{:S(2)}, u32[]{:S(2)}) %collective-permute-start.41) | collective-permute-done | bytes 4128 | tf_op jit(solution)/shard_map/ppermute | solution.py:29
  113.3 1.5 collective-permute-start.56
  116.9 2.2 %collective-permute-start.46 = (bf16[64,384]{1,0:T(8,128)(2,1)S(1)}, bf16[64,384]{1,0:T(8,128)(2,1)S(1)}, u32[]{:S(2)}, u32[]{:S(2)}) collective-permute-start(bf16[64,384]{1,0:T(8,128)(2,1)S(1)} %get-tuple-element.72), channel_id=1, source_target_pairs={{0,3},{1,2},{2,1},{3,0},{4,7},{5,6},{6,5},{7,4},{8,11},{9,10},{10,... | collective-permute-start | bytes 147464 | tf_op jit(solution)/shard_map/ppermute | solution.py:29
  119.9 1.4 collective-permute-start.44
  121.5 2.4 %collective-permute-start.59 = (bf16[128,384]{1,0:T(8,128)(2,1)S(1)}, bf16[128,384]{1,0:T(8,128)(2,1)S(1)}, u32[]{:S(2)}, u32[]{:S(2)}) collective-permute-start(bf16[128,384]{1,0:T(8,128)(2,1)S(1)} %constant_dynamic-update-slice_fusion.12.rest_8_), channel_id=1, source_target_pairs={{0,3},{1,2},{2,1},{3,0},{4,7},{5,6},{6,5},{7,4},{8,11},{9,10},{10,... | collective-permute-start | bytes 294920 | tf_op jit(solution)/shard_map/ppermute | solution.py:29
  124.5 1.9 %collective-permute-start.58 = (bf16[128,384]{1,0:T(8,128)(2,1)S(1)}, bf16[128,384]{1,0:T(8,128)(2,1)S(1)}, u32[]{:S(2)}, u32[]{:S(2)}) collective-permute-start(bf16[128,384]{1,0:T(8,128)(2,1)S(1)} %constant_dynamic-update-slice_fusion.12.rest_8_), channel_id=1, source_target_pairs={{0,2},{1,3},{2,0},{3,1},{4,6},{5,7},{6,4},{7,5},{8,10},{9,11},{10,... | collective-permute-start | bytes 294920 | tf_op jit(solution)/shard_map/ppermute | solution.py:29
  126.4 1.5 collective-permute-start.49
  129.9 2.0 %collective-permute-start.57 = (bf16[128,384]{1,0:T(8,128)(2,1)S(1)}, bf16[128,384]{1,0:T(8,128)(2,1)S(1)}, u32[]{:S(2)}, u32[]{:S(2)}) collective-permute-start(bf16[128,384]{1,0:T(8,128)(2,1)S(1)} %constant_dynamic-update-slice_fusion.12.rest_8_), channel_id=1, source_target_pairs={{0,1},{1,0},{2,3},{3,2},{4,5},{5,4},{6,7},{7,6},{8,9},{9,8},{10,11... | collective-permute-start | bytes 294920 | tf_op jit(solution)/shard_map/ppermute | solution.py:29
  133.2 1.7 collective-permute-done.57.rest_9_
  138.0 8.2 %apply_triples.5 = (f32[304,128]{1,0:T(8,128)S(1)}, bf16[304,128]{1,0:T(8,128)(2,1)S(1)}, bf16[304,128]{1,0:T(8,128)(2,1)S(1)}, bf16[304,128]{1,0:T(8,128)(2,1)S(1)}) custom-call(s32[3,20]{1,0:T(4,128)S(1)} %get-tuple-element.43.table, f32[20]{0:T(128)S(1)} %get-tuple-element.44.weights, s32[2]{0:T(128)S(1)} %pad_add_fusion.place, ...), custom_call_target="tpu_custom_call" | custom-call | flops 4076863488 | bytes 7372800 | tf_op jit(solution)/shard_map/apply_triples/pallas_call | solution.py:292
  146.2 1.8 %collective-permute-start.64 = (bf16[304,128]{1,0:T(8,128)(2,1)S(1)}, bf16[304,128]{1,0:T(8,128)(2,1)S(1)}, u32[]{:S(2)}, u32[]{:S(2)}) collective-permute-start(bf16[304,128]{1,0:T(8,128)(2,1)S(1)} %get-tuple-element.75), channel_id=1, source_target_pairs={{0,1},{1,0},{2,3},{3,2},{4,5},{5,4},{6,7},{7,6},{8,9},{9,8},{10,11... | collective-permute-start | bytes 233480 | tf_op jit(solution)/shard_map/ppermute | solution.py:29
  149.0 1.7 collective-permute-start.66
  150.8 6.5 %collective-permute-done.65.rest_2_ = bf16[304,128]{1,0:T(8,128)(2,1)S(1)} collective-permute-done((bf16[304,128]{1,0:T(8,128)(2,1)S(1)}, bf16[304,128]{1,0:T(8,128)(2,1)S(1)}, u32[]{:S(2)}, u32[]{:S(2)}) %collective-permute-start.65) | collective-permute-done | bytes 77856 | tf_op jit(solution)/shard_map/ppermute | solution.py:29
  160.3 1.5 collective-permute-start.68
  163.0 1.8 %collective-permute-done.68 = f32[8,128]{1,0:T(8,128)S(1)} collective-permute-done((f32[8,128]{1,0:T(8,128)S(1)}, f32[8,128]{1,0:T(8,128)S(1)}, u32[]{:S(2)}, u32[]{:S(2)}) %collective-permute-start.68) | collective-permute-done | bytes 4128 | tf_op jit(solution)/shard_map/ppermute | solution.py:29
  164.8 1.5 collective-permute-start.72
  166.3 2.2 %collective-permute-start.71 = (f32[8,128]{1,0:T(8,128)S(1)}, f32[8,128]{1,0:T(8,128)S(1)}, u32[]{:S(2)}, u32[]{:S(2)}) collective-permute-start(f32[8,128]{1,0:T(8,128)S(1)} %add_add_fusion.1), channel_id=1, source_target_pairs={{0,3},{1,2},{2,1},{3,0},{4,7},{5,6},{6,5},{7,4},{8,11},{9,10},{10,... | collective-permute-start | bytes 12296 | tf_op jit(solution)/shard_map/ppermute | solution.py:29
  168.6 3.2 %collective-permute-done.71 = f32[8,128]{1,0:T(8,128)S(1)} collective-permute-done((f32[8,128]{1,0:T(8,128)S(1)}, f32[8,128]{1,0:T(8,128)S(1)}, u32[]{:S(2)}, u32[]{:S(2)}) %collective-permute-start.71) | collective-permute-done | bytes 4128 | tf_op jit(solution)/shard_map/ppermute | solution.py:29
  171.8 1.4 final_vector.1
  (159 shorter events, 39.0 us)
Async XLA Ops:
  1.6 5.7 %collective-permute-start.2 = (bf16[96,384]{1,0:T(8,128)(2,1)S(1)}, bf16[96,384]{1,0:T(8,128)(2,1)S(1)}, u32[]{:S(2)}, u32[]{:S(2)}) collective-permute-start(bf16[96,384]{1,0:T(8,128)(2,1)S(1)} %get-tuple-element.49), channel_id=1, source_target_pairs={{0,1},{1,0},{2,3},{3,2},{4,5},{5,4},{6,7},{7,6},{8,9},{9,8},{10,11... | collective-permute-start | bytes 221192 | tf_op jit(solution)/shard_map/ppermute | solution.py:29
  4.7 7.8 %collective-permute-start.1 = (bf16[96,384]{1,0:T(8,128)(2,1)S(1)}, bf16[96,384]{1,0:T(8,128)(2,1)S(1)}, u32[]{:S(2)}, u32[]{:S(2)}) collective-permute-start(bf16[96,384]{1,0:T(8,128)(2,1)S(1)} %get-tuple-element.49), channel_id=1, source_target_pairs={{0,2},{1,3},{2,0},{3,1},{4,6},{5,7},{6,4},{7,5},{8,10},{9,11},{10,... | collective-permute-start | bytes 221192 | tf_op jit(solution)/shard_map/ppermute | solution.py:29
  7.3 6.3 %collective-permute-start = (bf16[96,384]{1,0:T(8,128)(2,1)S(1)}, bf16[96,384]{1,0:T(8,128)(2,1)S(1)}, u32[]{:S(2)}, u32[]{:S(2)}) collective-permute-start(bf16[96,384]{1,0:T(8,128)(2,1)S(1)} %get-tuple-element.49), channel_id=1, source_target_pairs={{0,3},{1,2},{2,1},{3,0},{4,7},{5,6},{6,5},{7,4},{8,11},{9,10},{10,... | collective-permute-start | bytes 221192 | tf_op jit(solution)/shard_map/ppermute | solution.py:29
  13.6 10.9 %collective-permute-start.5 = (bf16[384,384]{1,0:T(8,128)(2,1)S(1)}, bf16[384,384]{1,0:T(8,128)(2,1)S(1)}, u32[]{:S(2)}, u32[]{:S(2)}) collective-permute-start(bf16[384,384]{1,0:T(8,128)(2,1)S(1)} %pad_maximum_fusion.rest_0_), channel_id=1, source_target_pairs={{0,24},{4,28},{8,16},{12,20},{16,8},{20,12},{24,0},{28,4},{1,25},{... | collective-permute-start | bytes 884744 | tf_op jit(solution)/shard_map/ppermute | solution.py:29
  16.2 11.7 %collective-permute-start.4 = (bf16[384,384]{1,0:T(8,128)(2,1)S(1)}, bf16[384,384]{1,0:T(8,128)(2,1)S(1)}, u32[]{:S(2)}, u32[]{:S(2)}) collective-permute-start(bf16[384,384]{1,0:T(8,128)(2,1)S(1)} %pad_maximum_fusion.rest_0_), channel_id=1, source_target_pairs={{0,16},{4,20},{8,24},{12,28},{16,0},{20,4},{24,8},{28,12},{1,17},{... | collective-permute-start | bytes 884744 | tf_op jit(solution)/shard_map/ppermute | solution.py:29
  16.7 11.3 %collective-permute-start.3 = (bf16[384,384]{1,0:T(8,128)(2,1)S(1)}, bf16[384,384]{1,0:T(8,128)(2,1)S(1)}, u32[]{:S(2)}, u32[]{:S(2)}) collective-permute-start(bf16[384,384]{1,0:T(8,128)(2,1)S(1)} %pad_maximum_fusion.rest_0_), channel_id=1, source_target_pairs={{0,8},{4,12},{8,0},{12,4},{16,24},{20,28},{24,16},{28,20},{1,9},{5... | collective-permute-start | bytes 884744 | tf_op jit(solution)/shard_map/ppermute | solution.py:29
  17.2 17.7 %collective-permute-start.6 = (bf16[384,384]{1,0:T(8,128)(2,1)S(1)}, bf16[384,384]{1,0:T(8,128)(2,1)S(1)}, u32[]{:S(2)}, u32[]{:S(2)}) collective-permute-start(bf16[384,384]{1,0:T(8,128)(2,1)S(1)} %pad_maximum_fusion.rest_0_), channel_id=1, source_target_pairs={{0,4},{4,0},{8,12},{12,8},{16,20},{20,16},{24,28},{28,24},{1,5},{5... | collective-permute-start | bytes 884744 | tf_op jit(solution)/shard_map/ppermute | solution.py:29
  24.5 10.4 %collective-permute-start.9 = (bf16[384,384]{1,0:T(8,128)(2,1)S(1)}, bf16[384,384]{1,0:T(8,128)(2,1)S(1)}, u32[]{:S(2)}, u32[]{:S(2)}) collective-permute-start(bf16[384,384]{1,0:T(8,128)(2,1)S(1)} %collective-permute-done.5.rest_3_), channel_id=1, source_target_pairs={{0,4},{4,0},{8,12},{12,8},{16,20},{20,16},{24,28},{28,24},{1,5},{5... | collective-permute-start | bytes 884744 | tf_op jit(solution)/shard_map/ppermute | solution.py:29
  27.9 7.0 %collective-permute-start.8 = (bf16[384,384]{1,0:T(8,128)(2,1)S(1)}, bf16[384,384]{1,0:T(8,128)(2,1)S(1)}, u32[]{:S(2)}, u32[]{:S(2)}) collective-permute-start(bf16[384,384]{1,0:T(8,128)(2,1)S(1)} %collective-permute-done.4.rest_2_), channel_id=1, source_target_pairs={{0,4},{4,0},{8,12},{12,8},{16,20},{20,16},{24,28},{28,24},{1,5},{5... | collective-permute-start | bytes 884744 | tf_op jit(solution)/shard_map/ppermute | solution.py:29
  28.0 6.9 %collective-permute-start.7 = (bf16[384,384]{1,0:T(8,128)(2,1)S(1)}, bf16[384,384]{1,0:T(8,128)(2,1)S(1)}, u32[]{:S(2)}, u32[]{:S(2)}) collective-permute-start(bf16[384,384]{1,0:T(8,128)(2,1)S(1)} %collective-permute-done.3.rest_1_), channel_id=1, source_target_pairs={{0,4},{4,0},{8,12},{12,8},{16,20},{20,16},{24,28},{28,24},{1,5},{5... | collective-permute-start | bytes 884744 | tf_op jit(solution)/shard_map/ppermute | solution.py:29
  43.2 4.5 %collective-permute-start.10 = (bf16[304,128]{1,0:T(8,128)(2,1)S(1)}, bf16[304,128]{1,0:T(8,128)(2,1)S(1)}, u32[]{:S(2)}, u32[]{:S(2)}) collective-permute-start(bf16[304,128]{1,0:T(8,128)(2,1)S(1)} %get-tuple-element.51), channel_id=1, source_target_pairs={{0,1},{1,0},{2,3},{3,2},{4,5},{5,4},{6,7},{7,6},{8,9},{9,8},{10,11... | collective-permute-start | bytes 233480 | tf_op jit(solution)/shard_map/ppermute | solution.py:29
  44.5 9.1 %collective-permute-start.11 = (bf16[304,128]{1,0:T(8,128)(2,1)S(1)}, bf16[304,128]{1,0:T(8,128)(2,1)S(1)}, u32[]{:S(2)}, u32[]{:S(2)}) collective-permute-start(bf16[304,128]{1,0:T(8,128)(2,1)S(1)} %get-tuple-element.52), channel_id=1, source_target_pairs={{0,2},{1,3},{2,0},{3,1},{4,6},{5,7},{6,4},{7,5},{8,10},{9,11},{10,... | collective-permute-start | bytes 233480 | tf_op jit(solution)/shard_map/ppermute | solution.py:29
  46.1 7.5 %collective-permute-start.12 = (bf16[304,128]{1,0:T(8,128)(2,1)S(1)}, bf16[304,128]{1,0:T(8,128)(2,1)S(1)}, u32[]{:S(2)}, u32[]{:S(2)}) collective-permute-start(bf16[304,128]{1,0:T(8,128)(2,1)S(1)} %get-tuple-element.53), channel_id=1, source_target_pairs={{0,3},{1,2},{2,1},{3,0},{4,7},{5,6},{6,5},{7,4},{8,11},{9,10},{10,... | collective-permute-start | bytes 233480 | tf_op jit(solution)/shard_map/ppermute | solution.py:29
  56.4 4.5 %collective-permute-start.14 = (f32[8,128]{1,0:T(8,128)S(1)}, f32[8,128]{1,0:T(8,128)S(1)}, u32[]{:S(2)}, u32[]{:S(2)}) collective-permute-start(f32[8,128]{1,0:T(8,128)S(1)} %add.45), channel_id=1, source_target_pairs={{0,24},{4,28},{8,16},{12,20},{16,8},{20,12},{24,0},{28,4},{1,25},{... | collective-permute-start | bytes 12296 | tf_op jit(solution)/shard_map/ppermute | solution.py:29
  61.7 8.1 %collective-permute-start.29 = (bf16[32,384]{1,0:T(8,128)(2,1)S(1)}, bf16[32,384]{1,0:T(8,128)(2,1)S(1)}, u32[]{:S(2)}, u32[]{:S(2)}) collective-permute-start(bf16[32,384]{1,0:T(8,128)(2,1)S(1)} %get-tuple-element.60), channel_id=1, source_target_pairs={{0,24},{4,28},{8,16},{12,20},{16,8},{20,12},{24,0},{28,4},{1,25},{... | collective-permute-start | bytes 73736 | tf_op jit(solution)/shard_map/ppermute | solution.py:29
  63.2 6.5 %collective-permute-start.28 = (bf16[32,384]{1,0:T(8,128)(2,1)S(1)}, bf16[32,384]{1,0:T(8,128)(2,1)S(1)}, u32[]{:S(2)}, u32[]{:S(2)}) collective-permute-start(bf16[32,384]{1,0:T(8,128)(2,1)S(1)} %get-tuple-element.60), channel_id=1, source_target_pairs={{0,16},{4,20},{8,24},{12,28},{16,0},{20,4},{24,8},{28,12},{1,17},{... | collective-permute-start | bytes 73736 | tf_op jit(solution)/shard_map/ppermute | solution.py:29
  63.7 4.7 %collective-permute-start.27 = (bf16[32,384]{1,0:T(8,128)(2,1)S(1)}, bf16[32,384]{1,0:T(8,128)(2,1)S(1)}, u32[]{:S(2)}, u32[]{:S(2)}) collective-permute-start(bf16[32,384]{1,0:T(8,128)(2,1)S(1)} %get-tuple-element.60), channel_id=1, source_target_pairs={{0,8},{4,12},{8,0},{12,4},{16,24},{20,28},{24,16},{28,20},{1,9},{5... | collective-permute-start | bytes 73736 | tf_op jit(solution)/shard_map/ppermute | solution.py:29
  65.2 9.3 %collective-permute-start.19 = (bf16[64,384]{1,0:T(8,128)(2,1)S(1)}, bf16[64,384]{1,0:T(8,128)(2,1)S(1)}, u32[]{:S(2)}, u32[]{:S(2)}) collective-permute-start(bf16[64,384]{1,0:T(8,128)(2,1)S(1)} %get-tuple-element.59), channel_id=1, source_target_pairs={{0,3},{1,2},{2,1},{3,0},{4,7},{5,6},{6,5},{7,4},{8,11},{9,10},{10,... | collective-permute-start | bytes 147464 | tf_op jit(solution)/shard_map/ppermute | solution.py:29
  67.4 7.1 %collective-permute-start.18 = (bf16[64,384]{1,0:T(8,128)(2,1)S(1)}, bf16[64,384]{1,0:T(8,128)(2,1)S(1)}, u32[]{:S(2)}, u32[]{:S(2)}) collective-permute-start(bf16[64,384]{1,0:T(8,128)(2,1)S(1)} %get-tuple-element.59), channel_id=1, source_target_pairs={{0,2},{1,3},{2,0},{3,1},{4,6},{5,7},{6,4},{7,5},{8,10},{9,11},{10,... | collective-permute-start | bytes 147464 | tf_op jit(solution)/shard_map/ppermute | solution.py:29
  68.4 4.5 %collective-permute-start.17 = (bf16[64,384]{1,0:T(8,128)(2,1)S(1)}, bf16[64,384]{1,0:T(8,128)(2,1)S(1)}, u32[]{:S(2)}, u32[]{:S(2)}) collective-permute-start(bf16[64,384]{1,0:T(8,128)(2,1)S(1)} %get-tuple-element.59), channel_id=1, source_target_pairs={{0,1},{1,0},{2,3},{3,2},{4,5},{5,4},{6,7},{7,6},{8,9},{9,8},{10,11... | collective-permute-start | bytes 147464 | tf_op jit(solution)/shard_map/ppermute | solution.py:29
  69.7 7.8 %collective-permute-start.33 = (bf16[128,384]{1,0:T(8,128)(2,1)S(1)}, bf16[128,384]{1,0:T(8,128)(2,1)S(1)}, u32[]{:S(2)}, u32[]{:S(2)}) collective-permute-start(bf16[128,384]{1,0:T(8,128)(2,1)S(1)} %constant_dynamic-update-slice_fusion.4.rest_8_), channel_id=1, source_target_pairs={{0,4},{4,0},{8,12},{12,8},{16,20},{20,16},{24,28},{28,24},{1,5},{5... | collective-permute-start | bytes 294920 | tf_op jit(solution)/shard_map/ppermute | solution.py:29
  69.8 8.3 %collective-permute-start.32 = (bf16[128,384]{1,0:T(8,128)(2,1)S(1)}, bf16[128,384]{1,0:T(8,128)(2,1)S(1)}, u32[]{:S(2)}, u32[]{:S(2)}) collective-permute-start(bf16[128,384]{1,0:T(8,128)(2,1)S(1)} %constant_dynamic-update-slice_fusion.4.rest_8_), channel_id=1, source_target_pairs={{0,3},{1,2},{2,1},{3,0},{4,7},{5,6},{6,5},{7,4},{8,11},{9,10},{10,... | collective-permute-start | bytes 294920 | tf_op jit(solution)/shard_map/ppermute | solution.py:29
  72.9 8.8 %collective-permute-start.31 = (bf16[128,384]{1,0:T(8,128)(2,1)S(1)}, bf16[128,384]{1,0:T(8,128)(2,1)S(1)}, u32[]{:S(2)}, u32[]{:S(2)}) collective-permute-start(bf16[128,384]{1,0:T(8,128)(2,1)S(1)} %constant_dynamic-update-slice_fusion.4.rest_8_), channel_id=1, source_target_pairs={{0,2},{1,3},{2,0},{3,1},{4,6},{5,7},{6,4},{7,5},{8,10},{9,11},{10,... | collective-permute-start | bytes 294920 | tf_op jit(solution)/shard_map/ppermute | solution.py:29
  74.5 9.2 %collective-permute-start.22 = (bf16[256,384]{1,0:T(8,128)(2,1)S(1)}, bf16[256,384]{1,0:T(8,128)(2,1)S(1)}, u32[]{:S(2)}, u32[]{:S(2)}) collective-permute-start(bf16[256,384]{1,0:T(8,128)(2,1)S(1)} %constant_dynamic-update-slice_fusion.rest_0_), channel_id=1, source_target_pairs={{0,24},{4,28},{8,16},{12,20},{16,8},{20,12},{24,0},{28,4},{1,25},{... | collective-permute-start | bytes 589832 | tf_op jit(solution)/shard_map/ppermute | solution.py:29
  76.3 8.0 %collective-permute-start.21 = (bf16[256,384]{1,0:T(8,128)(2,1)S(1)}, bf16[256,384]{1,0:T(8,128)(2,1)S(1)}, u32[]{:S(2)}, u32[]{:S(2)}) collective-permute-start(bf16[256,384]{1,0:T(8,128)(2,1)S(1)} %constant_dynamic-update-slice_fusion.rest_0_), channel_id=1, source_target_pairs={{0,16},{4,20},{8,24},{12,28},{16,0},{20,4},{24,8},{28,12},{1,17},{... | collective-permute-start | bytes 589832 | tf_op jit(solution)/shard_map/ppermute | solution.py:29
  77.6 6.8 %collective-permute-start.20 = (bf16[256,384]{1,0:T(8,128)(2,1)S(1)}, bf16[256,384]{1,0:T(8,128)(2,1)S(1)}, u32[]{:S(2)}, u32[]{:S(2)}) collective-permute-start(bf16[256,384]{1,0:T(8,128)(2,1)S(1)} %constant_dynamic-update-slice_fusion.rest_0_), channel_id=1, source_target_pairs={{0,8},{4,12},{8,0},{12,4},{16,24},{20,28},{24,16},{28,20},{1,9},{5... | collective-permute-start | bytes 589832 | tf_op jit(solution)/shard_map/ppermute | solution.py:29
  78.1 5.1 %collective-permute-start.30 = (bf16[128,384]{1,0:T(8,128)(2,1)S(1)}, bf16[128,384]{1,0:T(8,128)(2,1)S(1)}, u32[]{:S(2)}, u32[]{:S(2)}) collective-permute-start(bf16[128,384]{1,0:T(8,128)(2,1)S(1)} %constant_dynamic-update-slice_fusion.4.rest_8_), channel_id=1, source_target_pairs={{0,1},{1,0},{2,3},{3,2},{4,5},{5,4},{6,7},{7,6},{8,9},{9,8},{10,11... | collective-permute-start | bytes 294920 | tf_op jit(solution)/shard_map/ppermute | solution.py:29
  94.6 4.8 %collective-permute-start.37 = (bf16[304,128]{1,0:T(8,128)(2,1)S(1)}, bf16[304,128]{1,0:T(8,128)(2,1)S(1)}, u32[]{:S(2)}, u32[]{:S(2)}) collective-permute-start(bf16[304,128]{1,0:T(8,128)(2,1)S(1)} %get-tuple-element.62), channel_id=1, source_target_pairs={{0,1},{1,0},{2,3},{3,2},{4,5},{5,4},{6,7},{7,6},{8,9},{9,8},{10,11... | collective-permute-start | bytes 233480 | tf_op jit(solution)/shard_map/ppermute | solution.py:29
  96.6 9.2 %collective-permute-start.38 = (bf16[304,128]{1,0:T(8,128)(2,1)S(1)}, bf16[304,128]{1,0:T(8,128)(2,1)S(1)}, u32[]{:S(2)}, u32[]{:S(2)}) collective-permute-start(bf16[304,128]{1,0:T(8,128)(2,1)S(1)} %get-tuple-element.63), channel_id=1, source_target_pairs={{0,2},{1,3},{2,0},{3,1},{4,6},{5,7},{6,4},{7,5},{8,10},{9,11},{10,... | collective-permute-start | bytes 233480 | tf_op jit(solution)/shard_map/ppermute | solution.py:29
  98.2 7.5 %collective-permute-start.39 = (bf16[304,128]{1,0:T(8,128)(2,1)S(1)}, bf16[304,128]{1,0:T(8,128)(2,1)S(1)}, u32[]{:S(2)}, u32[]{:S(2)}) collective-permute-start(bf16[304,128]{1,0:T(8,128)(2,1)S(1)} %get-tuple-element.64), channel_id=1, source_target_pairs={{0,3},{1,2},{2,1},{3,0},{4,7},{5,6},{6,5},{7,4},{8,11},{9,10},{10,... | collective-permute-start | bytes 233480 | tf_op jit(solution)/shard_map/ppermute | solution.py:29
  108.1 4.5 %collective-permute-start.41 = (f32[8,128]{1,0:T(8,128)S(1)}, f32[8,128]{1,0:T(8,128)S(1)}, u32[]{:S(2)}, u32[]{:S(2)}) collective-permute-start(f32[8,128]{1,0:T(8,128)S(1)} %add.49), channel_id=1, source_target_pairs={{0,24},{4,28},{8,16},{12,20},{16,8},{20,12},{24,0},{28,4},{1,25},{... | collective-permute-start | bytes 12296 | tf_op jit(solution)/shard_map/ppermute | solution.py:29
  113.3 8.1 %collective-permute-start.56 = (bf16[32,384]{1,0:T(8,128)(2,1)S(1)}, bf16[32,384]{1,0:T(8,128)(2,1)S(1)}, u32[]{:S(2)}, u32[]{:S(2)}) collective-permute-start(bf16[32,384]{1,0:T(8,128)(2,1)S(1)} %get-tuple-element.73), channel_id=1, source_target_pairs={{0,24},{4,28},{8,16},{12,20},{16,8},{20,12},{24,0},{28,4},{1,25},{... | collective-permute-start | bytes 73736 | tf_op jit(solution)/shard_map/ppermute | solution.py:29
  114.8 6.5 %collective-permute-start.55 = (bf16[32,384]{1,0:T(8,128)(2,1)S(1)}, bf16[32,384]{1,0:T(8,128)(2,1)S(1)}, u32[]{:S(2)}, u32[]{:S(2)}) collective-permute-start(bf16[32,384]{1,0:T(8,128)(2,1)S(1)} %get-tuple-element.73), channel_id=1, source_target_pairs={{0,16},{4,20},{8,24},{12,28},{16,0},{20,4},{24,8},{28,12},{1,17},{... | collective-permute-start | bytes 73736 | tf_op jit(solution)/shard_map/ppermute | solution.py:29
  116.9 9.5 %collective-permute-start.46 = (bf16[64,384]{1,0:T(8,128)(2,1)S(1)}, bf16[64,384]{1,0:T(8,128)(2,1)S(1)}, u32[]{:S(2)}, u32[]{:S(2)}) collective-permute-start(bf16[64,384]{1,0:T(8,128)(2,1)S(1)} %get-tuple-element.72), channel_id=1, source_target_pairs={{0,3},{1,2},{2,1},{3,0},{4,7},{5,6},{6,5},{7,4},{8,11},{9,10},{10,... | collective-permute-start | bytes 147464 | tf_op jit(solution)/shard_map/ppermute | solution.py:29
  119.1 7.3 %collective-permute-start.45 = (bf16[64,384]{1,0:T(8,128)(2,1)S(1)}, bf16[64,384]{1,0:T(8,128)(2,1)S(1)}, u32[]{:S(2)}, u32[]{:S(2)}) collective-permute-start(bf16[64,384]{1,0:T(8,128)(2,1)S(1)} %get-tuple-element.72), channel_id=1, source_target_pairs={{0,2},{1,3},{2,0},{3,1},{4,6},{5,7},{6,4},{7,5},{8,10},{9,11},{10,... | collective-permute-start | bytes 147464 | tf_op jit(solution)/shard_map/ppermute | solution.py:29
  119.9 4.5 %collective-permute-start.44 = (bf16[64,384]{1,0:T(8,128)(2,1)S(1)}, bf16[64,384]{1,0:T(8,128)(2,1)S(1)}, u32[]{:S(2)}, u32[]{:S(2)}) collective-permute-start(bf16[64,384]{1,0:T(8,128)(2,1)S(1)} %get-tuple-element.72), channel_id=1, source_target_pairs={{0,1},{1,0},{2,3},{3,2},{4,5},{5,4},{6,7},{7,6},{8,9},{9,8},{10,11... | collective-permute-start | bytes 147464 | tf_op jit(solution)/shard_map/ppermute | solution.py:29
  121.4 7.5 %collective-permute-start.60 = (bf16[128,384]{1,0:T(8,128)(2,1)S(1)}, bf16[128,384]{1,0:T(8,128)(2,1)S(1)}, u32[]{:S(2)}, u32[]{:S(2)}) collective-permute-start(bf16[128,384]{1,0:T(8,128)(2,1)S(1)} %constant_dynamic-update-slice_fusion.12.rest_8_), channel_id=1, source_target_pairs={{0,4},{4,0},{8,12},{12,8},{16,20},{20,16},{24,28},{28,24},{1,5},{5... | collective-permute-start | bytes 294920 | tf_op jit(solution)/shard_map/ppermute | solution.py:29
  121.5 8.5 %collective-permute-start.59 = (bf16[128,384]{1,0:T(8,128)(2,1)S(1)}, bf16[128,384]{1,0:T(8,128)(2,1)S(1)}, u32[]{:S(2)}, u32[]{:S(2)}) collective-permute-start(bf16[128,384]{1,0:T(8,128)(2,1)S(1)} %constant_dynamic-update-slice_fusion.12.rest_8_), channel_id=1, source_target_pairs={{0,3},{1,2},{2,1},{3,0},{4,7},{5,6},{6,5},{7,4},{8,11},{9,10},{10,... | collective-permute-start | bytes 294920 | tf_op jit(solution)/shard_map/ppermute | solution.py:29
  124.5 8.8 %collective-permute-start.58 = (bf16[128,384]{1,0:T(8,128)(2,1)S(1)}, bf16[128,384]{1,0:T(8,128)(2,1)S(1)}, u32[]{:S(2)}, u32[]{:S(2)}) collective-permute-start(bf16[128,384]{1,0:T(8,128)(2,1)S(1)} %constant_dynamic-update-slice_fusion.12.rest_8_), channel_id=1, source_target_pairs={{0,2},{1,3},{2,0},{3,1},{4,6},{5,7},{6,4},{7,5},{8,10},{9,11},{10,... | collective-permute-start | bytes 294920 | tf_op jit(solution)/shard_map/ppermute | solution.py:29
  126.4 9.0 %collective-permute-start.49 = (bf16[256,384]{1,0:T(8,128)(2,1)S(1)}, bf16[256,384]{1,0:T(8,128)(2,1)S(1)}, u32[]{:S(2)}, u32[]{:S(2)}) collective-permute-start(bf16[256,384]{1,0:T(8,128)(2,1)S(1)} %constant_dynamic-update-slice_fusion.8.rest_0_), channel_id=1, source_target_pairs={{0,24},{4,28},{8,16},{12,20},{16,8},{20,12},{24,0},{28,4},{1,25},{... | collective-permute-start | bytes 589832 | tf_op jit(solution)/shard_map/ppermute | solution.py:29
  127.9 8.2 %collective-permute-start.48 = (bf16[256,384]{1,0:T(8,128)(2,1)S(1)}, bf16[256,384]{1,0:T(8,128)(2,1)S(1)}, u32[]{:S(2)}, u32[]{:S(2)}) collective-permute-start(bf16[256,384]{1,0:T(8,128)(2,1)S(1)} %constant_dynamic-update-slice_fusion.8.rest_0_), channel_id=1, source_target_pairs={{0,16},{4,20},{8,24},{12,28},{16,0},{20,4},{24,8},{28,12},{1,17},{... | collective-permute-start | bytes 589832 | tf_op jit(solution)/shard_map/ppermute | solution.py:29
  128.9 7.2 %collective-permute-start.47 = (bf16[256,384]{1,0:T(8,128)(2,1)S(1)}, bf16[256,384]{1,0:T(8,128)(2,1)S(1)}, u32[]{:S(2)}, u32[]{:S(2)}) collective-permute-start(bf16[256,384]{1,0:T(8,128)(2,1)S(1)} %constant_dynamic-update-slice_fusion.8.rest_0_), channel_id=1, source_target_pairs={{0,8},{4,12},{8,0},{12,4},{16,24},{20,28},{24,16},{28,20},{1,9},{5... | collective-permute-start | bytes 589832 | tf_op jit(solution)/shard_map/ppermute | solution.py:29
  129.9 5.0 %collective-permute-start.57 = (bf16[128,384]{1,0:T(8,128)(2,1)S(1)}, bf16[128,384]{1,0:T(8,128)(2,1)S(1)}, u32[]{:S(2)}, u32[]{:S(2)}) collective-permute-start(bf16[128,384]{1,0:T(8,128)(2,1)S(1)} %constant_dynamic-update-slice_fusion.12.rest_8_), channel_id=1, source_target_pairs={{0,1},{1,0},{2,3},{3,2},{4,5},{5,4},{6,7},{7,6},{8,9},{9,8},{10,11... | collective-permute-start | bytes 294920 | tf_op jit(solution)/shard_map/ppermute | solution.py:29
  146.2 4.6 %collective-permute-start.64 = (bf16[304,128]{1,0:T(8,128)(2,1)S(1)}, bf16[304,128]{1,0:T(8,128)(2,1)S(1)}, u32[]{:S(2)}, u32[]{:S(2)}) collective-permute-start(bf16[304,128]{1,0:T(8,128)(2,1)S(1)} %get-tuple-element.75), channel_id=1, source_target_pairs={{0,1},{1,0},{2,3},{3,2},{4,5},{5,4},{6,7},{7,6},{8,9},{9,8},{10,11... | collective-permute-start | bytes 233480 | tf_op jit(solution)/shard_map/ppermute | solution.py:29
  148.1 9.2 %collective-permute-start.65 = (bf16[304,128]{1,0:T(8,128)(2,1)S(1)}, bf16[304,128]{1,0:T(8,128)(2,1)S(1)}, u32[]{:S(2)}, u32[]{:S(2)}) collective-permute-start(bf16[304,128]{1,0:T(8,128)(2,1)S(1)} %get-tuple-element.76), channel_id=1, source_target_pairs={{0,2},{1,3},{2,0},{3,1},{4,6},{5,7},{6,4},{7,5},{8,10},{9,11},{10,... | collective-permute-start | bytes 233480 | tf_op jit(solution)/shard_map/ppermute | solution.py:29
  149.0 8.3 %collective-permute-start.66 = (bf16[304,128]{1,0:T(8,128)(2,1)S(1)}, bf16[304,128]{1,0:T(8,128)(2,1)S(1)}, u32[]{:S(2)}, u32[]{:S(2)}) collective-permute-start(bf16[304,128]{1,0:T(8,128)(2,1)S(1)} %get-tuple-element.77), channel_id=1, source_target_pairs={{0,3},{1,2},{2,1},{3,0},{4,7},{5,6},{6,5},{7,4},{8,11},{9,10},{10,... | collective-permute-start | bytes 233480 | tf_op jit(solution)/shard_map/ppermute | solution.py:29
  160.3 4.5 %collective-permute-start.68 = (f32[8,128]{1,0:T(8,128)S(1)}, f32[8,128]{1,0:T(8,128)S(1)}, u32[]{:S(2)}, u32[]{:S(2)}) collective-permute-start(f32[8,128]{1,0:T(8,128)S(1)} %add.53), channel_id=1, source_target_pairs={{0,24},{4,28},{8,16},{12,20},{16,8},{20,12},{24,0},{28,4},{1,25},{... | collective-permute-start | bytes 12296 | tf_op jit(solution)/shard_map/ppermute | solution.py:29
  166.3 5.4 %collective-permute-start.71 = (f32[8,128]{1,0:T(8,128)S(1)}, f32[8,128]{1,0:T(8,128)S(1)}, u32[]{:S(2)}, u32[]{:S(2)}) collective-permute-start(f32[8,128]{1,0:T(8,128)S(1)} %add_add_fusion.1), channel_id=1, source_target_pairs={{0,3},{1,2},{2,1},{3,0},{4,7},{5,6},{6,5},{7,4},{8,11},{9,10},{10,... | collective-permute-start | bytes 12296 | tf_op jit(solution)/shard_map/ppermute | solution.py:29
  (36 other events, 171.3 us)

commit v2 on v1

--- a/solution.py
+++ b/solution.py
@@ -90,49 +90,43 @@
     return parts
 
 
-def gather(pieces, sectors, term_count):
-    if len(pieces) == 1:
-        groups = [over_chips(gather_ordered(pieces[0], term_count), sectors)]
+def gather(rows, sectors, term_count):
+    if rows.shape[0] % HEAD:
+        own = over_chips(gather_ordered(rows, term_count), sectors)
     else:
-        main = jnp.concatenate(over_term(pieces[0], term_count))
-        rest = jnp.concatenate(over_chips(pieces[1], sectors))
-        groups = [over_chips(main, sectors), over_term(rest, term_count)]
-    arrays = []
-    for group in groups:
-        arrays += group
-        arrays += [exchange(array, "sector", 1) for array in group]
-    return arrays
-
-
-def main_rows(share):
-    return share - share // 3 if share % (3 * HEAD) == 0 else share
+        over = over_term(rows, term_count)
+        across = over_chips(rows, sectors)[1:]
+        near = jnp.concatenate(over + across)
+        own = [near]
+        if term_count > 1:
+            own += over_chips(jnp.concatenate(over[1:]), sectors)[1:]
+    swapped = []
+    for array in own:
+        swapped.append(exchange(array, "sector", 1))
+    return own + swapped
 
 
 def place_waves(wave, arrays, place, sectors, term_count):
-    size = wave.shape[1]
-    share = size // term_count
-    cut = main_rows(share)
+    share = wave.shape[1] // term_count
     chips = sectors // 2
-    mains = arrays[:sectors]
-    if len(arrays) == sectors:
-        cut = share
+    count = len(arrays) // 2
+
+    def put(slot, flip, source, entry):
+        start = pl.multiple_of((place[1] ^ flip) * share, HEAD)
+        wave[slot, pl.ds(start, share), :] = source[entry * share : (entry + 1) * share, :]
+
     for core in range(2):
-        for chip in range(chips):
-            source = mains[core * chips + chip]
-            slot = 2 * chip + core
-            if cut == share:
-                wave[slot] = source[...]
-                continue
-            for flip in range(term_count):
-                start = pl.multiple_of((place[1] ^ flip) * share, HEAD)
-                wave[slot, pl.ds(start, cut), :] = source[flip * cut : (flip + 1) * cut, :]
-    left_over = share - cut
-    for i, source in enumerate(arrays[sectors:]):
-        core, flip = divmod(i, term_count)
-        start = pl.multiple_of((place[1] ^ flip) * share + cut, HEAD)
-        for chip in range(chips):
-            rows = source[chip * left_over : (chip + 1) * left_over, :]
-            wave[2 * chip + core, pl.ds(start, left_over), :] = rows
+        held = arrays[core * count : (core + 1) * count]
+        if share % HEAD:
+            for chip in range(chips):
+                wave[2 * chip + core] = held[chip][...]
+            continue
+        for flip in range(term_count):
+            put(core, flip, held[0], flip)
+        for chip in range(1, chips):
+            put(2 * chip + core, 0, held[0], term_count + chip - 1)
+            for flip in range(1, term_count):
+                put(2 * chip + core, flip, held[chip], flip - 1)
 
 
 def fold(values):
@@ -287,7 +281,7 @@
     slots = weights.shape[0]
     envs, size, _ = left.shape
     share = size // term_count
-    unroll = next(u for u in (5, 4, 2, 1) if slots % u == 0)
+    unroll = next(u for u in (10, 8, 5, 4, 2, 1) if slots % u == 0)
     kinds = [F32] + [BF16] * (term_count - 1)
     return pl.pallas_call(
         functools.partial(apply_kernel, sectors, term_count, len(arrays), unroll),
@@ -343,41 +337,24 @@
     )(*chunks)
 
 
-def first_kernel(rows, *out):
-    *pieces, overlap, square = out
+def first_kernel(rows, wave, overlap, square):
     held = rows[...]
     rounded = held.astype(BF16)
-    store_pieces(pieces, rounded)
+    wave[...] = rounded
     overlap[...] = fold(held * rounded.astype(F32))
     square[...] = fold(held * held)
 
 
-def store_pieces(pieces, rows):
-    start = 0
-    for piece in pieces:
-        stop = start + piece.shape[0]
-        piece[...] = rows[start:stop]
-        start = stop
-
-
-def piece_shapes(share, size):
-    cut = main_rows(share)
-    counts = (cut, share - cut) if cut < share else (share,)
-    return [jax.ShapeDtypeStruct((count, size), BF16) for count in counts]
-
-
 def first(rows):
-    pieces = [jax.ShapeDtypeStruct(rows.shape, BF16)]
     tile = jax.ShapeDtypeStruct((SUBLANES, LANES), F32)
-    *pieces, overlap, square = pl.pallas_call(
+    return pl.pallas_call(
         first_kernel,
-        out_shape=pieces + [tile, tile],
+        out_shape=[jax.ShapeDtypeStruct(rows.shape, BF16), tile, tile],
         in_specs=[NEAR],
-        out_specs=[NEAR] * (len(pieces) + 2),
+        out_specs=[NEAR] * 3,
         name="first_wave",
         compiler_params=SMALL_CALL,
     )(rows)
-    return pieces, overlap, square
 
 
 def advance_kernel(
@@ -391,9 +368,12 @@
     previous,
     diagonal,
     following,
-    *rest,
+    wave,
+    overlap,
+    square,
+    quotient,
+    scale_out,
 ):
-    *pieces, overlap, square, quotient, scale_out = rest
     stats = sums[...]
     ratio = stats[:1, :1] / stats[1:2, :1]
     if position > 0:
@@ -406,7 +386,7 @@
     scaled = diagonal[...] * residual
     rounded = scaled.astype(BF16)
     following[...] = scaled
-    store_pieces(pieces, rounded)
+    wave[...] = rounded
     overlap[...] = fold(scaled * rounded.astype(F32))
     square[...] = fold(scaled * scaled)
     quotient[...] = jnp.broadcast_to(ratio, quotient.shape)
@@ -415,16 +395,16 @@
 
 def advance(cell_count, position, beta, scale, sums, applied, current, previous, diagonal):
     tile = jax.ShapeDtypeStruct((SUBLANES, LANES), F32)
-    pieces = piece_shapes(*current.shape)
-    following, *pieces, overlap, square, quotient, scale = pl.pallas_call(
+    rows = jax.ShapeDtypeStruct(current.shape, F32)
+    wave = jax.ShapeDtypeStruct(current.shape, BF16)
+    return pl.pallas_call(
         functools.partial(advance_kernel, cell_count, position),
-        out_shape=[jax.ShapeDtypeStruct(current.shape, F32)] + pieces + [tile] * 4,
+        out_shape=[rows, wave] + [tile] * 4,
         in_specs=[SCALARS] + [NEAR] * 6,
-        out_specs=[NEAR] * (5 + len(pieces)),
+        out_specs=[NEAR] * 6,
         name="advance",
         compiler_params=SMALL_CALL,
     )(beta, scale, sums, applied, current, previous, diagonal)
-    return following, pieces, overlap, square, quotient, scale
 
 
 def closing_kernel(
@@ -537,7 +517,7 @@
 
     normaliser = 1.0 / math.sqrt(term_count * triples.shape[0])
     current, previous, diagonal = x_start[0], x_prev[0], precond[0]
-    pieces, overlap, square = first(current)
+    rows, overlap, square = first(current)
     table, weights = plan(
         normaliser, triples.T, block_owner, trip_count, term_coef, place
     )
@@ -545,7 +525,7 @@
     scale = jnp.ones((SUBLANES, LANES), F32)
     quotients = []
     for position in range(APPS):
-        arrays = gather(pieces, sectors, term_count)
+        arrays = gather(rows, sectors, term_count)
         chunks = apply_local(
             table,
             weights,
@@ -564,7 +544,7 @@
         if position < APPS - 1:
             applied, stats = collect(arrived, current.shape)
             sums = sum_sector(stats, sectors)
-            following, pieces, overlap, square, quotient, scale_new = advance(
+            following, rows, overlap, square, quotient, scale_new = advance(
                 cell_count,
                 position,
                 lanczos_beta,

time: 174 us -> 189 us (1.086)
  waiting for transfers between devices: 62.5 us -> 93.7 us
  starting transfers between devices: 73.4 us -> 58.7 us
    ppermute x70 -> x59, waiting for transfers between devices: 59.7 us -> 90.1 us  [exchange(): return lax.ppermute(array, axis, [(i, i ^ flip) for i in range(count)])]
    ppermute x70 -> x59, starting transfers between devices: 68.3 us -> 53.7 us  [exchange(): return lax.ppermute(array, axis, [(i, i ^ flip) for i in range(count)])]
    unnamed x32 -> x35, local copies, waits for them, and re-layouts: 4.37 us -> 4.53 us
  transfers between devices with their start and end apart: 74 -> 63, of which waited for: 30 -> 36; matrix products, arithmetic and copies ran while one was open for 0% -> 0% of each run, Pallas kernels for 1% -> 1%
where the time goes in v2:
time: 189 us
  waiting for transfers between devices  93.7 us (50%)
  starting transfers between devices  58.7 us (31%)
  Pallas kernels  30.2 us (16%)
  local copies, waits for them, and re-layouts  4.67 us (2%)
  between operations  1.93 us (1%)
    ppermute x59, waiting for transfers between devices, exchange(): return lax.ppermute(array, axis, [(i, i ^ flip) for i in range(count)])  90.1 us
    ppermute x59, starting transfers between devices, exchange(): return lax.ppermute(array, axis, [(i, i ^ flip) for i in range(count)])  53.7 us
    pallas_call x3, Pallas kernels, apply_local(): pl.pallas_call(functools.partial(apply_kernel, sectors, term_count, len(a...  24.1 us
    ppermute x4, starting transfers between devices, exchange_by_core(): return lax.ppermute(array, ('sector', 'term'), pairs)  4.97 us
    unnamed x35, local copies, waits for them, and re-layouts  4.53 us
  transfers between devices with their start and end apart: 63, of which 36 were waited for; matrix products, arithmetic and copies ran while one was open for 0% of the time, Pallas kernels for 1%

profile of v2, /device:TPU:0, one launch (start us, length us, event | category | flops | bytes accessed | tf_op | source)
XLA Modules:
  0.0 189.2 jit_solution(4019120312833600832)
XLA Ops:
  1.6 4.0 %collective-permute-start.5 = (bf16[96,384]{1,0:T(8,128)(2,1)S(1)}, bf16[96,384]{1,0:T(8,128)(2,1)S(1)}, u32[]{:S(2)}, u32[]{:S(2)}) collective-permute-start(bf16[96,384]{1,0:T(8,128)(2,1)S(1)} %get-tuple-element.47), channel_id=1, source_target_pairs={{0,24},{4,28},{8,16},{12,20},{16,8},{20,12},{24,0},{28,4},{1,25},{... | collective-permute-start | bytes 221192 | tf_op jit(solution)/shard_map/ppermute | solution.py:29
  6.2 4.0 %collective-permute-start.2 = (bf16[96,384]{1,0:T(8,128)(2,1)S(1)}, bf16[96,384]{1,0:T(8,128)(2,1)S(1)}, u32[]{:S(2)}, u32[]{:S(2)}) collective-permute-start(bf16[96,384]{1,0:T(8,128)(2,1)S(1)} %get-tuple-element.47), channel_id=1, source_target_pairs={{0,3},{1,2},{2,1},{3,0},{4,7},{5,6},{6,5},{7,4},{8,11},{9,10},{10,... | collective-permute-start | bytes 221192 | tf_op jit(solution)/shard_map/ppermute | solution.py:29
  10.2 4.3 %collective-permute-done = bf16[96,384]{1,0:T(8,128)(2,1)S(1)} collective-permute-done((bf16[96,384]{1,0:T(8,128)(2,1)S(1)}, bf16[96,384]{1,0:T(8,128)(2,1)S(1)}, u32[]{:S(2)}, u32[]{:S(2)}) %collective-permute-start) | collective-permute-done | bytes 73760 | tf_op jit(solution)/shard_map/ppermute | solution.py:29
  14.6 6.0 %collective-permute-done.1 = bf16[96,384]{1,0:T(8,128)(2,1)S(1)} collective-permute-done((bf16[96,384]{1,0:T(8,128)(2,1)S(1)}, bf16[96,384]{1,0:T(8,128)(2,1)S(1)}, u32[]{:S(2)}, u32[]{:S(2)}) %collective-permute-start.1) | collective-permute-done | bytes 73760 | tf_op jit(solution)/shard_map/ppermute | solution.py:29
  20.9 2.5 %collective-permute-start.8 = (bf16[288,384]{1,0:T(8,128)(2,1)S(1)}, bf16[288,384]{1,0:T(8,128)(2,1)S(1)}, u32[]{:S(2)}, u32[]{:S(2)}) collective-permute-start(bf16[288,384]{1,0:T(8,128)(2,1)S(1)} %get-tuple-element.92), channel_id=1, source_target_pairs={{0,24},{4,28},{8,16},{12,20},{16,8},{20,12},{24,0},{28,4},{1,25},{... | collective-permute-start | bytes 663560 | tf_op jit(solution)/shard_map/ppermute | solution.py:29
  24.4 5.8 %collective-permute-done.8.rest_3_ = bf16[288,384]{1,0:T(8,128)(2,1)S(1)} collective-permute-done((bf16[288,384]{1,0:T(8,128)(2,1)S(1)}, bf16[288,384]{1,0:T(8,128)(2,1)S(1)}, u32[]{:S(2)}, u32[]{:S(2)}) %collective-permute-start.8) | collective-permute-done | bytes 221216 | tf_op jit(solution)/shard_map/ppermute | solution.py:29
  30.2 4.2 %collective-permute-done.7.rest_2_ = bf16[288,384]{1,0:T(8,128)(2,1)S(1)} collective-permute-done((bf16[288,384]{1,0:T(8,128)(2,1)S(1)}, bf16[288,384]{1,0:T(8,128)(2,1)S(1)}, u32[]{:S(2)}, u32[]{:S(2)}) %collective-permute-start.7) | collective-permute-done | bytes 221216 | tf_op jit(solution)/shard_map/ppermute | solution.py:29
  35.5 1.7 copy-done
  37.2 1.7 copy-done.1
  41.4 8.0 %apply_triples.3 = (f32[304,128]{1,0:T(8,128)S(1)}, bf16[304,128]{1,0:T(8,128)(2,1)S(1)}, bf16[304,128]{1,0:T(8,128)(2,1)S(1)}, bf16[304,128]{1,0:T(8,128)(2,1)S(1)}) custom-call(s32[3,20]{1,0:T(4,128)S(1)} %get-tuple-element.41.table, f32[20]{0:T(128)S(1)} %get-tuple-element.42.weights, s32[2]{0:T(128)S(1)} %pad_add_fusion.place, ...), custom_call_target="tpu_custom_call" | custom-call | flops 4076863488 | bytes 7372800 | tf_op jit(solution)/shard_map/apply_triples/pallas_call | solution.py:286
  50.7 3.2 %collective-permute-start.15 = (bf16[304,128]{1,0:T(8,128)(2,1)S(1)}, bf16[304,128]{1,0:T(8,128)(2,1)S(1)}, u32[]{:S(2)}, u32[]{:S(2)}) collective-permute-start(bf16[304,128]{1,0:T(8,128)(2,1)S(1)} %get-tuple-element.51), channel_id=1, source_target_pairs={{0,3},{1,2},{2,1},{3,0},{4,7},{5,6},{6,5},{7,4},{8,11},{9,10},{10,... | collective-permute-start | bytes 233480 | tf_op jit(solution)/shard_map/ppermute | solution.py:29
  54.9 4.1 %collective-permute-done.14.rest_2_ = bf16[304,128]{1,0:T(8,128)(2,1)S(1)} collective-permute-done((bf16[304,128]{1,0:T(8,128)(2,1)S(1)}, bf16[304,128]{1,0:T(8,128)(2,1)S(1)}, u32[]{:S(2)}, u32[]{:S(2)}) %collective-permute-start.14) | collective-permute-done | bytes 77856 | tf_op jit(solution)/shard_map/ppermute | solution.py:29
  60.3 1.5 collective-permute-start.18
  61.8 1.4 collective-permute-start.17
  63.9 2.4 %collective-permute-done.17 = f32[8,128]{1,0:T(8,128)S(1)} collective-permute-done((f32[8,128]{1,0:T(8,128)S(1)}, f32[8,128]{1,0:T(8,128)S(1)}, u32[]{:S(2)}, u32[]{:S(2)}) %collective-permute-start.17) | collective-permute-done | bytes 4128 | tf_op jit(solution)/shard_map/ppermute | solution.py:29
  67.0 1.5 collective-permute-start.25
  69.1 1.5 collective-permute-start.23
  72.4 5.0 %collective-permute-done.20 = bf16[96,384]{1,0:T(8,128)(2,1)S(1)} collective-permute-done((bf16[96,384]{1,0:T(8,128)(2,1)S(1)}, bf16[96,384]{1,0:T(8,128)(2,1)S(1)}, u32[]{:S(2)}, u32[]{:S(2)}) %collective-permute-start.20) | collective-permute-done | bytes 73760 | tf_op jit(solution)/shard_map/ppermute | solution.py:29
  78.5 4.3 %collective-permute-done.21 = bf16[96,384]{1,0:T(8,128)(2,1)S(1)} collective-permute-done((bf16[96,384]{1,0:T(8,128)(2,1)S(1)}, bf16[96,384]{1,0:T(8,128)(2,1)S(1)}, u32[]{:S(2)}, u32[]{:S(2)}) %collective-permute-start.21) | collective-permute-done | bytes 73760 | tf_op jit(solution)/shard_map/ppermute | solution.py:29
  83.0 1.6 collective-permute-start.28
  84.7 1.8 collective-permute-start.26
  86.5 5.8 %collective-permute-done.28.rest_3_ = bf16[288,384]{1,0:T(8,128)(2,1)S(1)} collective-permute-done((bf16[288,384]{1,0:T(8,128)(2,1)S(1)}, bf16[288,384]{1,0:T(8,128)(2,1)S(1)}, u32[]{:S(2)}, u32[]{:S(2)}) %collective-permute-start.28) | collective-permute-done | bytes 221216 | tf_op jit(solution)/shard_map/ppermute | solution.py:29
  92.3 4.2 %collective-permute-done.27.rest_2_ = bf16[288,384]{1,0:T(8,128)(2,1)S(1)} collective-permute-done((bf16[288,384]{1,0:T(8,128)(2,1)S(1)}, bf16[288,384]{1,0:T(8,128)(2,1)S(1)}, u32[]{:S(2)}, u32[]{:S(2)}) %collective-permute-start.27) | collective-permute-done | bytes 221216 | tf_op jit(solution)/shard_map/ppermute | solution.py:29
  98.2 8.2 %apply_triples.4 = (f32[304,128]{1,0:T(8,128)S(1)}, bf16[304,128]{1,0:T(8,128)(2,1)S(1)}, bf16[304,128]{1,0:T(8,128)(2,1)S(1)}, bf16[304,128]{1,0:T(8,128)(2,1)S(1)}) custom-call(s32[3,20]{1,0:T(4,128)S(1)} %get-tuple-element.41.table, f32[20]{0:T(128)S(1)} %get-tuple-element.42.weights, s32[2]{0:T(128)S(1)} %pad_add_fusion.place, ...), custom_call_target="tpu_custom_call" | custom-call | flops 4076863488 | bytes 7372800 | tf_op jit(solution)/shard_map/apply_triples/pallas_call | solution.py:286
  106.5 2.6 %collective-permute-start.34 = (bf16[304,128]{1,0:T(8,128)(2,1)S(1)}, bf16[304,128]{1,0:T(8,128)(2,1)S(1)}, u32[]{:S(2)}, u32[]{:S(2)}) collective-permute-start(bf16[304,128]{1,0:T(8,128)(2,1)S(1)} %get-tuple-element.60), channel_id=1, source_target_pairs={{0,2},{1,3},{2,0},{3,1},{4,6},{5,7},{6,4},{7,5},{8,10},{9,11},{10,... | collective-permute-start | bytes 233480 | tf_op jit(solution)/shard_map/ppermute | solution.py:29
  109.1 1.8 collective-permute-start.35
  112.0 4.0 %collective-permute-done.34.rest_2_ = bf16[304,128]{1,0:T(8,128)(2,1)S(1)} collective-permute-done((bf16[304,128]{1,0:T(8,128)(2,1)S(1)}, bf16[304,128]{1,0:T(8,128)(2,1)S(1)}, u32[]{:S(2)}, u32[]{:S(2)}) %collective-permute-start.34) | collective-permute-done | bytes 77856 | tf_op jit(solution)/shard_map/ppermute | solution.py:29
  117.5 1.6 collective-permute-start.37
  119.1 1.8 collective-permute-done.38
  122.7 1.6 collective-permute-start.45
  124.3 1.7 collective-permute-start.44
  126.3 2.4 %collective-permute-start.42 = (bf16[96,384]{1,0:T(8,128)(2,1)S(1)}, bf16[96,384]{1,0:T(8,128)(2,1)S(1)}, u32[]{:S(2)}, u32[]{:S(2)}) collective-permute-start(bf16[96,384]{1,0:T(8,128)(2,1)S(1)} %get-tuple-element.69), channel_id=1, source_target_pairs={{0,3},{1,2},{2,1},{3,0},{4,7},{5,6},{6,5},{7,4},{8,11},{9,10},{10,... | collective-permute-start | bytes 221192 | tf_op jit(solution)/shard_map/ppermute | solution.py:29
  129.2 4.0 %collective-permute-done.40 = bf16[96,384]{1,0:T(8,128)(2,1)S(1)} collective-permute-done((bf16[96,384]{1,0:T(8,128)(2,1)S(1)}, bf16[96,384]{1,0:T(8,128)(2,1)S(1)}, u32[]{:S(2)}, u32[]{:S(2)}) %collective-permute-start.40) | collective-permute-done | bytes 73760 | tf_op jit(solution)/shard_map/ppermute | solution.py:29
  133.8 5.5 %collective-permute-done.41 = bf16[96,384]{1,0:T(8,128)(2,1)S(1)} collective-permute-done((bf16[96,384]{1,0:T(8,128)(2,1)S(1)}, bf16[96,384]{1,0:T(8,128)(2,1)S(1)}, u32[]{:S(2)}, u32[]{:S(2)}) %collective-permute-start.41) | collective-permute-done | bytes 73760 | tf_op jit(solution)/shard_map/ppermute | solution.py:29
  139.5 1.7 collective-permute-start.48
  141.2 1.6 collective-permute-start.47
  143.1 5.8 %collective-permute-done.48.rest_3_ = bf16[288,384]{1,0:T(8,128)(2,1)S(1)} collective-permute-done((bf16[288,384]{1,0:T(8,128)(2,1)S(1)}, bf16[288,384]{1,0:T(8,128)(2,1)S(1)}, u32[]{:S(2)}, u32[]{:S(2)}) %collective-permute-start.48) | collective-permute-done | bytes 221216 | tf_op jit(solution)/shard_map/ppermute | solution.py:29
  148.8 4.2 %collective-permute-done.47.rest_2_ = bf16[288,384]{1,0:T(8,128)(2,1)S(1)} collective-permute-done((bf16[288,384]{1,0:T(8,128)(2,1)S(1)}, bf16[288,384]{1,0:T(8,128)(2,1)S(1)}, u32[]{:S(2)}, u32[]{:S(2)}) %collective-permute-start.47) | collective-permute-done | bytes 221216 | tf_op jit(solution)/shard_map/ppermute | solution.py:29
  154.8 8.0 %apply_triples.5 = (f32[304,128]{1,0:T(8,128)S(1)}, bf16[304,128]{1,0:T(8,128)(2,1)S(1)}, bf16[304,128]{1,0:T(8,128)(2,1)S(1)}, bf16[304,128]{1,0:T(8,128)(2,1)S(1)}) custom-call(s32[3,20]{1,0:T(4,128)S(1)} %get-tuple-element.41.table, f32[20]{0:T(128)S(1)} %get-tuple-element.42.weights, s32[2]{0:T(128)S(1)} %pad_add_fusion.place, ...), custom_call_target="tpu_custom_call" | custom-call | flops 4076863488 | bytes 7372800 | tf_op jit(solution)/shard_map/apply_triples/pallas_call | solution.py:286
  162.8 2.6 %collective-permute-start.54 = (bf16[304,128]{1,0:T(8,128)(2,1)S(1)}, bf16[304,128]{1,0:T(8,128)(2,1)S(1)}, u32[]{:S(2)}, u32[]{:S(2)}) collective-permute-start(bf16[304,128]{1,0:T(8,128)(2,1)S(1)} %get-tuple-element.72), channel_id=1, source_target_pairs={{0,2},{1,3},{2,0},{3,1},{4,6},{5,7},{6,4},{7,5},{8,10},{9,11},{10,... | collective-permute-start | bytes 233480 | tf_op jit(solution)/shard_map/ppermute | solution.py:29
  165.5 1.8 collective-permute-start.55
  168.3 4.0 %collective-permute-done.54.rest_2_ = bf16[304,128]{1,0:T(8,128)(2,1)S(1)} collective-permute-done((bf16[304,128]{1,0:T(8,128)(2,1)S(1)}, bf16[304,128]{1,0:T(8,128)(2,1)S(1)}, u32[]{:S(2)}, u32[]{:S(2)}) %collective-permute-start.54) | collective-permute-done | bytes 77856 | tf_op jit(solution)/shard_map/ppermute | solution.py:29
  174.4 1.8 collective-permute-start.58
  178.0 2.7 %collective-permute-done.57 = f32[8,128]{1,0:T(8,128)S(1)} collective-permute-done((f32[8,128]{1,0:T(8,128)S(1)}, f32[8,128]{1,0:T(8,128)S(1)}, u32[]{:S(2)}, u32[]{:S(2)}) %collective-permute-start.57) | collective-permute-done | bytes 4128 | tf_op jit(solution)/shard_map/ppermute | solution.py:29
  180.7 1.5 collective-permute-start.61
  182.2 1.5 collective-permute-start.60
  184.4 3.3 %collective-permute-done.60 = f32[8,128]{1,0:T(8,128)S(1)} collective-permute-done((f32[8,128]{1,0:T(8,128)S(1)}, f32[8,128]{1,0:T(8,128)S(1)}, u32[]{:S(2)}, u32[]{:S(2)}) %collective-permute-start.60) | collective-permute-done | bytes 4128 | tf_op jit(solution)/shard_map/ppermute | solution.py:29
  187.7 1.4 final_vector.1
  (140 shorter events, 30.3 us)
Async XLA Ops:
  1.6 19.2 %collective-permute-start.5 = (bf16[96,384]{1,0:T(8,128)(2,1)S(1)}, bf16[96,384]{1,0:T(8,128)(2,1)S(1)}, u32[]{:S(2)}, u32[]{:S(2)}) collective-permute-start(bf16[96,384]{1,0:T(8,128)(2,1)S(1)} %get-tuple-element.47), channel_id=1, source_target_pairs={{0,24},{4,28},{8,16},{12,20},{16,8},{20,12},{24,0},{28,4},{1,25},{... | collective-permute-start | bytes 221192 | tf_op jit(solution)/shard_map/ppermute | solution.py:29
  5.6 15.1 %collective-permute-start.4 = (bf16[96,384]{1,0:T(8,128)(2,1)S(1)}, bf16[96,384]{1,0:T(8,128)(2,1)S(1)}, u32[]{:S(2)}, u32[]{:S(2)}) collective-permute-start(bf16[96,384]{1,0:T(8,128)(2,1)S(1)} %get-tuple-element.47), channel_id=1, source_target_pairs={{0,16},{4,20},{8,24},{12,28},{16,0},{20,4},{24,8},{28,12},{1,17},{... | collective-permute-start | bytes 221192 | tf_op jit(solution)/shard_map/ppermute | solution.py:29
  6.1 14.6 %collective-permute-start.3 = (bf16[96,384]{1,0:T(8,128)(2,1)S(1)}, bf16[96,384]{1,0:T(8,128)(2,1)S(1)}, u32[]{:S(2)}, u32[]{:S(2)}) collective-permute-start(bf16[96,384]{1,0:T(8,128)(2,1)S(1)} %get-tuple-element.47), channel_id=1, source_target_pairs={{0,8},{4,12},{8,0},{12,4},{16,24},{20,28},{24,16},{28,20},{1,9},{5... | collective-permute-start | bytes 221192 | tf_op jit(solution)/shard_map/ppermute | solution.py:29
  6.2 14.4 %collective-permute-start.2 = (bf16[96,384]{1,0:T(8,128)(2,1)S(1)}, bf16[96,384]{1,0:T(8,128)(2,1)S(1)}, u32[]{:S(2)}, u32[]{:S(2)}) collective-permute-start(bf16[96,384]{1,0:T(8,128)(2,1)S(1)} %get-tuple-element.47), channel_id=1, source_target_pairs={{0,3},{1,2},{2,1},{3,0},{4,7},{5,6},{6,5},{7,4},{8,11},{9,10},{10,... | collective-permute-start | bytes 221192 | tf_op jit(solution)/shard_map/ppermute | solution.py:29
  10.2 4.4 %collective-permute-start = (bf16[96,384]{1,0:T(8,128)(2,1)S(1)}, bf16[96,384]{1,0:T(8,128)(2,1)S(1)}, u32[]{:S(2)}, u32[]{:S(2)}) collective-permute-start(bf16[96,384]{1,0:T(8,128)(2,1)S(1)} %get-tuple-element.47), channel_id=1, source_target_pairs={{0,1},{1,0},{2,3},{3,2},{4,5},{5,4},{6,7},{7,6},{8,9},{9,8},{10,11... | collective-permute-start | bytes 221192 | tf_op jit(solution)/shard_map/ppermute | solution.py:29
  14.6 6.0 %collective-permute-start.1 = (bf16[96,384]{1,0:T(8,128)(2,1)S(1)}, bf16[96,384]{1,0:T(8,128)(2,1)S(1)}, u32[]{:S(2)}, u32[]{:S(2)}) collective-permute-start(bf16[96,384]{1,0:T(8,128)(2,1)S(1)} %get-tuple-element.47), channel_id=1, source_target_pairs={{0,2},{1,3},{2,0},{3,1},{4,6},{5,7},{6,4},{7,5},{8,10},{9,11},{10,... | collective-permute-start | bytes 221192 | tf_op jit(solution)/shard_map/ppermute | solution.py:29
  20.8 20.6 %collective-permute-start.9 = (bf16[672,384]{1,0:T(8,128)(2,1)S(1)}, bf16[672,384]{1,0:T(8,128)(2,1)S(1)}, u32[]{:S(2)}, u32[]{:S(2)}) collective-permute-start(bf16[672,384]{1,0:T(8,128)(2,1)S(1)} %constant_dynamic-update-slice_fusion.rest_0_), channel_id=1, source_target_pairs={{0,4},{4,0},{8,12},{12,8},{16,20},{20,16},{24,28},{28,24},{1,5},{5... | collective-permute-start | bytes 1548296 | tf_op jit(solution)/shard_map/ppermute | solution.py:29
  20.9 9.3 %collective-permute-start.8 = (bf16[288,384]{1,0:T(8,128)(2,1)S(1)}, bf16[288,384]{1,0:T(8,128)(2,1)S(1)}, u32[]{:S(2)}, u32[]{:S(2)}) collective-permute-start(bf16[288,384]{1,0:T(8,128)(2,1)S(1)} %get-tuple-element.92), channel_id=1, source_target_pairs={{0,24},{4,28},{8,16},{12,20},{16,8},{20,12},{24,0},{28,4},{1,25},{... | collective-permute-start | bytes 663560 | tf_op jit(solution)/shard_map/ppermute | solution.py:29
  23.4 11.0 %collective-permute-start.7 = (bf16[288,384]{1,0:T(8,128)(2,1)S(1)}, bf16[288,384]{1,0:T(8,128)(2,1)S(1)}, u32[]{:S(2)}, u32[]{:S(2)}) collective-permute-start(bf16[288,384]{1,0:T(8,128)(2,1)S(1)} %get-tuple-element.92), channel_id=1, source_target_pairs={{0,16},{4,20},{8,24},{12,28},{16,0},{20,4},{24,8},{28,12},{1,17},{... | collective-permute-start | bytes 663560 | tf_op jit(solution)/shard_map/ppermute | solution.py:29
  23.9 10.6 %collective-permute-start.6 = (bf16[288,384]{1,0:T(8,128)(2,1)S(1)}, bf16[288,384]{1,0:T(8,128)(2,1)S(1)}, u32[]{:S(2)}, u32[]{:S(2)}) collective-permute-start(bf16[288,384]{1,0:T(8,128)(2,1)S(1)} %get-tuple-element.92), channel_id=1, source_target_pairs={{0,8},{4,12},{8,0},{12,4},{16,24},{20,28},{24,16},{28,20},{1,9},{5... | collective-permute-start | bytes 663560 | tf_op jit(solution)/shard_map/ppermute | solution.py:29
  30.2 11.2 %collective-permute-start.12 = (bf16[288,384]{1,0:T(8,128)(2,1)S(1)}, bf16[288,384]{1,0:T(8,128)(2,1)S(1)}, u32[]{:S(2)}, u32[]{:S(2)}) collective-permute-start(bf16[288,384]{1,0:T(8,128)(2,1)S(1)} %collective-permute-done.8.rest_3_), channel_id=1, source_target_pairs={{0,4},{4,0},{8,12},{12,8},{16,20},{20,16},{24,28},{28,24},{1,5},{5... | collective-permute-start | bytes 663560 | tf_op jit(solution)/shard_map/ppermute | solution.py:29
  34.3 7.0 %collective-permute-start.11 = (bf16[288,384]{1,0:T(8,128)(2,1)S(1)}, bf16[288,384]{1,0:T(8,128)(2,1)S(1)}, u32[]{:S(2)}, u32[]{:S(2)}) collective-permute-start(bf16[288,384]{1,0:T(8,128)(2,1)S(1)} %collective-permute-done.7.rest_2_), channel_id=1, source_target_pairs={{0,4},{4,0},{8,12},{12,8},{16,20},{20,16},{24,28},{28,24},{1,5},{5... | collective-permute-start | bytes 663560 | tf_op jit(solution)/shard_map/ppermute | solution.py:29
  34.4 6.9 %collective-permute-start.10 = (bf16[288,384]{1,0:T(8,128)(2,1)S(1)}, bf16[288,384]{1,0:T(8,128)(2,1)S(1)}, u32[]{:S(2)}, u32[]{:S(2)}) collective-permute-start(bf16[288,384]{1,0:T(8,128)(2,1)S(1)} %collective-permute-done.6.rest_1_), channel_id=1, source_target_pairs={{0,4},{4,0},{8,12},{12,8},{16,20},{20,16},{24,28},{28,24},{1,5},{5... | collective-permute-start | bytes 663560 | tf_op jit(solution)/shard_map/ppermute | solution.py:29
  49.4 5.5 %collective-permute-start.13 = (bf16[304,128]{1,0:T(8,128)(2,1)S(1)}, bf16[304,128]{1,0:T(8,128)(2,1)S(1)}, u32[]{:S(2)}, u32[]{:S(2)}) collective-permute-start(bf16[304,128]{1,0:T(8,128)(2,1)S(1)} %get-tuple-element.49), channel_id=1, source_target_pairs={{0,1},{1,0},{2,3},{3,2},{4,5},{5,4},{6,7},{7,6},{8,9},{9,8},{10,11... | collective-permute-start | bytes 233480 | tf_op jit(solution)/shard_map/ppermute | solution.py:29
  49.6 9.4 %collective-permute-start.14 = (bf16[304,128]{1,0:T(8,128)(2,1)S(1)}, bf16[304,128]{1,0:T(8,128)(2,1)S(1)}, u32[]{:S(2)}, u32[]{:S(2)}) collective-permute-start(bf16[304,128]{1,0:T(8,128)(2,1)S(1)} %get-tuple-element.50), channel_id=1, source_target_pairs={{0,2},{1,3},{2,0},{3,1},{4,6},{5,7},{6,4},{7,5},{8,10},{9,11},{10,... | collective-permute-start | bytes 233480 | tf_op jit(solution)/shard_map/ppermute | solution.py:29
  50.7 8.3 %collective-permute-start.15 = (bf16[304,128]{1,0:T(8,128)(2,1)S(1)}, bf16[304,128]{1,0:T(8,128)(2,1)S(1)}, u32[]{:S(2)}, u32[]{:S(2)}) collective-permute-start(bf16[304,128]{1,0:T(8,128)(2,1)S(1)} %get-tuple-element.51), channel_id=1, source_target_pairs={{0,3},{1,2},{2,1},{3,0},{4,7},{5,6},{6,5},{7,4},{8,11},{9,10},{10,... | collective-permute-start | bytes 233480 | tf_op jit(solution)/shard_map/ppermute | solution.py:29
  61.8 4.5 %collective-permute-start.17 = (f32[8,128]{1,0:T(8,128)S(1)}, f32[8,128]{1,0:T(8,128)S(1)}, u32[]{:S(2)}, u32[]{:S(2)}) collective-permute-start(f32[8,128]{1,0:T(8,128)S(1)} %add.45), channel_id=1, source_target_pairs={{0,24},{4,28},{8,16},{12,20},{16,8},{20,12},{24,0},{28,4},{1,25},{... | collective-permute-start | bytes 12296 | tf_op jit(solution)/shard_map/ppermute | solution.py:29
  67.0 15.9 %collective-permute-start.25 = (bf16[96,384]{1,0:T(8,128)(2,1)S(1)}, bf16[96,384]{1,0:T(8,128)(2,1)S(1)}, u32[]{:S(2)}, u32[]{:S(2)}) collective-permute-start(bf16[96,384]{1,0:T(8,128)(2,1)S(1)} %get-tuple-element.57), channel_id=1, source_target_pairs={{0,24},{4,28},{8,16},{12,20},{16,8},{20,12},{24,0},{28,4},{1,25},{... | collective-permute-start | bytes 221192 | tf_op jit(solution)/shard_map/ppermute | solution.py:29
  68.5 14.3 %collective-permute-start.24 = (bf16[96,384]{1,0:T(8,128)(2,1)S(1)}, bf16[96,384]{1,0:T(8,128)(2,1)S(1)}, u32[]{:S(2)}, u32[]{:S(2)}) collective-permute-start(bf16[96,384]{1,0:T(8,128)(2,1)S(1)} %get-tuple-element.57), channel_id=1, source_target_pairs={{0,16},{4,20},{8,24},{12,28},{16,0},{20,4},{24,8},{28,12},{1,17},{... | collective-permute-start | bytes 221192 | tf_op jit(solution)/shard_map/ppermute | solution.py:29
  69.1 13.7 %collective-permute-start.23 = (bf16[96,384]{1,0:T(8,128)(2,1)S(1)}, bf16[96,384]{1,0:T(8,128)(2,1)S(1)}, u32[]{:S(2)}, u32[]{:S(2)}) collective-permute-start(bf16[96,384]{1,0:T(8,128)(2,1)S(1)} %get-tuple-element.57), channel_id=1, source_target_pairs={{0,8},{4,12},{8,0},{12,4},{16,24},{20,28},{24,16},{28,20},{1,9},{5... | collective-permute-start | bytes 221192 | tf_op jit(solution)/shard_map/ppermute | solution.py:29
  70.6 12.2 %collective-permute-start.22 = (bf16[96,384]{1,0:T(8,128)(2,1)S(1)}, bf16[96,384]{1,0:T(8,128)(2,1)S(1)}, u32[]{:S(2)}, u32[]{:S(2)}) collective-permute-start(bf16[96,384]{1,0:T(8,128)(2,1)S(1)} %get-tuple-element.57), channel_id=1, source_target_pairs={{0,3},{1,2},{2,1},{3,0},{4,7},{5,6},{6,5},{7,4},{8,11},{9,10},{10,... | collective-permute-start | bytes 221192 | tf_op jit(solution)/shard_map/ppermute | solution.py:29
  71.8 5.7 %collective-permute-start.20 = (bf16[96,384]{1,0:T(8,128)(2,1)S(1)}, bf16[96,384]{1,0:T(8,128)(2,1)S(1)}, u32[]{:S(2)}, u32[]{:S(2)}) collective-permute-start(bf16[96,384]{1,0:T(8,128)(2,1)S(1)} %get-tuple-element.57), channel_id=1, source_target_pairs={{0,1},{1,0},{2,3},{3,2},{4,5},{5,4},{6,7},{7,6},{8,9},{9,8},{10,11... | collective-permute-start | bytes 221192 | tf_op jit(solution)/shard_map/ppermute | solution.py:29
  77.5 5.3 %collective-permute-start.21 = (bf16[96,384]{1,0:T(8,128)(2,1)S(1)}, bf16[96,384]{1,0:T(8,128)(2,1)S(1)}, u32[]{:S(2)}, u32[]{:S(2)}) collective-permute-start(bf16[96,384]{1,0:T(8,128)(2,1)S(1)} %get-tuple-element.57), channel_id=1, source_target_pairs={{0,2},{1,3},{2,0},{3,1},{4,6},{5,7},{6,4},{7,5},{8,10},{9,11},{10,... | collective-permute-start | bytes 221192 | tf_op jit(solution)/shard_map/ppermute | solution.py:29
  82.9 15.3 %collective-permute-start.29 = (bf16[672,384]{1,0:T(8,128)(2,1)S(1)}, bf16[672,384]{1,0:T(8,128)(2,1)S(1)}, u32[]{:S(2)}, u32[]{:S(2)}) collective-permute-start(bf16[672,384]{1,0:T(8,128)(2,1)S(1)} %constant_dynamic-update-slice_fusion.10.rest_0_), channel_id=1, source_target_pairs={{0,4},{4,0},{8,12},{12,8},{16,20},{20,16},{24,28},{28,24},{1,5},{5... | collective-permute-start | bytes 1548296 | tf_op jit(solution)/shard_map/ppermute | solution.py:29
  83.0 9.3 %collective-permute-start.28 = (bf16[288,384]{1,0:T(8,128)(2,1)S(1)}, bf16[288,384]{1,0:T(8,128)(2,1)S(1)}, u32[]{:S(2)}, u32[]{:S(2)}) collective-permute-start(bf16[288,384]{1,0:T(8,128)(2,1)S(1)} %get-tuple-element.86), channel_id=1, source_target_pairs={{0,24},{4,28},{8,16},{12,20},{16,8},{20,12},{24,0},{28,4},{1,25},{... | collective-permute-start | bytes 663560 | tf_op jit(solution)/shard_map/ppermute | solution.py:29
  84.6 11.9 %collective-permute-start.27 = (bf16[288,384]{1,0:T(8,128)(2,1)S(1)}, bf16[288,384]{1,0:T(8,128)(2,1)S(1)}, u32[]{:S(2)}, u32[]{:S(2)}) collective-permute-start(bf16[288,384]{1,0:T(8,128)(2,1)S(1)} %get-tuple-element.86), channel_id=1, source_target_pairs={{0,16},{4,20},{8,24},{12,28},{16,0},{20,4},{24,8},{28,12},{1,17},{... | collective-permute-start | bytes 663560 | tf_op jit(solution)/shard_map/ppermute | solution.py:29
  84.7 11.8 %collective-permute-start.26 = (bf16[288,384]{1,0:T(8,128)(2,1)S(1)}, bf16[288,384]{1,0:T(8,128)(2,1)S(1)}, u32[]{:S(2)}, u32[]{:S(2)}) collective-permute-start(bf16[288,384]{1,0:T(8,128)(2,1)S(1)} %get-tuple-element.86), channel_id=1, source_target_pairs={{0,8},{4,12},{8,0},{12,4},{16,24},{20,28},{24,16},{28,20},{1,9},{5... | collective-permute-start | bytes 663560 | tf_op jit(solution)/shard_map/ppermute | solution.py:29
  92.3 4.7 %collective-permute-start.32 = (bf16[288,384]{1,0:T(8,128)(2,1)S(1)}, bf16[288,384]{1,0:T(8,128)(2,1)S(1)}, u32[]{:S(2)}, u32[]{:S(2)}) collective-permute-start(bf16[288,384]{1,0:T(8,128)(2,1)S(1)} %collective-permute-done.28.rest_3_), channel_id=1, source_target_pairs={{0,4},{4,0},{8,12},{12,8},{16,20},{20,16},{24,28},{28,24},{1,5},{5... | collective-permute-start | bytes 663560 | tf_op jit(solution)/shard_map/ppermute | solution.py:29
  106.4 5.6 %collective-permute-start.33 = (bf16[304,128]{1,0:T(8,128)(2,1)S(1)}, bf16[304,128]{1,0:T(8,128)(2,1)S(1)}, u32[]{:S(2)}, u32[]{:S(2)}) collective-permute-start(bf16[304,128]{1,0:T(8,128)(2,1)S(1)} %get-tuple-element.59), channel_id=1, source_target_pairs={{0,1},{1,0},{2,3},{3,2},{4,5},{5,4},{6,7},{7,6},{8,9},{9,8},{10,11... | collective-permute-start | bytes 233480 | tf_op jit(solution)/shard_map/ppermute | solution.py:29
  106.5 9.5 %collective-permute-start.34 = (bf16[304,128]{1,0:T(8,128)(2,1)S(1)}, bf16[304,128]{1,0:T(8,128)(2,1)S(1)}, u32[]{:S(2)}, u32[]{:S(2)}) collective-permute-start(bf16[304,128]{1,0:T(8,128)(2,1)S(1)} %get-tuple-element.60), channel_id=1, source_target_pairs={{0,2},{1,3},{2,0},{3,1},{4,6},{5,7},{6,4},{7,5},{8,10},{9,11},{10,... | collective-permute-start | bytes 233480 | tf_op jit(solution)/shard_map/ppermute | solution.py:29
  109.1 6.9 %collective-permute-start.35 = (bf16[304,128]{1,0:T(8,128)(2,1)S(1)}, bf16[304,128]{1,0:T(8,128)(2,1)S(1)}, u32[]{:S(2)}, u32[]{:S(2)}) collective-permute-start(bf16[304,128]{1,0:T(8,128)(2,1)S(1)} %get-tuple-element.61), channel_id=1, source_target_pairs={{0,3},{1,2},{2,1},{3,0},{4,7},{5,6},{6,5},{7,4},{8,11},{9,10},{10,... | collective-permute-start | bytes 233480 | tf_op jit(solution)/shard_map/ppermute | solution.py:29
  117.5 4.5 %collective-permute-start.37 = (f32[8,128]{1,0:T(8,128)S(1)}, f32[8,128]{1,0:T(8,128)S(1)}, u32[]{:S(2)}, u32[]{:S(2)}) collective-permute-start(f32[8,128]{1,0:T(8,128)S(1)} %add.49), channel_id=1, source_target_pairs={{0,24},{4,28},{8,16},{12,20},{16,8},{20,12},{24,0},{28,4},{1,25},{... | collective-permute-start | bytes 12296 | tf_op jit(solution)/shard_map/ppermute | solution.py:29
  122.7 16.7 %collective-permute-start.45 = (bf16[96,384]{1,0:T(8,128)(2,1)S(1)}, bf16[96,384]{1,0:T(8,128)(2,1)S(1)}, u32[]{:S(2)}, u32[]{:S(2)}) collective-permute-start(bf16[96,384]{1,0:T(8,128)(2,1)S(1)} %get-tuple-element.69), channel_id=1, source_target_pairs={{0,24},{4,28},{8,16},{12,20},{16,8},{20,12},{24,0},{28,4},{1,25},{... | collective-permute-start | bytes 221192 | tf_op jit(solution)/shard_map/ppermute | solution.py:29
  124.3 15.0 %collective-permute-start.44 = (bf16[96,384]{1,0:T(8,128)(2,1)S(1)}, bf16[96,384]{1,0:T(8,128)(2,1)S(1)}, u32[]{:S(2)}, u32[]{:S(2)}) collective-permute-start(bf16[96,384]{1,0:T(8,128)(2,1)S(1)} %get-tuple-element.69), channel_id=1, source_target_pairs={{0,16},{4,20},{8,24},{12,28},{16,0},{20,4},{24,8},{28,12},{1,17},{... | collective-permute-start | bytes 221192 | tf_op jit(solution)/shard_map/ppermute | solution.py:29
  126.0 13.3 %collective-permute-start.43 = (bf16[96,384]{1,0:T(8,128)(2,1)S(1)}, bf16[96,384]{1,0:T(8,128)(2,1)S(1)}, u32[]{:S(2)}, u32[]{:S(2)}) collective-permute-start(bf16[96,384]{1,0:T(8,128)(2,1)S(1)} %get-tuple-element.69), channel_id=1, source_target_pairs={{0,8},{4,12},{8,0},{12,4},{16,24},{20,28},{24,16},{28,20},{1,9},{5... | collective-permute-start | bytes 221192 | tf_op jit(solution)/shard_map/ppermute | solution.py:29
  126.3 13.0 %collective-permute-start.42 = (bf16[96,384]{1,0:T(8,128)(2,1)S(1)}, bf16[96,384]{1,0:T(8,128)(2,1)S(1)}, u32[]{:S(2)}, u32[]{:S(2)}) collective-permute-start(bf16[96,384]{1,0:T(8,128)(2,1)S(1)} %get-tuple-element.69), channel_id=1, source_target_pairs={{0,3},{1,2},{2,1},{3,0},{4,7},{5,6},{6,5},{7,4},{8,11},{9,10},{10,... | collective-permute-start | bytes 221192 | tf_op jit(solution)/shard_map/ppermute | solution.py:29
  128.7 4.6 %collective-permute-start.40 = (bf16[96,384]{1,0:T(8,128)(2,1)S(1)}, bf16[96,384]{1,0:T(8,128)(2,1)S(1)}, u32[]{:S(2)}, u32[]{:S(2)}) collective-permute-start(bf16[96,384]{1,0:T(8,128)(2,1)S(1)} %get-tuple-element.69), channel_id=1, source_target_pairs={{0,1},{1,0},{2,3},{3,2},{4,5},{5,4},{6,7},{7,6},{8,9},{9,8},{10,11... | collective-permute-start | bytes 221192 | tf_op jit(solution)/shard_map/ppermute | solution.py:29
  133.2 6.0 %collective-permute-start.41 = (bf16[96,384]{1,0:T(8,128)(2,1)S(1)}, bf16[96,384]{1,0:T(8,128)(2,1)S(1)}, u32[]{:S(2)}, u32[]{:S(2)}) collective-permute-start(bf16[96,384]{1,0:T(8,128)(2,1)S(1)} %get-tuple-element.69), channel_id=1, source_target_pairs={{0,2},{1,3},{2,0},{3,1},{4,6},{5,7},{6,4},{7,5},{8,10},{9,11},{10,... | collective-permute-start | bytes 221192 | tf_op jit(solution)/shard_map/ppermute | solution.py:29
  139.4 15.3 %collective-permute-start.49 = (bf16[672,384]{1,0:T(8,128)(2,1)S(1)}, bf16[672,384]{1,0:T(8,128)(2,1)S(1)}, u32[]{:S(2)}, u32[]{:S(2)}) collective-permute-start(bf16[672,384]{1,0:T(8,128)(2,1)S(1)} %constant_dynamic-update-slice_fusion.20.rest_0_), channel_id=1, source_target_pairs={{0,4},{4,0},{8,12},{12,8},{16,20},{20,16},{24,28},{28,24},{1,5},{5... | collective-permute-start | bytes 1548296 | tf_op jit(solution)/shard_map/ppermute | solution.py:29
  139.5 9.3 %collective-permute-start.48 = (bf16[288,384]{1,0:T(8,128)(2,1)S(1)}, bf16[288,384]{1,0:T(8,128)(2,1)S(1)}, u32[]{:S(2)}, u32[]{:S(2)}) collective-permute-start(bf16[288,384]{1,0:T(8,128)(2,1)S(1)} %get-tuple-element.80), channel_id=1, source_target_pairs={{0,24},{4,28},{8,16},{12,20},{16,8},{20,12},{24,0},{28,4},{1,25},{... | collective-permute-start | bytes 663560 | tf_op jit(solution)/shard_map/ppermute | solution.py:29
  141.2 11.8 %collective-permute-start.47 = (bf16[288,384]{1,0:T(8,128)(2,1)S(1)}, bf16[288,384]{1,0:T(8,128)(2,1)S(1)}, u32[]{:S(2)}, u32[]{:S(2)}) collective-permute-start(bf16[288,384]{1,0:T(8,128)(2,1)S(1)} %get-tuple-element.80), channel_id=1, source_target_pairs={{0,16},{4,20},{8,24},{12,28},{16,0},{20,4},{24,8},{28,12},{1,17},{... | collective-permute-start | bytes 663560 | tf_op jit(solution)/shard_map/ppermute | solution.py:29
  142.8 10.4 %collective-permute-start.46 = (bf16[288,384]{1,0:T(8,128)(2,1)S(1)}, bf16[288,384]{1,0:T(8,128)(2,1)S(1)}, u32[]{:S(2)}, u32[]{:S(2)}) collective-permute-start(bf16[288,384]{1,0:T(8,128)(2,1)S(1)} %get-tuple-element.80), channel_id=1, source_target_pairs={{0,8},{4,12},{8,0},{12,4},{16,24},{20,28},{24,16},{28,20},{1,9},{5... | collective-permute-start | bytes 663560 | tf_op jit(solution)/shard_map/ppermute | solution.py:29
  148.8 4.7 %collective-permute-start.52 = (bf16[288,384]{1,0:T(8,128)(2,1)S(1)}, bf16[288,384]{1,0:T(8,128)(2,1)S(1)}, u32[]{:S(2)}, u32[]{:S(2)}) collective-permute-start(bf16[288,384]{1,0:T(8,128)(2,1)S(1)} %collective-permute-done.48.rest_3_), channel_id=1, source_target_pairs={{0,4},{4,0},{8,12},{12,8},{16,20},{20,16},{24,28},{28,24},{1,5},{5... | collective-permute-start | bytes 663560 | tf_op jit(solution)/shard_map/ppermute | solution.py:29
  162.8 5.6 %collective-permute-start.53 = (bf16[304,128]{1,0:T(8,128)(2,1)S(1)}, bf16[304,128]{1,0:T(8,128)(2,1)S(1)}, u32[]{:S(2)}, u32[]{:S(2)}) collective-permute-start(bf16[304,128]{1,0:T(8,128)(2,1)S(1)} %get-tuple-element.71), channel_id=1, source_target_pairs={{0,1},{1,0},{2,3},{3,2},{4,5},{5,4},{6,7},{7,6},{8,9},{9,8},{10,11... | collective-permute-start | bytes 233480 | tf_op jit(solution)/shard_map/ppermute | solution.py:29
  162.8 9.5 %collective-permute-start.54 = (bf16[304,128]{1,0:T(8,128)(2,1)S(1)}, bf16[304,128]{1,0:T(8,128)(2,1)S(1)}, u32[]{:S(2)}, u32[]{:S(2)}) collective-permute-start(bf16[304,128]{1,0:T(8,128)(2,1)S(1)} %get-tuple-element.72), channel_id=1, source_target_pairs={{0,2},{1,3},{2,0},{3,1},{4,6},{5,7},{6,4},{7,5},{8,10},{9,11},{10,... | collective-permute-start | bytes 233480 | tf_op jit(solution)/shard_map/ppermute | solution.py:29
  165.5 6.9 %collective-permute-start.55 = (bf16[304,128]{1,0:T(8,128)(2,1)S(1)}, bf16[304,128]{1,0:T(8,128)(2,1)S(1)}, u32[]{:S(2)}, u32[]{:S(2)}) collective-permute-start(bf16[304,128]{1,0:T(8,128)(2,1)S(1)} %get-tuple-element.73), channel_id=1, source_target_pairs={{0,3},{1,2},{2,1},{3,0},{4,7},{5,6},{6,5},{7,4},{8,11},{9,10},{10,... | collective-permute-start | bytes 233480 | tf_op jit(solution)/shard_map/ppermute | solution.py:29
  176.2 4.5 %collective-permute-start.57 = (f32[8,128]{1,0:T(8,128)S(1)}, f32[8,128]{1,0:T(8,128)S(1)}, u32[]{:S(2)}, u32[]{:S(2)}) collective-permute-start(f32[8,128]{1,0:T(8,128)S(1)} %add.53), channel_id=1, source_target_pairs={{0,24},{4,28},{8,16},{12,20},{16,8},{20,12},{24,0},{28,4},{1,25},{... | collective-permute-start | bytes 12296 | tf_op jit(solution)/shard_map/ppermute | solution.py:29
  182.2 5.4 %collective-permute-start.60 = (f32[8,128]{1,0:T(8,128)S(1)}, f32[8,128]{1,0:T(8,128)S(1)}, u32[]{:S(2)}, u32[]{:S(2)}) collective-permute-start(f32[8,128]{1,0:T(8,128)S(1)} %add_add_fusion.1), channel_id=1, source_target_pairs={{0,3},{1,2},{2,1},{3,0},{4,7},{5,6},{6,5},{7,4},{8,11},{9,10},{10,... | collective-permute-start | bytes 12296 | tf_op jit(solution)/shard_map/ppermute | solution.py:29
  (25 other events, 141.6 us)

commit v3 on v2

--- a/solution.py
+++ b/solution.py
@@ -90,16 +90,20 @@
     return parts
 
 
-def gather(rows, sectors, term_count):
+def gather(rows, sectors, term_count, split):
     if rows.shape[0] % HEAD:
         own = over_chips(gather_ordered(rows, term_count), sectors)
     else:
         over = over_term(rows, term_count)
         across = over_chips(rows, sectors)[1:]
-        near = jnp.concatenate(over + across)
-        own = [near]
-        if term_count > 1:
-            own += over_chips(jnp.concatenate(over[1:]), sectors)[1:]
+        own = [jnp.concatenate(over + across)]
+        if over[1:] and across:
+            cut = rows.shape[0] - HEAD * split
+            main = jnp.concatenate([array[:cut] for array in over[1:]])
+            own += over_chips(main, sectors)[1:]
+            if split:
+                tail = jnp.concatenate([array[cut:] for array in across])
+                own += over_term(tail, term_count)[1:]
     swapped = []
     for array in own:
         swapped.append(exchange(array, "sector", 1))
@@ -111,9 +115,13 @@
     chips = sectors // 2
     count = len(arrays) // 2
 
-    def put(slot, flip, source, entry):
-        start = pl.multiple_of((place[1] ^ flip) * share, HEAD)
-        wave[slot, pl.ds(start, share), :] = source[entry * share : (entry + 1) * share, :]
+    split = count > chips
+    cut = share - HEAD * split
+
+    def put(slot, flip, source, entry, height, first=0):
+        start = pl.multiple_of((place[1] ^ flip) * share + first, HEAD)
+        rows = source[entry * height : (entry + 1) * height, :]
+        wave[slot, pl.ds(start, height), :] = rows
 
     for core in range(2):
         held = arrays[core * count : (core + 1) * count]
@@ -122,11 +130,14 @@
                 wave[2 * chip + core] = held[chip][...]
             continue
         for flip in range(term_count):
-            put(core, flip, held[0], flip)
+            put(core, flip, held[0], flip, share)
         for chip in range(1, chips):
-            put(2 * chip + core, 0, held[0], term_count + chip - 1)
+            slot = 2 * chip + core
+            put(slot, 0, held[0], term_count + chip - 1, share)
             for flip in range(1, term_count):
-                put(2 * chip + core, flip, held[chip], flip - 1)
+                put(slot, flip, held[chip], flip - 1, cut)
+                if split:
+                    put(slot, flip, held[chips - 1 + flip], chip - 1, HEAD, cut)
 
 
 def fold(values):
@@ -142,24 +153,29 @@
     return total
 
 
-def plan_kernel(normaliser, triples, owner, live, coef, place, table, weights):
+def plan_kernel(normaliser, triples, owner, live, coef, place, table, weights, used):
+    for env in range(used.shape[0]):
+        used[env] = 0
     for k in range(triples.shape[1]):
+        table[3, k] = used[triples[2, k]]
+        used[triples[2, k]] = 1
         table[0, k] = triples[0, k]
         table[1, k] = owner[triples[1, k]] ^ place[0]
         table[2, k] = triples[2, k]
         weights[k] = jnp.where(k < live[0, 0], coef[triples[3, k]], 0.0) * normaliser
 
 
-def plan(normaliser, triples, owner, live, coef, place):
+def plan(normaliser, envs, triples, owner, live, coef, place):
     slots = triples.shape[1]
     return pl.pallas_call(
         functools.partial(plan_kernel, normaliser),
         out_shape=[
-            jax.ShapeDtypeStruct((3, slots), jnp.int32),
+            jax.ShapeDtypeStruct((4, slots), jnp.int32),
             jax.ShapeDtypeStruct((slots,), F32),
+            jax.ShapeDtypeStruct((envs,), jnp.int32),
         ],
         in_specs=[SCALARS] * 5,
-        out_specs=[SCALARS] * 2,
+        out_specs=[SCALARS] * 3,
         name="plan",
         compiler_params=SMALL_CALL,
     )(triples, owner, live, coef, place)
@@ -219,6 +235,7 @@
     unroll,
     table,
     weights,
+    used,
     place,
     left,
     right,
@@ -234,14 +251,18 @@
     envs = right.shape[0]
     share = size // term_count
     for env in range(envs):
-        total[env] = jnp.zeros((size, size), F32)
+
+        @pl.when(used[env] == 0)
+        def _():
+            total[env] = jnp.zeros((size, size), F32)
+
     place_waves(wave, arrays, place, sectors, term_count)
 
     def one(k):
         slot = table[2, k]
-        total[slot] += weights[k] * jnp.dot(
-            left[table[0, k]], wave[table[1, k]], preferred_element_type=F32
-        )
+        product = jnp.dot(left[table[0, k]], wave[table[1, k]], preferred_element_type=F32)
+        before = jnp.where(table[3, k] == 0, 0.0, total[slot])
+        total[slot] = before + weights[k] * product
 
     def step(i, carry):
         for u in range(unroll):
@@ -275,9 +296,8 @@
             chunks[flip][HEAD + i * share : HEAD + (i + 1) * share] = slab.astype(kind)
 
 
-def apply_local(
-    table, weights, place, left, right, overlap, square, arrays, sectors, term_count
-):
+def apply_local(steps, place, left, right, overlap, square, arrays, sectors, term_count):
+    table, weights, used = steps
     slots = weights.shape[0]
     envs, size, _ = left.shape
     share = size // term_count
@@ -286,7 +306,7 @@
     return pl.pallas_call(
         functools.partial(apply_kernel, sectors, term_count, len(arrays), unroll),
         out_shape=[jax.ShapeDtypeStruct((HEAD + size // LANES * share, LANES), kind) for kind in kinds],
-        in_specs=[SCALARS] * 3 + [NEAR] * (4 + len(arrays)),
+        in_specs=[SCALARS] * 4 + [NEAR] * (4 + len(arrays)),
         out_specs=[NEAR] * term_count,
         scratch_shapes=[
             pltpu.VMEM((sectors, size, size), BF16),
@@ -301,7 +321,7 @@
             transcendentals=0,
         ),
         compiler_params=pltpu.CompilerParams(vmem_limit_bytes=18 << 20),
-    )(table, weights, place, left, right, overlap, square, *arrays)
+    )(table, weights, used, place, left, right, overlap, square, *arrays)
 
 
 def add_chunks(chunks, applied):
@@ -518,17 +538,18 @@
     normaliser = 1.0 / math.sqrt(term_count * triples.shape[0])
     current, previous, diagonal = x_start[0], x_prev[0], precond[0]
     rows, overlap, square = first(current)
-    table, weights = plan(
-        normaliser, triples.T, block_owner, trip_count, term_coef, place
+    steps = plan(
+        normaliser,
+        left_env.shape[0],
+        triples.T, block_owner, trip_count, term_coef, place
     )
     left, right = load(left_env, right_env)
     scale = jnp.ones((SUBLANES, LANES), F32)
     quotients = []
     for position in range(APPS):
-        arrays = gather(rows, sectors, term_count)
+        arrays = gather(rows, sectors, term_count, position > 0)
         chunks = apply_local(
-            table,
-            weights,
+            steps,
             place,
             left,
             right,

time: 189 us -> 189 us (level)
  starting transfers between devices: 58.7 us -> 74 us
  waiting for transfers between devices: 93.7 us -> 78.8 us
    ppermute x59 -> x71, waiting for transfers between devices: 90.1 us -> 75.3 us  [exchange(): return lax.ppermute(array, axis, [(i, i ^ flip) for i in range(count)])]
    ppermute x59 -> x71, starting transfers between devices: 53.7 us -> 68 us  [exchange(): return lax.ppermute(array, axis, [(i, i ^ flip) for i in range(count)])]
    unnamed x35 -> x37, local copies, waits for them, and re-layouts: 4.53 us -> 4.53 us
  transfers between devices with their start and end apart: 63 -> 75, of which waited for: 36 -> 43; matrix products, arithmetic and copies ran while one was open for 0% -> 0% of each run, Pallas kernels for 1% -> 1%
where the time goes in v3:
time: 189 us
  waiting for transfers between devices  78.8 us (42%)
  starting transfers between devices  74 us (39%)
  Pallas kernels  29.3 us (16%)
  local copies, waits for them, and re-layouts  4.67 us (2%)
  between operations  1.97 us (1%)
    ppermute x71, waiting for transfers between devices, exchange(): return lax.ppermute(array, axis, [(i, i ^ flip) for i in range(count)])  75.3 us
    ppermute x71, starting transfers between devices, exchange(): return lax.ppermute(array, axis, [(i, i ^ flip) for i in range(count)])  68 us
    pallas_call x3, Pallas kernels, apply_local(): pl.pallas_call(functools.partial(apply_kernel, sectors, term_count, len(a...  23.1 us
    ppermute x4, starting transfers between devices, exchange_by_core(): return lax.ppermute(array, ('sector', 'term'), pairs)  5.95 us
    unnamed x37, local copies, waits for them, and re-layouts  4.53 us
  transfers between devices with their start and end apart: 75, of which 43 were waited for; matrix products, arithmetic and copies ran while one was open for 0% of the time, Pallas kernels for 1%

profile of v3, /device:TPU:0, one launch (start us, length us, event | category | flops | bytes accessed | tf_op | source)
XLA Modules:
  0.0 188.9 jit_solution(10383545872543019104)
XLA Ops:
  1.6 3.1 %collective-permute-start = (bf16[96,384]{1,0:T(8,128)(2,1)S(1)}, bf16[96,384]{1,0:T(8,128)(2,1)S(1)}, u32[]{:S(2)}, u32[]{:S(2)}) collective-permute-start(bf16[96,384]{1,0:T(8,128)(2,1)S(1)} %get-tuple-element.49), channel_id=1, source_target_pairs={{0,1},{1,0},{2,3},{3,2},{4,5},{5,4},{6,7},{7,6},{8,9},{9,8},{10,11... | collective-permute-start | bytes 221192 | tf_op jit(solution)/shard_map/ppermute | solution.py:29
  4.7 2.6 %collective-permute-start.1 = (bf16[96,384]{1,0:T(8,128)(2,1)S(1)}, bf16[96,384]{1,0:T(8,128)(2,1)S(1)}, u32[]{:S(2)}, u32[]{:S(2)}) collective-permute-start(bf16[96,384]{1,0:T(8,128)(2,1)S(1)} %get-tuple-element.49), channel_id=1, source_target_pairs={{0,2},{1,3},{2,0},{3,1},{4,6},{5,7},{6,4},{7,5},{8,10},{9,11},{10,... | collective-permute-start | bytes 221192 | tf_op jit(solution)/shard_map/ppermute | solution.py:29
  7.3 1.7 collective-permute-start.3
  9.0 1.5 collective-permute-start.4
  10.9 1.6 collective-permute-done.1
  14.2 1.7 collective-permute-done.5
  16.8 2.7 %collective-permute-start.8 = (bf16[288,384]{1,0:T(8,128)(2,1)S(1)}, bf16[288,384]{1,0:T(8,128)(2,1)S(1)}, u32[]{:S(2)}, u32[]{:S(2)}) collective-permute-start(bf16[288,384]{1,0:T(8,128)(2,1)S(1)} %get-tuple-element.82), channel_id=1, source_target_pairs={{0,24},{4,28},{8,16},{12,20},{16,8},{20,12},{24,0},{28,4},{1,25},{... | collective-permute-start | bytes 663560 | tf_op jit(solution)/shard_map/ppermute | solution.py:29
  19.5 4.8 %collective-permute-done.6.rest_1_ = bf16[288,384]{1,0:T(8,128)(2,1)S(1)} collective-permute-done((bf16[288,384]{1,0:T(8,128)(2,1)S(1)}, bf16[288,384]{1,0:T(8,128)(2,1)S(1)}, u32[]{:S(2)}, u32[]{:S(2)}) %collective-permute-start.6) | collective-permute-done | bytes 221216 | tf_op jit(solution)/shard_map/ppermute | solution.py:29
  24.3 4.5 %collective-permute-done.7.rest_2_ = bf16[288,384]{1,0:T(8,128)(2,1)S(1)} collective-permute-done((bf16[288,384]{1,0:T(8,128)(2,1)S(1)}, bf16[288,384]{1,0:T(8,128)(2,1)S(1)}, u32[]{:S(2)}, u32[]{:S(2)}) %collective-permute-start.7) | collective-permute-done | bytes 221216 | tf_op jit(solution)/shard_map/ppermute | solution.py:29
  30.0 1.7 copy-done
  31.6 1.7 copy-done.1
  35.9 7.6 %apply_triples.3 = (f32[304,128]{1,0:T(8,128)S(1)}, bf16[304,128]{1,0:T(8,128)(2,1)S(1)}, bf16[304,128]{1,0:T(8,128)(2,1)S(1)}, bf16[304,128]{1,0:T(8,128)(2,1)S(1)}) custom-call(s32[4,20]{1,0:T(4,128)S(1)} %get-tuple-element.42.table, f32[20]{0:T(128)S(1)} %get-tuple-element.43.weights, s32[8]{0:T(128)S(1)} %get-tuple-element.44.used, ...), custom_call_target="tpu_custom_call" | custom-call | flops 4076863488 | bytes 7372800 | tf_op jit(solution)/shard_map/apply_triples/pallas_call | solution.py:306
  44.3 3.5 %collective-permute-start.14 = (bf16[304,128]{1,0:T(8,128)(2,1)S(1)}, bf16[304,128]{1,0:T(8,128)(2,1)S(1)}, u32[]{:S(2)}, u32[]{:S(2)}) collective-permute-start(bf16[304,128]{1,0:T(8,128)(2,1)S(1)} %get-tuple-element.52), channel_id=1, source_target_pairs={{0,2},{1,3},{2,0},{3,1},{4,6},{5,7},{6,4},{7,5},{8,10},{9,11},{10,... | collective-permute-start | bytes 233480 | tf_op jit(solution)/shard_map/ppermute | solution.py:29
  48.0 5.2 %collective-permute-done.14.rest_2_ = bf16[304,128]{1,0:T(8,128)(2,1)S(1)} collective-permute-done((bf16[304,128]{1,0:T(8,128)(2,1)S(1)}, bf16[304,128]{1,0:T(8,128)(2,1)S(1)}, u32[]{:S(2)}, u32[]{:S(2)}) %collective-permute-start.14) | collective-permute-done | bytes 77856 | tf_op jit(solution)/shard_map/ppermute | solution.py:29
  58.9 2.3 %collective-permute-done.17 = f32[8,128]{1,0:T(8,128)S(1)} collective-permute-done((f32[8,128]{1,0:T(8,128)S(1)}, f32[8,128]{1,0:T(8,128)S(1)}, u32[]{:S(2)}, u32[]{:S(2)}) %collective-permute-start.17) | collective-permute-done | bytes 4128 | tf_op jit(solution)/shard_map/ppermute | solution.py:29
  62.0 1.6 collective-permute-start.20
  63.6 1.6 collective-permute-start.21
  68.0 2.1 %collective-permute-start.25 = (bf16[96,384]{1,0:T(8,128)(2,1)S(1)}, bf16[96,384]{1,0:T(8,128)(2,1)S(1)}, u32[]{:S(2)}, u32[]{:S(2)}) collective-permute-start(bf16[96,384]{1,0:T(8,128)(2,1)S(1)} %get-tuple-element.59), channel_id=1, source_target_pairs={{0,24},{4,28},{8,16},{12,20},{16,8},{20,12},{24,0},{28,4},{1,25},{... | collective-permute-start | bytes 221192 | tf_op jit(solution)/shard_map/ppermute | solution.py:29
  71.6 1.7 collective-permute-done.25
  78.0 3.0 %collective-permute-done.29.rest_4_ = bf16[48,384]{1,0:T(8,128)(2,1)S(1)} collective-permute-done((bf16[48,384]{1,0:T(8,128)(2,1)S(1)}, bf16[48,384]{1,0:T(8,128)(2,1)S(1)}, u32[]{:S(2)}, u32[]{:S(2)}) %collective-permute-start.29) | collective-permute-done | bytes 36896 | tf_op jit(solution)/shard_map/ppermute | solution.py:29
  81.1 1.9 %collective-permute-start.30 = (bf16[48,384]{1,0:T(8,128)(2,1)S(1)}, bf16[48,384]{1,0:T(8,128)(2,1)S(1)}, u32[]{:S(2)}, u32[]{:S(2)}) collective-permute-start(bf16[48,384]{1,0:T(8,128)(2,1)S(1)} %pad_maximum_fusion.2), channel_id=1, source_target_pairs={{0,2},{1,3},{2,0},{3,1},{4,6},{5,7},{6,4},{7,5},{8,10},{9,11},{10,... | collective-permute-start | bytes 110600 | tf_op jit(solution)/shard_map/ppermute | solution.py:29
  83.0 2.3 %collective-permute-done.27.rest_2_ = bf16[240,384]{1,0:T(8,128)(2,1)S(1)} collective-permute-done((bf16[240,384]{1,0:T(8,128)(2,1)S(1)}, bf16[240,384]{1,0:T(8,128)(2,1)S(1)}, u32[]{:S(2)}, u32[]{:S(2)}) %collective-permute-start.27) | collective-permute-done | bytes 184352 | tf_op jit(solution)/shard_map/ppermute | solution.py:29
  85.9 2.5 %collective-permute-start.31 = (bf16[48,384]{1,0:T(8,128)(2,1)S(1)}, bf16[48,384]{1,0:T(8,128)(2,1)S(1)}, u32[]{:S(2)}, u32[]{:S(2)}) collective-permute-start(bf16[48,384]{1,0:T(8,128)(2,1)S(1)} %pad_maximum_fusion.2), channel_id=1, source_target_pairs={{0,3},{1,2},{2,1},{3,0},{4,7},{5,6},{6,5},{7,4},{8,11},{9,10},{10,... | collective-permute-start | bytes 110600 | tf_op jit(solution)/shard_map/ppermute | solution.py:29
  88.4 3.3 %collective-permute-done.31.rest_6_ = bf16[48,384]{1,0:T(8,128)(2,1)S(1)} collective-permute-done((bf16[48,384]{1,0:T(8,128)(2,1)S(1)}, bf16[48,384]{1,0:T(8,128)(2,1)S(1)}, u32[]{:S(2)}, u32[]{:S(2)}) %collective-permute-start.31) | collective-permute-done | bytes 36896 | tf_op jit(solution)/shard_map/ppermute | solution.py:29
  95.4 7.8 %apply_triples.4 = (f32[304,128]{1,0:T(8,128)S(1)}, bf16[304,128]{1,0:T(8,128)(2,1)S(1)}, bf16[304,128]{1,0:T(8,128)(2,1)S(1)}, bf16[304,128]{1,0:T(8,128)(2,1)S(1)}) custom-call(s32[4,20]{1,0:T(4,128)S(1)} %get-tuple-element.42.table, f32[20]{0:T(128)S(1)} %get-tuple-element.43.weights, s32[8]{0:T(128)S(1)} %get-tuple-element.44.used, ...), custom_call_target="tpu_custom_call" | custom-call | flops 4076863488 | bytes 7372800 | tf_op jit(solution)/shard_map/apply_triples/pallas_call | solution.py:306
  103.2 3.0 %collective-permute-start.40 = (bf16[304,128]{1,0:T(8,128)(2,1)S(1)}, bf16[304,128]{1,0:T(8,128)(2,1)S(1)}, u32[]{:S(2)}, u32[]{:S(2)}) collective-permute-start(bf16[304,128]{1,0:T(8,128)(2,1)S(1)} %get-tuple-element.62), channel_id=1, source_target_pairs={{0,2},{1,3},{2,0},{3,1},{4,6},{5,7},{6,4},{7,5},{8,10},{9,11},{10,... | collective-permute-start | bytes 233480 | tf_op jit(solution)/shard_map/ppermute | solution.py:29
  108.9 3.7 %collective-permute-done.40.rest_2_ = bf16[304,128]{1,0:T(8,128)(2,1)S(1)} collective-permute-done((bf16[304,128]{1,0:T(8,128)(2,1)S(1)}, bf16[304,128]{1,0:T(8,128)(2,1)S(1)}, u32[]{:S(2)}, u32[]{:S(2)}) %collective-permute-start.40) | collective-permute-done | bytes 77856 | tf_op jit(solution)/shard_map/ppermute | solution.py:29
  115.3 1.6 collective-permute-start.43
  117.5 2.3 %collective-permute-done.43 = f32[8,128]{1,0:T(8,128)S(1)} collective-permute-done((f32[8,128]{1,0:T(8,128)S(1)}, f32[8,128]{1,0:T(8,128)S(1)}, u32[]{:S(2)}, u32[]{:S(2)}) %collective-permute-start.43) | collective-permute-done | bytes 4128 | tf_op jit(solution)/shard_map/ppermute | solution.py:29
  120.5 1.8 collective-permute-start.46
  122.2 1.5 collective-permute-start.47
  125.5 1.5 collective-permute-start.50
  130.7 1.7 collective-permute-done.51
  132.5 1.5 collective-permute-start.52
  134.5 1.6 collective-permute-start.54
  137.0 3.2 %collective-permute-done.55.rest_4_ = bf16[48,384]{1,0:T(8,128)(2,1)S(1)} collective-permute-done((bf16[48,384]{1,0:T(8,128)(2,1)S(1)}, bf16[48,384]{1,0:T(8,128)(2,1)S(1)}, u32[]{:S(2)}, u32[]{:S(2)}) %collective-permute-start.55) | collective-permute-done | bytes 36896 | tf_op jit(solution)/shard_map/ppermute | solution.py:29
  140.1 1.7 collective-permute-start.56
  141.9 2.9 %collective-permute-done.53.rest_2_ = bf16[240,384]{1,0:T(8,128)(2,1)S(1)} collective-permute-done((bf16[240,384]{1,0:T(8,128)(2,1)S(1)}, bf16[240,384]{1,0:T(8,128)(2,1)S(1)}, u32[]{:S(2)}, u32[]{:S(2)}) %collective-permute-start.53) | collective-permute-done | bytes 184352 | tf_op jit(solution)/shard_map/ppermute | solution.py:29
  145.4 2.6 %collective-permute-start.57 = (bf16[48,384]{1,0:T(8,128)(2,1)S(1)}, bf16[48,384]{1,0:T(8,128)(2,1)S(1)}, u32[]{:S(2)}, u32[]{:S(2)}) collective-permute-start(bf16[48,384]{1,0:T(8,128)(2,1)S(1)} %pad_maximum_fusion.3), channel_id=1, source_target_pairs={{0,3},{1,2},{2,1},{3,0},{4,7},{5,6},{6,5},{7,4},{8,11},{9,10},{10,... | collective-permute-start | bytes 110600 | tf_op jit(solution)/shard_map/ppermute | solution.py:29
  148.0 3.1 %collective-permute-done.57.rest_6_ = bf16[48,384]{1,0:T(8,128)(2,1)S(1)} collective-permute-done((bf16[48,384]{1,0:T(8,128)(2,1)S(1)}, bf16[48,384]{1,0:T(8,128)(2,1)S(1)}, u32[]{:S(2)}, u32[]{:S(2)}) %collective-permute-start.57) | collective-permute-done | bytes 36896 | tf_op jit(solution)/shard_map/ppermute | solution.py:29
  154.8 7.8 %apply_triples.5 = (f32[304,128]{1,0:T(8,128)S(1)}, bf16[304,128]{1,0:T(8,128)(2,1)S(1)}, bf16[304,128]{1,0:T(8,128)(2,1)S(1)}, bf16[304,128]{1,0:T(8,128)(2,1)S(1)}) custom-call(s32[4,20]{1,0:T(4,128)S(1)} %get-tuple-element.42.table, f32[20]{0:T(128)S(1)} %get-tuple-element.43.weights, s32[8]{0:T(128)S(1)} %get-tuple-element.44.used, ...), custom_call_target="tpu_custom_call" | custom-call | flops 4076863488 | bytes 7372800 | tf_op jit(solution)/shard_map/apply_triples/pallas_call | solution.py:306
  162.7 3.2 %collective-permute-start.66 = (bf16[304,128]{1,0:T(8,128)(2,1)S(1)}, bf16[304,128]{1,0:T(8,128)(2,1)S(1)}, u32[]{:S(2)}, u32[]{:S(2)}) collective-permute-start(bf16[304,128]{1,0:T(8,128)(2,1)S(1)} %get-tuple-element.74), channel_id=1, source_target_pairs={{0,2},{1,3},{2,0},{3,1},{4,6},{5,7},{6,4},{7,5},{8,10},{9,11},{10,... | collective-permute-start | bytes 233480 | tf_op jit(solution)/shard_map/ppermute | solution.py:29
  168.3 3.9 %collective-permute-done.66.rest_2_ = bf16[304,128]{1,0:T(8,128)(2,1)S(1)} collective-permute-done((bf16[304,128]{1,0:T(8,128)(2,1)S(1)}, bf16[304,128]{1,0:T(8,128)(2,1)S(1)}, u32[]{:S(2)}, u32[]{:S(2)}) %collective-permute-start.66) | collective-permute-done | bytes 77856 | tf_op jit(solution)/shard_map/ppermute | solution.py:29
  176.3 1.6 collective-permute-done.70
  177.9 2.3 %collective-permute-done.69 = f32[8,128]{1,0:T(8,128)S(1)} collective-permute-done((f32[8,128]{1,0:T(8,128)S(1)}, f32[8,128]{1,0:T(8,128)S(1)}, u32[]{:S(2)}, u32[]{:S(2)}) %collective-permute-start.69) | collective-permute-done | bytes 4128 | tf_op jit(solution)/shard_map/ppermute | solution.py:29
  180.2 1.7 collective-permute-start.73
  181.9 2.4 %collective-permute-start.72 = (f32[8,128]{1,0:T(8,128)S(1)}, f32[8,128]{1,0:T(8,128)S(1)}, u32[]{:S(2)}, u32[]{:S(2)}) collective-permute-start(f32[8,128]{1,0:T(8,128)S(1)} %add_add_fusion.1), channel_id=1, source_target_pairs={{0,3},{1,2},{2,1},{3,0},{4,7},{5,6},{6,5},{7,4},{8,11},{9,10},{10,... | collective-permute-start | bytes 12296 | tf_op jit(solution)/shard_map/ppermute | solution.py:29
  184.3 3.0 %collective-permute-done.72 = f32[8,128]{1,0:T(8,128)S(1)} collective-permute-done((f32[8,128]{1,0:T(8,128)S(1)}, f32[8,128]{1,0:T(8,128)S(1)}, u32[]{:S(2)}, u32[]{:S(2)}) %collective-permute-start.72) | collective-permute-done | bytes 4128 | tf_op jit(solution)/shard_map/ppermute | solution.py:29
  (180 shorter events, 53.5 us)
Async XLA Ops:
  1.6 9.0 %collective-permute-start = (bf16[96,384]{1,0:T(8,128)(2,1)S(1)}, bf16[96,384]{1,0:T(8,128)(2,1)S(1)}, u32[]{:S(2)}, u32[]{:S(2)}) collective-permute-start(bf16[96,384]{1,0:T(8,128)(2,1)S(1)} %get-tuple-element.49), channel_id=1, source_target_pairs={{0,1},{1,0},{2,3},{3,2},{4,5},{5,4},{6,7},{7,6},{8,9},{9,8},{10,11... | collective-permute-start | bytes 221192 | tf_op jit(solution)/shard_map/ppermute | solution.py:29
  4.7 7.8 %collective-permute-start.1 = (bf16[96,384]{1,0:T(8,128)(2,1)S(1)}, bf16[96,384]{1,0:T(8,128)(2,1)S(1)}, u32[]{:S(2)}, u32[]{:S(2)}) collective-permute-start(bf16[96,384]{1,0:T(8,128)(2,1)S(1)} %get-tuple-element.49), channel_id=1, source_target_pairs={{0,2},{1,3},{2,0},{3,1},{4,6},{5,7},{6,4},{7,5},{8,10},{9,11},{10,... | collective-permute-start | bytes 221192 | tf_op jit(solution)/shard_map/ppermute | solution.py:29
  7.3 6.3 %collective-permute-start.2 = (bf16[96,384]{1,0:T(8,128)(2,1)S(1)}, bf16[96,384]{1,0:T(8,128)(2,1)S(1)}, u32[]{:S(2)}, u32[]{:S(2)}) collective-permute-start(bf16[96,384]{1,0:T(8,128)(2,1)S(1)} %get-tuple-element.49), channel_id=1, source_target_pairs={{0,3},{1,2},{2,1},{3,0},{4,7},{5,6},{6,5},{7,4},{8,11},{9,10},{10,... | collective-permute-start | bytes 221192 | tf_op jit(solution)/shard_map/ppermute | solution.py:29
  7.3 6.3 %collective-permute-start.3 = (bf16[96,384]{1,0:T(8,128)(2,1)S(1)}, bf16[96,384]{1,0:T(8,128)(2,1)S(1)}, u32[]{:S(2)}, u32[]{:S(2)}) collective-permute-start(bf16[96,384]{1,0:T(8,128)(2,1)S(1)} %get-tuple-element.49), channel_id=1, source_target_pairs={{0,8},{4,12},{8,0},{12,4},{16,24},{20,28},{24,16},{28,20},{1,9},{5... | collective-permute-start | bytes 221192 | tf_op jit(solution)/shard_map/ppermute | solution.py:29
  9.0 5.1 %collective-permute-start.4 = (bf16[96,384]{1,0:T(8,128)(2,1)S(1)}, bf16[96,384]{1,0:T(8,128)(2,1)S(1)}, u32[]{:S(2)}, u32[]{:S(2)}) collective-permute-start(bf16[96,384]{1,0:T(8,128)(2,1)S(1)} %get-tuple-element.49), channel_id=1, source_target_pairs={{0,16},{4,20},{8,24},{12,28},{16,0},{20,4},{24,8},{28,12},{1,17},{... | collective-permute-start | bytes 221192 | tf_op jit(solution)/shard_map/ppermute | solution.py:29
  10.5 5.3 %collective-permute-start.5 = (bf16[96,384]{1,0:T(8,128)(2,1)S(1)}, bf16[96,384]{1,0:T(8,128)(2,1)S(1)}, u32[]{:S(2)}, u32[]{:S(2)}) collective-permute-start(bf16[96,384]{1,0:T(8,128)(2,1)S(1)} %get-tuple-element.49), channel_id=1, source_target_pairs={{0,24},{4,28},{8,16},{12,20},{16,8},{20,12},{24,0},{28,4},{1,25},{... | collective-permute-start | bytes 221192 | tf_op jit(solution)/shard_map/ppermute | solution.py:29
  15.9 20.0 %collective-permute-start.9 = (bf16[672,384]{1,0:T(8,128)(2,1)S(1)}, bf16[672,384]{1,0:T(8,128)(2,1)S(1)}, u32[]{:S(2)}, u32[]{:S(2)}) collective-permute-start(bf16[672,384]{1,0:T(8,128)(2,1)S(1)} %constant_dynamic-update-slice_fusion.rest_0_), channel_id=1, source_target_pairs={{0,4},{4,0},{8,12},{12,8},{16,20},{20,16},{24,28},{28,24},{1,5},{5... | collective-permute-start | bytes 1548296 | tf_op jit(solution)/shard_map/ppermute | solution.py:29
  16.0 8.4 %collective-permute-start.6 = (bf16[288,384]{1,0:T(8,128)(2,1)S(1)}, bf16[288,384]{1,0:T(8,128)(2,1)S(1)}, u32[]{:S(2)}, u32[]{:S(2)}) collective-permute-start(bf16[288,384]{1,0:T(8,128)(2,1)S(1)} %get-tuple-element.82), channel_id=1, source_target_pairs={{0,8},{4,12},{8,0},{12,4},{16,24},{20,28},{24,16},{28,20},{1,9},{5... | collective-permute-start | bytes 663560 | tf_op jit(solution)/shard_map/ppermute | solution.py:29
  16.6 12.2 %collective-permute-start.7 = (bf16[288,384]{1,0:T(8,128)(2,1)S(1)}, bf16[288,384]{1,0:T(8,128)(2,1)S(1)}, u32[]{:S(2)}, u32[]{:S(2)}) collective-permute-start(bf16[288,384]{1,0:T(8,128)(2,1)S(1)} %get-tuple-element.82), channel_id=1, source_target_pairs={{0,16},{4,20},{8,24},{12,28},{16,0},{20,4},{24,8},{28,12},{1,17},{... | collective-permute-start | bytes 663560 | tf_op jit(solution)/shard_map/ppermute | solution.py:29
  16.8 11.9 %collective-permute-start.8 = (bf16[288,384]{1,0:T(8,128)(2,1)S(1)}, bf16[288,384]{1,0:T(8,128)(2,1)S(1)}, u32[]{:S(2)}, u32[]{:S(2)}) collective-permute-start(bf16[288,384]{1,0:T(8,128)(2,1)S(1)} %get-tuple-element.82), channel_id=1, source_target_pairs={{0,24},{4,28},{8,16},{12,20},{16,8},{20,12},{24,0},{28,4},{1,25},{... | collective-permute-start | bytes 663560 | tf_op jit(solution)/shard_map/ppermute | solution.py:29
  24.3 11.5 %collective-permute-start.10 = (bf16[288,384]{1,0:T(8,128)(2,1)S(1)}, bf16[288,384]{1,0:T(8,128)(2,1)S(1)}, u32[]{:S(2)}, u32[]{:S(2)}) collective-permute-start(bf16[288,384]{1,0:T(8,128)(2,1)S(1)} %collective-permute-done.6.rest_1_), channel_id=1, source_target_pairs={{0,4},{4,0},{8,12},{12,8},{16,20},{20,16},{24,28},{28,24},{1,5},{5... | collective-permute-start | bytes 663560 | tf_op jit(solution)/shard_map/ppermute | solution.py:29
  28.8 7.1 %collective-permute-start.11 = (bf16[288,384]{1,0:T(8,128)(2,1)S(1)}, bf16[288,384]{1,0:T(8,128)(2,1)S(1)}, u32[]{:S(2)}, u32[]{:S(2)}) collective-permute-start(bf16[288,384]{1,0:T(8,128)(2,1)S(1)} %collective-permute-done.7.rest_2_), channel_id=1, source_target_pairs={{0,4},{4,0},{8,12},{12,8},{16,20},{20,16},{24,28},{28,24},{1,5},{5... | collective-permute-start | bytes 663560 | tf_op jit(solution)/shard_map/ppermute | solution.py:29
  28.8 7.1 %collective-permute-start.12 = (bf16[288,384]{1,0:T(8,128)(2,1)S(1)}, bf16[288,384]{1,0:T(8,128)(2,1)S(1)}, u32[]{:S(2)}, u32[]{:S(2)}) collective-permute-start(bf16[288,384]{1,0:T(8,128)(2,1)S(1)} %collective-permute-done.8.rest_3_), channel_id=1, source_target_pairs={{0,4},{4,0},{8,12},{12,8},{16,20},{20,16},{24,28},{28,24},{1,5},{5... | collective-permute-start | bytes 663560 | tf_op jit(solution)/shard_map/ppermute | solution.py:29
  44.3 8.9 %collective-permute-start.14 = (bf16[304,128]{1,0:T(8,128)(2,1)S(1)}, bf16[304,128]{1,0:T(8,128)(2,1)S(1)}, u32[]{:S(2)}, u32[]{:S(2)}) collective-permute-start(bf16[304,128]{1,0:T(8,128)(2,1)S(1)} %get-tuple-element.52), channel_id=1, source_target_pairs={{0,2},{1,3},{2,0},{3,1},{4,6},{5,7},{6,4},{7,5},{8,10},{9,11},{10,... | collective-permute-start | bytes 233480 | tf_op jit(solution)/shard_map/ppermute | solution.py:29
  47.7 6.3 %collective-permute-start.15 = (bf16[304,128]{1,0:T(8,128)(2,1)S(1)}, bf16[304,128]{1,0:T(8,128)(2,1)S(1)}, u32[]{:S(2)}, u32[]{:S(2)}) collective-permute-start(bf16[304,128]{1,0:T(8,128)(2,1)S(1)} %get-tuple-element.53), channel_id=1, source_target_pairs={{0,3},{1,2},{2,1},{3,0},{4,7},{5,6},{6,5},{7,4},{8,11},{9,10},{10,... | collective-permute-start | bytes 233480 | tf_op jit(solution)/shard_map/ppermute | solution.py:29
  62.0 5.9 %collective-permute-start.20 = (bf16[96,384]{1,0:T(8,128)(2,1)S(1)}, bf16[96,384]{1,0:T(8,128)(2,1)S(1)}, u32[]{:S(2)}, u32[]{:S(2)}) collective-permute-start(bf16[96,384]{1,0:T(8,128)(2,1)S(1)} %get-tuple-element.59), channel_id=1, source_target_pairs={{0,1},{1,0},{2,3},{3,2},{4,5},{5,4},{6,7},{7,6},{8,9},{9,8},{10,11... | collective-permute-start | bytes 221192 | tf_op jit(solution)/shard_map/ppermute | solution.py:29
  63.6 6.9 %collective-permute-start.21 = (bf16[96,384]{1,0:T(8,128)(2,1)S(1)}, bf16[96,384]{1,0:T(8,128)(2,1)S(1)}, u32[]{:S(2)}, u32[]{:S(2)}) collective-permute-start(bf16[96,384]{1,0:T(8,128)(2,1)S(1)} %get-tuple-element.59), channel_id=1, source_target_pairs={{0,2},{1,3},{2,0},{3,1},{4,6},{5,7},{6,4},{7,5},{8,10},{9,11},{10,... | collective-permute-start | bytes 221192 | tf_op jit(solution)/shard_map/ppermute | solution.py:29
  65.2 6.3 %collective-permute-start.22 = (bf16[96,384]{1,0:T(8,128)(2,1)S(1)}, bf16[96,384]{1,0:T(8,128)(2,1)S(1)}, u32[]{:S(2)}, u32[]{:S(2)}) collective-permute-start(bf16[96,384]{1,0:T(8,128)(2,1)S(1)} %get-tuple-element.59), channel_id=1, source_target_pairs={{0,3},{1,2},{2,1},{3,0},{4,7},{5,6},{6,5},{7,4},{8,11},{9,10},{10,... | collective-permute-start | bytes 221192 | tf_op jit(solution)/shard_map/ppermute | solution.py:29
  68.0 5.3 %collective-permute-start.25 = (bf16[96,384]{1,0:T(8,128)(2,1)S(1)}, bf16[96,384]{1,0:T(8,128)(2,1)S(1)}, u32[]{:S(2)}, u32[]{:S(2)}) collective-permute-start(bf16[96,384]{1,0:T(8,128)(2,1)S(1)} %get-tuple-element.59), channel_id=1, source_target_pairs={{0,24},{4,28},{8,16},{12,20},{16,8},{20,12},{24,0},{28,4},{1,25},{... | collective-permute-start | bytes 221192 | tf_op jit(solution)/shard_map/ppermute | solution.py:29
  73.3 22.0 %collective-permute-start.32 = (bf16[672,384]{1,0:T(8,128)(2,1)S(1)}, bf16[672,384]{1,0:T(8,128)(2,1)S(1)}, u32[]{:S(2)}, u32[]{:S(2)}) collective-permute-start(bf16[672,384]{1,0:T(8,128)(2,1)S(1)} %constant_dynamic-update-slice_fusion.10.rest_0_), channel_id=1, source_target_pairs={{0,4},{4,0},{8,12},{12,8},{16,20},{20,16},{24,28},{28,24},{1,5},{5... | collective-permute-start | bytes 1548296 | tf_op jit(solution)/shard_map/ppermute | solution.py:29
  73.5 9.5 %collective-permute-start.26 = (bf16[240,384]{1,0:T(8,128)(2,1)S(1)}, bf16[240,384]{1,0:T(8,128)(2,1)S(1)}, u32[]{:S(2)}, u32[]{:S(2)}) collective-permute-start(bf16[240,384]{1,0:T(8,128)(2,1)S(1)} %pad_maximum_fusion), channel_id=1, source_target_pairs={{0,8},{4,12},{8,0},{12,4},{16,24},{20,28},{24,16},{28,20},{1,9},{5... | collective-permute-start | bytes 552968 | tf_op jit(solution)/shard_map/ppermute | solution.py:29
  74.6 10.7 %collective-permute-start.27 = (bf16[240,384]{1,0:T(8,128)(2,1)S(1)}, bf16[240,384]{1,0:T(8,128)(2,1)S(1)}, u32[]{:S(2)}, u32[]{:S(2)}) collective-permute-start(bf16[240,384]{1,0:T(8,128)(2,1)S(1)} %pad_maximum_fusion), channel_id=1, source_target_pairs={{0,16},{4,20},{8,24},{12,28},{16,0},{20,4},{24,8},{28,12},{1,17},{... | collective-permute-start | bytes 552968 | tf_op jit(solution)/shard_map/ppermute | solution.py:29
  76.1 9.2 %collective-permute-start.28 = (bf16[240,384]{1,0:T(8,128)(2,1)S(1)}, bf16[240,384]{1,0:T(8,128)(2,1)S(1)}, u32[]{:S(2)}, u32[]{:S(2)}) collective-permute-start(bf16[240,384]{1,0:T(8,128)(2,1)S(1)} %pad_maximum_fusion), channel_id=1, source_target_pairs={{0,24},{4,28},{8,16},{12,20},{16,8},{20,12},{24,0},{28,4},{1,25},{... | collective-permute-start | bytes 552968 | tf_op jit(solution)/shard_map/ppermute | solution.py:29
  83.0 12.3 %collective-permute-start.33 = (bf16[240,384]{1,0:T(8,128)(2,1)S(1)}, bf16[240,384]{1,0:T(8,128)(2,1)S(1)}, u32[]{:S(2)}, u32[]{:S(2)}) collective-permute-start(bf16[240,384]{1,0:T(8,128)(2,1)S(1)} %collective-permute-done.26.rest_1_), channel_id=1, source_target_pairs={{0,4},{4,0},{8,12},{12,8},{16,20},{20,16},{24,28},{28,24},{1,5},{5... | collective-permute-start | bytes 552968 | tf_op jit(solution)/shard_map/ppermute | solution.py:29
  85.3 10.0 %collective-permute-start.34 = (bf16[240,384]{1,0:T(8,128)(2,1)S(1)}, bf16[240,384]{1,0:T(8,128)(2,1)S(1)}, u32[]{:S(2)}, u32[]{:S(2)}) collective-permute-start(bf16[240,384]{1,0:T(8,128)(2,1)S(1)} %collective-permute-done.27.rest_2_), channel_id=1, source_target_pairs={{0,4},{4,0},{8,12},{12,8},{16,20},{20,16},{24,28},{28,24},{1,5},{5... | collective-permute-start | bytes 552968 | tf_op jit(solution)/shard_map/ppermute | solution.py:29
  85.3 10.0 %collective-permute-start.35 = (bf16[240,384]{1,0:T(8,128)(2,1)S(1)}, bf16[240,384]{1,0:T(8,128)(2,1)S(1)}, u32[]{:S(2)}, u32[]{:S(2)}) collective-permute-start(bf16[240,384]{1,0:T(8,128)(2,1)S(1)} %collective-permute-done.28.rest_3_), channel_id=1, source_target_pairs={{0,4},{4,0},{8,12},{12,8},{16,20},{20,16},{24,28},{28,24},{1,5},{5... | collective-permute-start | bytes 552968 | tf_op jit(solution)/shard_map/ppermute | solution.py:29
  85.9 5.8 %collective-permute-start.31 = (bf16[48,384]{1,0:T(8,128)(2,1)S(1)}, bf16[48,384]{1,0:T(8,128)(2,1)S(1)}, u32[]{:S(2)}, u32[]{:S(2)}) collective-permute-start(bf16[48,384]{1,0:T(8,128)(2,1)S(1)} %pad_maximum_fusion.2), channel_id=1, source_target_pairs={{0,3},{1,2},{2,1},{3,0},{4,7},{5,6},{6,5},{7,4},{8,11},{9,10},{10,... | collective-permute-start | bytes 110600 | tf_op jit(solution)/shard_map/ppermute | solution.py:29
  103.1 5.8 %collective-permute-start.39 = (bf16[304,128]{1,0:T(8,128)(2,1)S(1)}, bf16[304,128]{1,0:T(8,128)(2,1)S(1)}, u32[]{:S(2)}, u32[]{:S(2)}) collective-permute-start(bf16[304,128]{1,0:T(8,128)(2,1)S(1)} %get-tuple-element.61), channel_id=1, source_target_pairs={{0,1},{1,0},{2,3},{3,2},{4,5},{5,4},{6,7},{7,6},{8,9},{9,8},{10,11... | collective-permute-start | bytes 233480 | tf_op jit(solution)/shard_map/ppermute | solution.py:29
  103.2 9.4 %collective-permute-start.40 = (bf16[304,128]{1,0:T(8,128)(2,1)S(1)}, bf16[304,128]{1,0:T(8,128)(2,1)S(1)}, u32[]{:S(2)}, u32[]{:S(2)}) collective-permute-start(bf16[304,128]{1,0:T(8,128)(2,1)S(1)} %get-tuple-element.62), channel_id=1, source_target_pairs={{0,2},{1,3},{2,0},{3,1},{4,6},{5,7},{6,4},{7,5},{8,10},{9,11},{10,... | collective-permute-start | bytes 233480 | tf_op jit(solution)/shard_map/ppermute | solution.py:29
  106.3 6.3 %collective-permute-start.41 = (bf16[304,128]{1,0:T(8,128)(2,1)S(1)}, bf16[304,128]{1,0:T(8,128)(2,1)S(1)}, u32[]{:S(2)}, u32[]{:S(2)}) collective-permute-start(bf16[304,128]{1,0:T(8,128)(2,1)S(1)} %get-tuple-element.63), channel_id=1, source_target_pairs={{0,3},{1,2},{2,1},{3,0},{4,7},{5,6},{6,5},{7,4},{8,11},{9,10},{10,... | collective-permute-start | bytes 233480 | tf_op jit(solution)/shard_map/ppermute | solution.py:29
  120.5 6.6 %collective-permute-start.46 = (bf16[96,384]{1,0:T(8,128)(2,1)S(1)}, bf16[96,384]{1,0:T(8,128)(2,1)S(1)}, u32[]{:S(2)}, u32[]{:S(2)}) collective-permute-start(bf16[96,384]{1,0:T(8,128)(2,1)S(1)} %get-tuple-element.71), channel_id=1, source_target_pairs={{0,1},{1,0},{2,3},{3,2},{4,5},{5,4},{6,7},{7,6},{8,9},{9,8},{10,11... | collective-permute-start | bytes 221192 | tf_op jit(solution)/shard_map/ppermute | solution.py:29
  122.2 7.0 %collective-permute-start.47 = (bf16[96,384]{1,0:T(8,128)(2,1)S(1)}, bf16[96,384]{1,0:T(8,128)(2,1)S(1)}, u32[]{:S(2)}, u32[]{:S(2)}) collective-permute-start(bf16[96,384]{1,0:T(8,128)(2,1)S(1)} %get-tuple-element.71), channel_id=1, source_target_pairs={{0,2},{1,3},{2,0},{3,1},{4,6},{5,7},{6,4},{7,5},{8,10},{9,11},{10,... | collective-permute-start | bytes 221192 | tf_op jit(solution)/shard_map/ppermute | solution.py:29
  123.7 6.3 %collective-permute-start.48 = (bf16[96,384]{1,0:T(8,128)(2,1)S(1)}, bf16[96,384]{1,0:T(8,128)(2,1)S(1)}, u32[]{:S(2)}, u32[]{:S(2)}) collective-permute-start(bf16[96,384]{1,0:T(8,128)(2,1)S(1)} %get-tuple-element.71), channel_id=1, source_target_pairs={{0,3},{1,2},{2,1},{3,0},{4,7},{5,6},{6,5},{7,4},{8,11},{9,10},{10,... | collective-permute-start | bytes 221192 | tf_op jit(solution)/shard_map/ppermute | solution.py:29
  124.9 5.1 %collective-permute-start.49 = (bf16[96,384]{1,0:T(8,128)(2,1)S(1)}, bf16[96,384]{1,0:T(8,128)(2,1)S(1)}, u32[]{:S(2)}, u32[]{:S(2)}) collective-permute-start(bf16[96,384]{1,0:T(8,128)(2,1)S(1)} %get-tuple-element.71), channel_id=1, source_target_pairs={{0,8},{4,12},{8,0},{12,4},{16,24},{20,28},{24,16},{28,20},{1,9},{5... | collective-permute-start | bytes 221192 | tf_op jit(solution)/shard_map/ppermute | solution.py:29
  127.1 5.3 %collective-permute-start.51 = (bf16[96,384]{1,0:T(8,128)(2,1)S(1)}, bf16[96,384]{1,0:T(8,128)(2,1)S(1)}, u32[]{:S(2)}, u32[]{:S(2)}) collective-permute-start(bf16[96,384]{1,0:T(8,128)(2,1)S(1)} %get-tuple-element.71), channel_id=1, source_target_pairs={{0,24},{4,28},{8,16},{12,20},{16,8},{20,12},{24,0},{28,4},{1,25},{... | collective-permute-start | bytes 221192 | tf_op jit(solution)/shard_map/ppermute | solution.py:29
  132.4 22.4 %collective-permute-start.58 = (bf16[672,384]{1,0:T(8,128)(2,1)S(1)}, bf16[672,384]{1,0:T(8,128)(2,1)S(1)}, u32[]{:S(2)}, u32[]{:S(2)}) collective-permute-start(bf16[672,384]{1,0:T(8,128)(2,1)S(1)} %constant_dynamic-update-slice_fusion.17.rest_0_), channel_id=1, source_target_pairs={{0,4},{4,0},{8,12},{12,8},{16,20},{20,16},{24,28},{28,24},{1,5},{5... | collective-permute-start | bytes 1548296 | tf_op jit(solution)/shard_map/ppermute | solution.py:29
  132.5 9.3 %collective-permute-start.52 = (bf16[240,384]{1,0:T(8,128)(2,1)S(1)}, bf16[240,384]{1,0:T(8,128)(2,1)S(1)}, u32[]{:S(2)}, u32[]{:S(2)}) collective-permute-start(bf16[240,384]{1,0:T(8,128)(2,1)S(1)} %pad_maximum_fusion.1), channel_id=1, source_target_pairs={{0,8},{4,12},{8,0},{12,4},{16,24},{20,28},{24,16},{28,20},{1,9},{5... | collective-permute-start | bytes 552968 | tf_op jit(solution)/shard_map/ppermute | solution.py:29
  134.0 10.7 %collective-permute-start.53 = (bf16[240,384]{1,0:T(8,128)(2,1)S(1)}, bf16[240,384]{1,0:T(8,128)(2,1)S(1)}, u32[]{:S(2)}, u32[]{:S(2)}) collective-permute-start(bf16[240,384]{1,0:T(8,128)(2,1)S(1)} %pad_maximum_fusion.1), channel_id=1, source_target_pairs={{0,16},{4,20},{8,24},{12,28},{16,0},{20,4},{24,8},{28,12},{1,17},{... | collective-permute-start | bytes 552968 | tf_op jit(solution)/shard_map/ppermute | solution.py:29
  134.5 10.2 %collective-permute-start.54 = (bf16[240,384]{1,0:T(8,128)(2,1)S(1)}, bf16[240,384]{1,0:T(8,128)(2,1)S(1)}, u32[]{:S(2)}, u32[]{:S(2)}) collective-permute-start(bf16[240,384]{1,0:T(8,128)(2,1)S(1)} %pad_maximum_fusion.1), channel_id=1, source_target_pairs={{0,24},{4,28},{8,16},{12,20},{16,8},{20,12},{24,0},{28,4},{1,25},{... | collective-permute-start | bytes 552968 | tf_op jit(solution)/shard_map/ppermute | solution.py:29
  140.1 5.3 %collective-permute-start.56 = (bf16[48,384]{1,0:T(8,128)(2,1)S(1)}, bf16[48,384]{1,0:T(8,128)(2,1)S(1)}, u32[]{:S(2)}, u32[]{:S(2)}) collective-permute-start(bf16[48,384]{1,0:T(8,128)(2,1)S(1)} %pad_maximum_fusion.3), channel_id=1, source_target_pairs={{0,2},{1,3},{2,0},{3,1},{4,6},{5,7},{6,4},{7,5},{8,10},{9,11},{10,... | collective-permute-start | bytes 110600 | tf_op jit(solution)/shard_map/ppermute | solution.py:29
  141.9 12.9 %collective-permute-start.59 = (bf16[240,384]{1,0:T(8,128)(2,1)S(1)}, bf16[240,384]{1,0:T(8,128)(2,1)S(1)}, u32[]{:S(2)}, u32[]{:S(2)}) collective-permute-start(bf16[240,384]{1,0:T(8,128)(2,1)S(1)} %collective-permute-done.52.rest_1_), channel_id=1, source_target_pairs={{0,4},{4,0},{8,12},{12,8},{16,20},{20,16},{24,28},{28,24},{1,5},{5... | collective-permute-start | bytes 552968 | tf_op jit(solution)/shard_map/ppermute | solution.py:29
  144.7 10.1 %collective-permute-start.60 = (bf16[240,384]{1,0:T(8,128)(2,1)S(1)}, bf16[240,384]{1,0:T(8,128)(2,1)S(1)}, u32[]{:S(2)}, u32[]{:S(2)}) collective-permute-start(bf16[240,384]{1,0:T(8,128)(2,1)S(1)} %collective-permute-done.53.rest_2_), channel_id=1, source_target_pairs={{0,4},{4,0},{8,12},{12,8},{16,20},{20,16},{24,28},{28,24},{1,5},{5... | collective-permute-start | bytes 552968 | tf_op jit(solution)/shard_map/ppermute | solution.py:29
  144.7 10.1 %collective-permute-start.61 = (bf16[240,384]{1,0:T(8,128)(2,1)S(1)}, bf16[240,384]{1,0:T(8,128)(2,1)S(1)}, u32[]{:S(2)}, u32[]{:S(2)}) collective-permute-start(bf16[240,384]{1,0:T(8,128)(2,1)S(1)} %collective-permute-done.54.rest_3_), channel_id=1, source_target_pairs={{0,4},{4,0},{8,12},{12,8},{16,20},{20,16},{24,28},{28,24},{1,5},{5... | collective-permute-start | bytes 552968 | tf_op jit(solution)/shard_map/ppermute | solution.py:29
  145.4 5.8 %collective-permute-start.57 = (bf16[48,384]{1,0:T(8,128)(2,1)S(1)}, bf16[48,384]{1,0:T(8,128)(2,1)S(1)}, u32[]{:S(2)}, u32[]{:S(2)}) collective-permute-start(bf16[48,384]{1,0:T(8,128)(2,1)S(1)} %pad_maximum_fusion.3), channel_id=1, source_target_pairs={{0,3},{1,2},{2,1},{3,0},{4,7},{5,6},{6,5},{7,4},{8,11},{9,10},{10,... | collective-permute-start | bytes 110600 | tf_op jit(solution)/shard_map/ppermute | solution.py:29
  162.6 5.7 %collective-permute-start.65 = (bf16[304,128]{1,0:T(8,128)(2,1)S(1)}, bf16[304,128]{1,0:T(8,128)(2,1)S(1)}, u32[]{:S(2)}, u32[]{:S(2)}) collective-permute-start(bf16[304,128]{1,0:T(8,128)(2,1)S(1)} %get-tuple-element.73), channel_id=1, source_target_pairs={{0,1},{1,0},{2,3},{3,2},{4,5},{5,4},{6,7},{7,6},{8,9},{9,8},{10,11... | collective-permute-start | bytes 233480 | tf_op jit(solution)/shard_map/ppermute | solution.py:29
  162.7 9.5 %collective-permute-start.66 = (bf16[304,128]{1,0:T(8,128)(2,1)S(1)}, bf16[304,128]{1,0:T(8,128)(2,1)S(1)}, u32[]{:S(2)}, u32[]{:S(2)}) collective-permute-start(bf16[304,128]{1,0:T(8,128)(2,1)S(1)} %get-tuple-element.74), channel_id=1, source_target_pairs={{0,2},{1,3},{2,0},{3,1},{4,6},{5,7},{6,4},{7,5},{8,10},{9,11},{10,... | collective-permute-start | bytes 233480 | tf_op jit(solution)/shard_map/ppermute | solution.py:29
  165.9 6.3 %collective-permute-start.67 = (bf16[304,128]{1,0:T(8,128)(2,1)S(1)}, bf16[304,128]{1,0:T(8,128)(2,1)S(1)}, u32[]{:S(2)}, u32[]{:S(2)}) collective-permute-start(bf16[304,128]{1,0:T(8,128)(2,1)S(1)} %get-tuple-element.75), channel_id=1, source_target_pairs={{0,3},{1,2},{2,1},{3,0},{4,7},{5,6},{6,5},{7,4},{8,11},{9,10},{10,... | collective-permute-start | bytes 233480 | tf_op jit(solution)/shard_map/ppermute | solution.py:29
  181.9 5.4 %collective-permute-start.72 = (f32[8,128]{1,0:T(8,128)S(1)}, f32[8,128]{1,0:T(8,128)S(1)}, u32[]{:S(2)}, u32[]{:S(2)}) collective-permute-start(f32[8,128]{1,0:T(8,128)S(1)} %add_add_fusion.1), channel_id=1, source_target_pairs={{0,3},{1,2},{2,1},{3,0},{4,7},{5,6},{6,5},{7,4},{8,11},{9,10},{10,... | collective-permute-start | bytes 12296 | tf_op jit(solution)/shard_map/ppermute | solution.py:29
  (37 other events, 190.9 us)

commit v4 on v3

--- a/solution.py
+++ b/solution.py
@@ -103,7 +103,7 @@
             own += over_chips(main, sectors)[1:]
             if split:
                 tail = jnp.concatenate([array[cut:] for array in across])
-                own += over_term(tail, term_count)[1:]
+                own.append(jnp.concatenate(over_term(tail, term_count)[1:]))
     swapped = []
     for array in own:
         swapped.append(exchange(array, "sector", 1))
@@ -137,7 +137,8 @@
             for flip in range(1, term_count):
                 put(slot, flip, held[chip], flip - 1, cut)
                 if split:
-                    put(slot, flip, held[chips - 1 + flip], chip - 1, HEAD, cut)
+                    entry = (flip - 1) * (chips - 1) + chip - 1
+                    put(slot, flip, held[chips], entry, HEAD, cut)
 
 
 def fold(values):

time: 189 us -> 184 us (0.974)
  starting transfers between devices: 74 us -> 69.6 us
    ppermute x71 -> x67, starting transfers between devices: 68 us -> 64.3 us  [exchange(): return lax.ppermute(array, axis, [(i, i ^ flip) for i in range(count)])]
    ppermute x71 -> x67, waiting for transfers between devices: 75.3 us -> 74.8 us  [exchange(): return lax.ppermute(array, axis, [(i, i ^ flip) for i in range(count)])]
    unnamed x37 -> x41, local copies, waits for them, and re-layouts: 4.53 us -> 4.57 us
  transfers between devices with their start and end apart: 75 -> 71, of which waited for: 43 -> 34; matrix products, arithmetic and copies ran while one was open for 0% -> 0% of each run, Pallas kernels for 1% -> 1%
where the time goes in v4:
time: 184 us
  waiting for transfers between devices  78.3 us (43%)
  starting transfers between devices  69.6 us (38%)
  Pallas kernels  29.2 us (16%)
  local copies, waits for them, and re-layouts  4.73 us (3%)
  between operations  2.05 us (1%)
    ppermute x67, waiting for transfers between devices, exchange(): return lax.ppermute(array, axis, [(i, i ^ flip) for i in range(count)])  74.8 us
    ppermute x67, starting transfers between devices, exchange(): return lax.ppermute(array, axis, [(i, i ^ flip) for i in range(count)])  64.3 us
    pallas_call x3, Pallas kernels, apply_local(): pl.pallas_call(functools.partial(apply_kernel, sectors, term_count, len(a...  23.1 us
    ppermute x4, starting transfers between devices, exchange_by_core(): return lax.ppermute(array, ('sector', 'term'), pairs)  5.22 us
    unnamed x41, local copies, waits for them, and re-layouts  4.57 us
  transfers between devices with their start and end apart: 71, of which 34 were waited for; matrix products, arithmetic and copies ran while one was open for 0% of the time, Pallas kernels for 1%

profile of v4, /device:TPU:0, one launch (start us, length us, event | category | flops | bytes accessed | tf_op | source)
XLA Modules:
  0.0 184.1 jit_solution(9346738368456371056)
XLA Ops:
  1.6 3.1 %collective-permute-start = (bf16[96,384]{1,0:T(8,128)(2,1)S(1)}, bf16[96,384]{1,0:T(8,128)(2,1)S(1)}, u32[]{:S(2)}, u32[]{:S(2)}) collective-permute-start(bf16[96,384]{1,0:T(8,128)(2,1)S(1)} %get-tuple-element.49), channel_id=1, source_target_pairs={{0,1},{1,0},{2,3},{3,2},{4,5},{5,4},{6,7},{7,6},{8,9},{9,8},{10,11... | collective-permute-start | bytes 221192 | tf_op jit(solution)/shard_map/ppermute | solution.py:29
  4.7 2.6 %collective-permute-start.1 = (bf16[96,384]{1,0:T(8,128)(2,1)S(1)}, bf16[96,384]{1,0:T(8,128)(2,1)S(1)}, u32[]{:S(2)}, u32[]{:S(2)}) collective-permute-start(bf16[96,384]{1,0:T(8,128)(2,1)S(1)} %get-tuple-element.49), channel_id=1, source_target_pairs={{0,2},{1,3},{2,0},{3,1},{4,6},{5,7},{6,4},{7,5},{8,10},{9,11},{10,... | collective-permute-start | bytes 221192 | tf_op jit(solution)/shard_map/ppermute | solution.py:29
  7.3 1.7 collective-permute-start.3
  9.0 1.5 collective-permute-start.4
  10.9 1.6 collective-permute-done.1
  14.2 1.7 collective-permute-done.5
  16.8 2.7 %collective-permute-start.8 = (bf16[288,384]{1,0:T(8,128)(2,1)S(1)}, bf16[288,384]{1,0:T(8,128)(2,1)S(1)}, u32[]{:S(2)}, u32[]{:S(2)}) collective-permute-start(bf16[288,384]{1,0:T(8,128)(2,1)S(1)} %get-tuple-element.82), channel_id=1, source_target_pairs={{0,24},{4,28},{8,16},{12,20},{16,8},{20,12},{24,0},{28,4},{1,25},{... | collective-permute-start | bytes 663560 | tf_op jit(solution)/shard_map/ppermute | solution.py:29
  19.5 4.8 %collective-permute-done.6.rest_1_ = bf16[288,384]{1,0:T(8,128)(2,1)S(1)} collective-permute-done((bf16[288,384]{1,0:T(8,128)(2,1)S(1)}, bf16[288,384]{1,0:T(8,128)(2,1)S(1)}, u32[]{:S(2)}, u32[]{:S(2)}) %collective-permute-start.6) | collective-permute-done | bytes 221216 | tf_op jit(solution)/shard_map/ppermute | solution.py:29
  24.3 4.5 %collective-permute-done.7.rest_2_ = bf16[288,384]{1,0:T(8,128)(2,1)S(1)} collective-permute-done((bf16[288,384]{1,0:T(8,128)(2,1)S(1)}, bf16[288,384]{1,0:T(8,128)(2,1)S(1)}, u32[]{:S(2)}, u32[]{:S(2)}) %collective-permute-start.7) | collective-permute-done | bytes 221216 | tf_op jit(solution)/shard_map/ppermute | solution.py:29
  30.0 1.7 copy-done
  31.6 1.7 copy-done.1
  35.9 7.6 %apply_triples.3 = (f32[304,128]{1,0:T(8,128)S(1)}, bf16[304,128]{1,0:T(8,128)(2,1)S(1)}, bf16[304,128]{1,0:T(8,128)(2,1)S(1)}, bf16[304,128]{1,0:T(8,128)(2,1)S(1)}) custom-call(s32[4,20]{1,0:T(4,128)S(1)} %get-tuple-element.42.table, f32[20]{0:T(128)S(1)} %get-tuple-element.43.weights, s32[8]{0:T(128)S(1)} %get-tuple-element.44.used, ...), custom_call_target="tpu_custom_call" | custom-call | flops 4076863488 | bytes 7372800 | tf_op jit(solution)/shard_map/apply_triples/pallas_call | solution.py:307
  44.3 3.5 %collective-permute-start.14 = (bf16[304,128]{1,0:T(8,128)(2,1)S(1)}, bf16[304,128]{1,0:T(8,128)(2,1)S(1)}, u32[]{:S(2)}, u32[]{:S(2)}) collective-permute-start(bf16[304,128]{1,0:T(8,128)(2,1)S(1)} %get-tuple-element.52), channel_id=1, source_target_pairs={{0,2},{1,3},{2,0},{3,1},{4,6},{5,7},{6,4},{7,5},{8,10},{9,11},{10,... | collective-permute-start | bytes 233480 | tf_op jit(solution)/shard_map/ppermute | solution.py:29
  48.0 5.2 %collective-permute-done.14.rest_2_ = bf16[304,128]{1,0:T(8,128)(2,1)S(1)} collective-permute-done((bf16[304,128]{1,0:T(8,128)(2,1)S(1)}, bf16[304,128]{1,0:T(8,128)(2,1)S(1)}, u32[]{:S(2)}, u32[]{:S(2)}) %collective-permute-start.14) | collective-permute-done | bytes 77856 | tf_op jit(solution)/shard_map/ppermute | solution.py:29
  55.3 1.5 collective-permute-start.18
  58.9 2.3 %collective-permute-done.17 = f32[8,128]{1,0:T(8,128)S(1)} collective-permute-done((f32[8,128]{1,0:T(8,128)S(1)}, f32[8,128]{1,0:T(8,128)S(1)}, u32[]{:S(2)}, u32[]{:S(2)}) %collective-permute-start.17) | collective-permute-done | bytes 4128 | tf_op jit(solution)/shard_map/ppermute | solution.py:29
  62.0 1.6 collective-permute-start.20
  63.6 1.6 collective-permute-start.21
  66.6 2.1 %collective-permute-start.25 = (bf16[96,384]{1,0:T(8,128)(2,1)S(1)}, bf16[96,384]{1,0:T(8,128)(2,1)S(1)}, u32[]{:S(2)}, u32[]{:S(2)}) collective-permute-start(bf16[96,384]{1,0:T(8,128)(2,1)S(1)} %get-tuple-element.59), channel_id=1, source_target_pairs={{0,24},{4,28},{8,16},{12,20},{16,8},{20,12},{24,0},{28,4},{1,25},{... | collective-permute-start | bytes 221192 | tf_op jit(solution)/shard_map/ppermute | solution.py:29
  68.7 3.2 %collective-permute-done.25 = bf16[96,384]{1,0:T(8,128)(2,1)S(1)} collective-permute-done((bf16[96,384]{1,0:T(8,128)(2,1)S(1)}, bf16[96,384]{1,0:T(8,128)(2,1)S(1)}, u32[]{:S(2)}, u32[]{:S(2)}) %collective-permute-start.25) | collective-permute-done | bytes 73760 | tf_op jit(solution)/shard_map/ppermute | solution.py:29
  74.3 3.8 %collective-permute-done.22 = bf16[96,384]{1,0:T(8,128)(2,1)S(1)} collective-permute-done((bf16[96,384]{1,0:T(8,128)(2,1)S(1)}, bf16[96,384]{1,0:T(8,128)(2,1)S(1)}, u32[]{:S(2)}, u32[]{:S(2)}) %collective-permute-start.22) | collective-permute-done | bytes 73760 | tf_op jit(solution)/shard_map/ppermute | solution.py:29
  79.5 1.5 collective-permute-start.27
  82.5 4.7 %collective-permute-done.30 = bf16[48,384]{1,0:T(8,128)(2,1)S(1)} collective-permute-done((bf16[48,384]{1,0:T(8,128)(2,1)S(1)}, bf16[48,384]{1,0:T(8,128)(2,1)S(1)}, u32[]{:S(2)}, u32[]{:S(2)}) %collective-permute-start.30) | collective-permute-done | bytes 36896 | tf_op jit(solution)/shard_map/ppermute | solution.py:29
  88.6 1.6 collective-permute-done.27.rest_2_
  90.7 2.3 %collective-permute-done.31 = bf16[48,384]{1,0:T(8,128)(2,1)S(1)} collective-permute-done((bf16[48,384]{1,0:T(8,128)(2,1)S(1)}, bf16[48,384]{1,0:T(8,128)(2,1)S(1)}, u32[]{:S(2)}, u32[]{:S(2)}) %collective-permute-start.31) | collective-permute-done | bytes 36896 | tf_op jit(solution)/shard_map/ppermute | solution.py:29
  94.4 7.8 %apply_triples.4 = (f32[304,128]{1,0:T(8,128)S(1)}, bf16[304,128]{1,0:T(8,128)(2,1)S(1)}, bf16[304,128]{1,0:T(8,128)(2,1)S(1)}, bf16[304,128]{1,0:T(8,128)(2,1)S(1)}) custom-call(s32[4,20]{1,0:T(4,128)S(1)} %get-tuple-element.42.table, f32[20]{0:T(128)S(1)} %get-tuple-element.43.weights, s32[8]{0:T(128)S(1)} %get-tuple-element.44.used, ...), custom_call_target="tpu_custom_call" | custom-call | flops 4076863488 | bytes 7372800 | tf_op jit(solution)/shard_map/apply_triples/pallas_call | solution.py:307
  102.2 1.9 %collective-permute-start.38 = (bf16[304,128]{1,0:T(8,128)(2,1)S(1)}, bf16[304,128]{1,0:T(8,128)(2,1)S(1)}, u32[]{:S(2)}, u32[]{:S(2)}) collective-permute-start(bf16[304,128]{1,0:T(8,128)(2,1)S(1)} %get-tuple-element.62), channel_id=1, source_target_pairs={{0,2},{1,3},{2,0},{3,1},{4,6},{5,7},{6,4},{7,5},{8,10},{9,11},{10,... | collective-permute-start | bytes 233480 | tf_op jit(solution)/shard_map/ppermute | solution.py:29
  104.1 2.5 %collective-permute-start.39 = (bf16[304,128]{1,0:T(8,128)(2,1)S(1)}, bf16[304,128]{1,0:T(8,128)(2,1)S(1)}, u32[]{:S(2)}, u32[]{:S(2)}) collective-permute-start(bf16[304,128]{1,0:T(8,128)(2,1)S(1)} %get-tuple-element.63), channel_id=1, source_target_pairs={{0,3},{1,2},{2,1},{3,0},{4,7},{5,6},{6,5},{7,4},{8,11},{9,10},{10,... | collective-permute-start | bytes 233480 | tf_op jit(solution)/shard_map/ppermute | solution.py:29
  107.6 4.1 %collective-permute-done.38.rest_2_ = bf16[304,128]{1,0:T(8,128)(2,1)S(1)} collective-permute-done((bf16[304,128]{1,0:T(8,128)(2,1)S(1)}, bf16[304,128]{1,0:T(8,128)(2,1)S(1)}, u32[]{:S(2)}, u32[]{:S(2)}) %collective-permute-start.38) | collective-permute-done | bytes 77856 | tf_op jit(solution)/shard_map/ppermute | solution.py:29
  113.6 1.5 collective-permute-start.41
  115.1 1.5 collective-permute-done.42
  116.6 1.5 collective-permute-done.41
  118.8 1.5 collective-permute-start.44
  124.1 3.9 %collective-permute-done.49 = bf16[96,384]{1,0:T(8,128)(2,1)S(1)} collective-permute-done((bf16[96,384]{1,0:T(8,128)(2,1)S(1)}, bf16[96,384]{1,0:T(8,128)(2,1)S(1)}, u32[]{:S(2)}, u32[]{:S(2)}) %collective-permute-start.49) | collective-permute-done | bytes 73760 | tf_op jit(solution)/shard_map/ppermute | solution.py:29
  128.0 2.6 %collective-permute-start.46 = (bf16[96,384]{1,0:T(8,128)(2,1)S(1)}, bf16[96,384]{1,0:T(8,128)(2,1)S(1)}, u32[]{:S(2)}, u32[]{:S(2)}) collective-permute-start(bf16[96,384]{1,0:T(8,128)(2,1)S(1)} %get-tuple-element.71), channel_id=1, source_target_pairs={{0,3},{1,2},{2,1},{3,0},{4,7},{5,6},{6,5},{7,4},{8,11},{9,10},{10,... | collective-permute-start | bytes 221192 | tf_op jit(solution)/shard_map/ppermute | solution.py:29
  131.4 2.9 %collective-permute-done.46 = bf16[96,384]{1,0:T(8,128)(2,1)S(1)} collective-permute-done((bf16[96,384]{1,0:T(8,128)(2,1)S(1)}, bf16[96,384]{1,0:T(8,128)(2,1)S(1)}, u32[]{:S(2)}, u32[]{:S(2)}) %collective-permute-start.46) | collective-permute-done | bytes 73760 | tf_op jit(solution)/shard_map/ppermute | solution.py:29
  134.5 1.5 collective-permute-start.50
  136.5 1.6 collective-permute-start.52
  138.8 4.1 %collective-permute-done.54 = bf16[48,384]{1,0:T(8,128)(2,1)S(1)} collective-permute-done((bf16[48,384]{1,0:T(8,128)(2,1)S(1)}, bf16[48,384]{1,0:T(8,128)(2,1)S(1)}, u32[]{:S(2)}, u32[]{:S(2)}) %collective-permute-start.54) | collective-permute-done | bytes 36896 | tf_op jit(solution)/shard_map/ppermute | solution.py:29
  142.9 2.5 %collective-permute-start.55 = (bf16[48,384]{1,0:T(8,128)(2,1)S(1)}, bf16[48,384]{1,0:T(8,128)(2,1)S(1)}, u32[]{:S(2)}, u32[]{:S(2)}) collective-permute-start(bf16[48,384]{1,0:T(8,128)(2,1)S(1)} %pad_maximum_fusion.3), channel_id=1, source_target_pairs={{0,3},{1,2},{2,1},{3,0},{4,7},{5,6},{6,5},{7,4},{8,11},{9,10},{10,... | collective-permute-start | bytes 110600 | tf_op jit(solution)/shard_map/ppermute | solution.py:29
  147.2 1.5 collective-permute-done.55
  150.1 7.8 %apply_triples.5 = (f32[304,128]{1,0:T(8,128)S(1)}, bf16[304,128]{1,0:T(8,128)(2,1)S(1)}, bf16[304,128]{1,0:T(8,128)(2,1)S(1)}, bf16[304,128]{1,0:T(8,128)(2,1)S(1)}) custom-call(s32[4,20]{1,0:T(4,128)S(1)} %get-tuple-element.42.table, f32[20]{0:T(128)S(1)} %get-tuple-element.43.weights, s32[8]{0:T(128)S(1)} %get-tuple-element.44.used, ...), custom_call_target="tpu_custom_call" | custom-call | flops 4076863488 | bytes 7372800 | tf_op jit(solution)/shard_map/apply_triples/pallas_call | solution.py:307
  158.0 3.0 %collective-permute-start.62 = (bf16[304,128]{1,0:T(8,128)(2,1)S(1)}, bf16[304,128]{1,0:T(8,128)(2,1)S(1)}, u32[]{:S(2)}, u32[]{:S(2)}) collective-permute-start(bf16[304,128]{1,0:T(8,128)(2,1)S(1)} %get-tuple-element.74), channel_id=1, source_target_pairs={{0,2},{1,3},{2,0},{3,1},{4,6},{5,7},{6,4},{7,5},{8,10},{9,11},{10,... | collective-permute-start | bytes 233480 | tf_op jit(solution)/shard_map/ppermute | solution.py:29
  163.6 3.7 %collective-permute-done.62.rest_2_ = bf16[304,128]{1,0:T(8,128)(2,1)S(1)} collective-permute-done((bf16[304,128]{1,0:T(8,128)(2,1)S(1)}, bf16[304,128]{1,0:T(8,128)(2,1)S(1)}, u32[]{:S(2)}, u32[]{:S(2)}) %collective-permute-start.62) | collective-permute-done | bytes 77856 | tf_op jit(solution)/shard_map/ppermute | solution.py:29
  173.0 2.3 %collective-permute-done.65 = f32[8,128]{1,0:T(8,128)S(1)} collective-permute-done((f32[8,128]{1,0:T(8,128)S(1)}, f32[8,128]{1,0:T(8,128)S(1)}, u32[]{:S(2)}, u32[]{:S(2)}) %collective-permute-start.65) | collective-permute-done | bytes 4128 | tf_op jit(solution)/shard_map/ppermute | solution.py:29
  175.4 1.7 collective-permute-start.69
  177.1 2.4 %collective-permute-start.68 = (f32[8,128]{1,0:T(8,128)S(1)}, f32[8,128]{1,0:T(8,128)S(1)}, u32[]{:S(2)}, u32[]{:S(2)}) collective-permute-start(f32[8,128]{1,0:T(8,128)S(1)} %add_add_fusion.1), channel_id=1, source_target_pairs={{0,3},{1,2},{2,1},{3,0},{4,7},{5,6},{6,5},{7,4},{8,11},{9,10},{10,... | collective-permute-start | bytes 12296 | tf_op jit(solution)/shard_map/ppermute | solution.py:29
  179.5 3.0 %collective-permute-done.68 = f32[8,128]{1,0:T(8,128)S(1)} collective-permute-done((f32[8,128]{1,0:T(8,128)S(1)}, f32[8,128]{1,0:T(8,128)S(1)}, u32[]{:S(2)}, u32[]{:S(2)}) %collective-permute-start.68) | collective-permute-done | bytes 4128 | tf_op jit(solution)/shard_map/ppermute | solution.py:29
  (178 shorter events, 45.5 us)
Async XLA Ops:
  1.6 9.0 %collective-permute-start = (bf16[96,384]{1,0:T(8,128)(2,1)S(1)}, bf16[96,384]{1,0:T(8,128)(2,1)S(1)}, u32[]{:S(2)}, u32[]{:S(2)}) collective-permute-start(bf16[96,384]{1,0:T(8,128)(2,1)S(1)} %get-tuple-element.49), channel_id=1, source_target_pairs={{0,1},{1,0},{2,3},{3,2},{4,5},{5,4},{6,7},{7,6},{8,9},{9,8},{10,11... | collective-permute-start | bytes 221192 | tf_op jit(solution)/shard_map/ppermute | solution.py:29
  4.7 7.8 %collective-permute-start.1 = (bf16[96,384]{1,0:T(8,128)(2,1)S(1)}, bf16[96,384]{1,0:T(8,128)(2,1)S(1)}, u32[]{:S(2)}, u32[]{:S(2)}) collective-permute-start(bf16[96,384]{1,0:T(8,128)(2,1)S(1)} %get-tuple-element.49), channel_id=1, source_target_pairs={{0,2},{1,3},{2,0},{3,1},{4,6},{5,7},{6,4},{7,5},{8,10},{9,11},{10,... | collective-permute-start | bytes 221192 | tf_op jit(solution)/shard_map/ppermute | solution.py:29
  7.3 6.3 %collective-permute-start.2 = (bf16[96,384]{1,0:T(8,128)(2,1)S(1)}, bf16[96,384]{1,0:T(8,128)(2,1)S(1)}, u32[]{:S(2)}, u32[]{:S(2)}) collective-permute-start(bf16[96,384]{1,0:T(8,128)(2,1)S(1)} %get-tuple-element.49), channel_id=1, source_target_pairs={{0,3},{1,2},{2,1},{3,0},{4,7},{5,6},{6,5},{7,4},{8,11},{9,10},{10,... | collective-permute-start | bytes 221192 | tf_op jit(solution)/shard_map/ppermute | solution.py:29
  7.3 6.3 %collective-permute-start.3 = (bf16[96,384]{1,0:T(8,128)(2,1)S(1)}, bf16[96,384]{1,0:T(8,128)(2,1)S(1)}, u32[]{:S(2)}, u32[]{:S(2)}) collective-permute-start(bf16[96,384]{1,0:T(8,128)(2,1)S(1)} %get-tuple-element.49), channel_id=1, source_target_pairs={{0,8},{4,12},{8,0},{12,4},{16,24},{20,28},{24,16},{28,20},{1,9},{5... | collective-permute-start | bytes 221192 | tf_op jit(solution)/shard_map/ppermute | solution.py:29
  9.0 5.1 %collective-permute-start.4 = (bf16[96,384]{1,0:T(8,128)(2,1)S(1)}, bf16[96,384]{1,0:T(8,128)(2,1)S(1)}, u32[]{:S(2)}, u32[]{:S(2)}) collective-permute-start(bf16[96,384]{1,0:T(8,128)(2,1)S(1)} %get-tuple-element.49), channel_id=1, source_target_pairs={{0,16},{4,20},{8,24},{12,28},{16,0},{20,4},{24,8},{28,12},{1,17},{... | collective-permute-start | bytes 221192 | tf_op jit(solution)/shard_map/ppermute | solution.py:29
  10.5 5.3 %collective-permute-start.5 = (bf16[96,384]{1,0:T(8,128)(2,1)S(1)}, bf16[96,384]{1,0:T(8,128)(2,1)S(1)}, u32[]{:S(2)}, u32[]{:S(2)}) collective-permute-start(bf16[96,384]{1,0:T(8,128)(2,1)S(1)} %get-tuple-element.49), channel_id=1, source_target_pairs={{0,24},{4,28},{8,16},{12,20},{16,8},{20,12},{24,0},{28,4},{1,25},{... | collective-permute-start | bytes 221192 | tf_op jit(solution)/shard_map/ppermute | solution.py:29
  15.9 20.0 %collective-permute-start.9 = (bf16[672,384]{1,0:T(8,128)(2,1)S(1)}, bf16[672,384]{1,0:T(8,128)(2,1)S(1)}, u32[]{:S(2)}, u32[]{:S(2)}) collective-permute-start(bf16[672,384]{1,0:T(8,128)(2,1)S(1)} %constant_dynamic-update-slice_fusion.rest_0_), channel_id=1, source_target_pairs={{0,4},{4,0},{8,12},{12,8},{16,20},{20,16},{24,28},{28,24},{1,5},{5... | collective-permute-start | bytes 1548296 | tf_op jit(solution)/shard_map/ppermute | solution.py:29
  16.0 8.4 %collective-permute-start.6 = (bf16[288,384]{1,0:T(8,128)(2,1)S(1)}, bf16[288,384]{1,0:T(8,128)(2,1)S(1)}, u32[]{:S(2)}, u32[]{:S(2)}) collective-permute-start(bf16[288,384]{1,0:T(8,128)(2,1)S(1)} %get-tuple-element.82), channel_id=1, source_target_pairs={{0,8},{4,12},{8,0},{12,4},{16,24},{20,28},{24,16},{28,20},{1,9},{5... | collective-permute-start | bytes 663560 | tf_op jit(solution)/shard_map/ppermute | solution.py:29
  16.6 12.2 %collective-permute-start.7 = (bf16[288,384]{1,0:T(8,128)(2,1)S(1)}, bf16[288,384]{1,0:T(8,128)(2,1)S(1)}, u32[]{:S(2)}, u32[]{:S(2)}) collective-permute-start(bf16[288,384]{1,0:T(8,128)(2,1)S(1)} %get-tuple-element.82), channel_id=1, source_target_pairs={{0,16},{4,20},{8,24},{12,28},{16,0},{20,4},{24,8},{28,12},{1,17},{... | collective-permute-start | bytes 663560 | tf_op jit(solution)/shard_map/ppermute | solution.py:29
  16.8 11.9 %collective-permute-start.8 = (bf16[288,384]{1,0:T(8,128)(2,1)S(1)}, bf16[288,384]{1,0:T(8,128)(2,1)S(1)}, u32[]{:S(2)}, u32[]{:S(2)}) collective-permute-start(bf16[288,384]{1,0:T(8,128)(2,1)S(1)} %get-tuple-element.82), channel_id=1, source_target_pairs={{0,24},{4,28},{8,16},{12,20},{16,8},{20,12},{24,0},{28,4},{1,25},{... | collective-permute-start | bytes 663560 | tf_op jit(solution)/shard_map/ppermute | solution.py:29
  24.3 11.5 %collective-permute-start.10 = (bf16[288,384]{1,0:T(8,128)(2,1)S(1)}, bf16[288,384]{1,0:T(8,128)(2,1)S(1)}, u32[]{:S(2)}, u32[]{:S(2)}) collective-permute-start(bf16[288,384]{1,0:T(8,128)(2,1)S(1)} %collective-permute-done.6.rest_1_), channel_id=1, source_target_pairs={{0,4},{4,0},{8,12},{12,8},{16,20},{20,16},{24,28},{28,24},{1,5},{5... | collective-permute-start | bytes 663560 | tf_op jit(solution)/shard_map/ppermute | solution.py:29
  28.8 7.1 %collective-permute-start.11 = (bf16[288,384]{1,0:T(8,128)(2,1)S(1)}, bf16[288,384]{1,0:T(8,128)(2,1)S(1)}, u32[]{:S(2)}, u32[]{:S(2)}) collective-permute-start(bf16[288,384]{1,0:T(8,128)(2,1)S(1)} %collective-permute-done.7.rest_2_), channel_id=1, source_target_pairs={{0,4},{4,0},{8,12},{12,8},{16,20},{20,16},{24,28},{28,24},{1,5},{5... | collective-permute-start | bytes 663560 | tf_op jit(solution)/shard_map/ppermute | solution.py:29
  28.8 7.1 %collective-permute-start.12 = (bf16[288,384]{1,0:T(8,128)(2,1)S(1)}, bf16[288,384]{1,0:T(8,128)(2,1)S(1)}, u32[]{:S(2)}, u32[]{:S(2)}) collective-permute-start(bf16[288,384]{1,0:T(8,128)(2,1)S(1)} %collective-permute-done.8.rest_3_), channel_id=1, source_target_pairs={{0,4},{4,0},{8,12},{12,8},{16,20},{20,16},{24,28},{28,24},{1,5},{5... | collective-permute-start | bytes 663560 | tf_op jit(solution)/shard_map/ppermute | solution.py:29
  44.3 8.9 %collective-permute-start.14 = (bf16[304,128]{1,0:T(8,128)(2,1)S(1)}, bf16[304,128]{1,0:T(8,128)(2,1)S(1)}, u32[]{:S(2)}, u32[]{:S(2)}) collective-permute-start(bf16[304,128]{1,0:T(8,128)(2,1)S(1)} %get-tuple-element.52), channel_id=1, source_target_pairs={{0,2},{1,3},{2,0},{3,1},{4,6},{5,7},{6,4},{7,5},{8,10},{9,11},{10,... | collective-permute-start | bytes 233480 | tf_op jit(solution)/shard_map/ppermute | solution.py:29
  47.7 6.3 %collective-permute-start.15 = (bf16[304,128]{1,0:T(8,128)(2,1)S(1)}, bf16[304,128]{1,0:T(8,128)(2,1)S(1)}, u32[]{:S(2)}, u32[]{:S(2)}) collective-permute-start(bf16[304,128]{1,0:T(8,128)(2,1)S(1)} %get-tuple-element.53), channel_id=1, source_target_pairs={{0,3},{1,2},{2,1},{3,0},{4,7},{5,6},{6,5},{7,4},{8,11},{9,10},{10,... | collective-permute-start | bytes 233480 | tf_op jit(solution)/shard_map/ppermute | solution.py:29
  62.0 12.2 %collective-permute-start.20 = (bf16[96,384]{1,0:T(8,128)(2,1)S(1)}, bf16[96,384]{1,0:T(8,128)(2,1)S(1)}, u32[]{:S(2)}, u32[]{:S(2)}) collective-permute-start(bf16[96,384]{1,0:T(8,128)(2,1)S(1)} %get-tuple-element.59), channel_id=1, source_target_pairs={{0,1},{1,0},{2,3},{3,2},{4,5},{5,4},{6,7},{7,6},{8,9},{9,8},{10,11... | collective-permute-start | bytes 221192 | tf_op jit(solution)/shard_map/ppermute | solution.py:29
  63.6 10.6 %collective-permute-start.21 = (bf16[96,384]{1,0:T(8,128)(2,1)S(1)}, bf16[96,384]{1,0:T(8,128)(2,1)S(1)}, u32[]{:S(2)}, u32[]{:S(2)}) collective-permute-start(bf16[96,384]{1,0:T(8,128)(2,1)S(1)} %get-tuple-element.59), channel_id=1, source_target_pairs={{0,2},{1,3},{2,0},{3,1},{4,6},{5,7},{6,4},{7,5},{8,10},{9,11},{10,... | collective-permute-start | bytes 221192 | tf_op jit(solution)/shard_map/ppermute | solution.py:29
  65.2 8.0 %collective-permute-start.23 = (bf16[96,384]{1,0:T(8,128)(2,1)S(1)}, bf16[96,384]{1,0:T(8,128)(2,1)S(1)}, u32[]{:S(2)}, u32[]{:S(2)}) collective-permute-start(bf16[96,384]{1,0:T(8,128)(2,1)S(1)} %get-tuple-element.59), channel_id=1, source_target_pairs={{0,8},{4,12},{8,0},{12,4},{16,24},{20,28},{24,16},{28,20},{1,9},{5... | collective-permute-start | bytes 221192 | tf_op jit(solution)/shard_map/ppermute | solution.py:29
  65.8 7.4 %collective-permute-start.24 = (bf16[96,384]{1,0:T(8,128)(2,1)S(1)}, bf16[96,384]{1,0:T(8,128)(2,1)S(1)}, u32[]{:S(2)}, u32[]{:S(2)}) collective-permute-start(bf16[96,384]{1,0:T(8,128)(2,1)S(1)} %get-tuple-element.59), channel_id=1, source_target_pairs={{0,16},{4,20},{8,24},{12,28},{16,0},{20,4},{24,8},{28,12},{1,17},{... | collective-permute-start | bytes 221192 | tf_op jit(solution)/shard_map/ppermute | solution.py:29
  66.6 5.3 %collective-permute-start.25 = (bf16[96,384]{1,0:T(8,128)(2,1)S(1)}, bf16[96,384]{1,0:T(8,128)(2,1)S(1)}, u32[]{:S(2)}, u32[]{:S(2)}) collective-permute-start(bf16[96,384]{1,0:T(8,128)(2,1)S(1)} %get-tuple-element.59), channel_id=1, source_target_pairs={{0,24},{4,28},{8,16},{12,20},{16,8},{20,12},{24,0},{28,4},{1,25},{... | collective-permute-start | bytes 221192 | tf_op jit(solution)/shard_map/ppermute | solution.py:29
  71.9 6.3 %collective-permute-start.22 = (bf16[96,384]{1,0:T(8,128)(2,1)S(1)}, bf16[96,384]{1,0:T(8,128)(2,1)S(1)}, u32[]{:S(2)}, u32[]{:S(2)}) collective-permute-start(bf16[96,384]{1,0:T(8,128)(2,1)S(1)} %get-tuple-element.59), channel_id=1, source_target_pairs={{0,3},{1,2},{2,1},{3,0},{4,7},{5,6},{6,5},{7,4},{8,11},{9,10},{10,... | collective-permute-start | bytes 221192 | tf_op jit(solution)/shard_map/ppermute | solution.py:29
  73.3 8.7 %collective-permute-start.29 = (bf16[48,384]{1,0:T(8,128)(2,1)S(1)}, bf16[48,384]{1,0:T(8,128)(2,1)S(1)}, u32[]{:S(2)}, u32[]{:S(2)}) collective-permute-start(bf16[48,384]{1,0:T(8,128)(2,1)S(1)} %pad_maximum_fusion.2), channel_id=1, source_target_pairs={{0,1},{1,0},{2,3},{3,2},{4,5},{5,4},{6,7},{7,6},{8,9},{9,8},{10,11... | collective-permute-start | bytes 110600 | tf_op jit(solution)/shard_map/ppermute | solution.py:29
  78.2 16.1 %collective-permute-start.32 = (bf16[672,384]{1,0:T(8,128)(2,1)S(1)}, bf16[672,384]{1,0:T(8,128)(2,1)S(1)}, u32[]{:S(2)}, u32[]{:S(2)}) collective-permute-start(bf16[672,384]{1,0:T(8,128)(2,1)S(1)} %constant_dynamic-update-slice_fusion.10.rest_0_), channel_id=1, source_target_pairs={{0,4},{4,0},{8,12},{12,8},{16,20},{20,16},{24,28},{28,24},{1,5},{5... | collective-permute-start | bytes 1548296 | tf_op jit(solution)/shard_map/ppermute | solution.py:29
  78.4 10.2 %collective-permute-start.26 = (bf16[240,384]{1,0:T(8,128)(2,1)S(1)}, bf16[240,384]{1,0:T(8,128)(2,1)S(1)}, u32[]{:S(2)}, u32[]{:S(2)}) collective-permute-start(bf16[240,384]{1,0:T(8,128)(2,1)S(1)} %pad_maximum_fusion), channel_id=1, source_target_pairs={{0,8},{4,12},{8,0},{12,4},{16,24},{20,28},{24,16},{28,20},{1,9},{5... | collective-permute-start | bytes 552968 | tf_op jit(solution)/shard_map/ppermute | solution.py:29
  79.5 10.7 %collective-permute-start.27 = (bf16[240,384]{1,0:T(8,128)(2,1)S(1)}, bf16[240,384]{1,0:T(8,128)(2,1)S(1)}, u32[]{:S(2)}, u32[]{:S(2)}) collective-permute-start(bf16[240,384]{1,0:T(8,128)(2,1)S(1)} %pad_maximum_fusion), channel_id=1, source_target_pairs={{0,16},{4,20},{8,24},{12,28},{16,0},{20,4},{24,8},{28,12},{1,17},{... | collective-permute-start | bytes 552968 | tf_op jit(solution)/shard_map/ppermute | solution.py:29
  81.0 9.2 %collective-permute-start.28 = (bf16[240,384]{1,0:T(8,128)(2,1)S(1)}, bf16[240,384]{1,0:T(8,128)(2,1)S(1)}, u32[]{:S(2)}, u32[]{:S(2)}) collective-permute-start(bf16[240,384]{1,0:T(8,128)(2,1)S(1)} %pad_maximum_fusion), channel_id=1, source_target_pairs={{0,24},{4,28},{8,16},{12,20},{16,8},{20,12},{24,0},{28,4},{1,25},{... | collective-permute-start | bytes 552968 | tf_op jit(solution)/shard_map/ppermute | solution.py:29
  81.9 5.3 %collective-permute-start.30 = (bf16[48,384]{1,0:T(8,128)(2,1)S(1)}, bf16[48,384]{1,0:T(8,128)(2,1)S(1)}, u32[]{:S(2)}, u32[]{:S(2)}) collective-permute-start(bf16[48,384]{1,0:T(8,128)(2,1)S(1)} %pad_maximum_fusion.2), channel_id=1, source_target_pairs={{0,2},{1,3},{2,0},{3,1},{4,6},{5,7},{6,4},{7,5},{8,10},{9,11},{10,... | collective-permute-start | bytes 110600 | tf_op jit(solution)/shard_map/ppermute | solution.py:29
  87.2 5.8 %collective-permute-start.31 = (bf16[48,384]{1,0:T(8,128)(2,1)S(1)}, bf16[48,384]{1,0:T(8,128)(2,1)S(1)}, u32[]{:S(2)}, u32[]{:S(2)}) collective-permute-start(bf16[48,384]{1,0:T(8,128)(2,1)S(1)} %pad_maximum_fusion.2), channel_id=1, source_target_pairs={{0,3},{1,2},{2,1},{3,0},{4,7},{5,6},{6,5},{7,4},{8,11},{9,10},{10,... | collective-permute-start | bytes 110600 | tf_op jit(solution)/shard_map/ppermute | solution.py:29
  88.5 5.8 %collective-permute-start.33 = (bf16[240,384]{1,0:T(8,128)(2,1)S(1)}, bf16[240,384]{1,0:T(8,128)(2,1)S(1)}, u32[]{:S(2)}, u32[]{:S(2)}) collective-permute-start(bf16[240,384]{1,0:T(8,128)(2,1)S(1)} %collective-permute-done.26.rest_1_), channel_id=1, source_target_pairs={{0,4},{4,0},{8,12},{12,8},{16,20},{20,16},{24,28},{28,24},{1,5},{5... | collective-permute-start | bytes 552968 | tf_op jit(solution)/shard_map/ppermute | solution.py:29
  102.1 5.5 %collective-permute-start.37 = (bf16[304,128]{1,0:T(8,128)(2,1)S(1)}, bf16[304,128]{1,0:T(8,128)(2,1)S(1)}, u32[]{:S(2)}, u32[]{:S(2)}) collective-permute-start(bf16[304,128]{1,0:T(8,128)(2,1)S(1)} %get-tuple-element.61), channel_id=1, source_target_pairs={{0,1},{1,0},{2,3},{3,2},{4,5},{5,4},{6,7},{7,6},{8,9},{9,8},{10,11... | collective-permute-start | bytes 233480 | tf_op jit(solution)/shard_map/ppermute | solution.py:29
  102.2 9.5 %collective-permute-start.38 = (bf16[304,128]{1,0:T(8,128)(2,1)S(1)}, bf16[304,128]{1,0:T(8,128)(2,1)S(1)}, u32[]{:S(2)}, u32[]{:S(2)}) collective-permute-start(bf16[304,128]{1,0:T(8,128)(2,1)S(1)} %get-tuple-element.62), channel_id=1, source_target_pairs={{0,2},{1,3},{2,0},{3,1},{4,6},{5,7},{6,4},{7,5},{8,10},{9,11},{10,... | collective-permute-start | bytes 233480 | tf_op jit(solution)/shard_map/ppermute | solution.py:29
  104.1 7.6 %collective-permute-start.39 = (bf16[304,128]{1,0:T(8,128)(2,1)S(1)}, bf16[304,128]{1,0:T(8,128)(2,1)S(1)}, u32[]{:S(2)}, u32[]{:S(2)}) collective-permute-start(bf16[304,128]{1,0:T(8,128)(2,1)S(1)} %get-tuple-element.63), channel_id=1, source_target_pairs={{0,3},{1,2},{2,1},{3,0},{4,7},{5,6},{6,5},{7,4},{8,11},{9,10},{10,... | collective-permute-start | bytes 233480 | tf_op jit(solution)/shard_map/ppermute | solution.py:29
  118.8 12.5 %collective-permute-start.44 = (bf16[96,384]{1,0:T(8,128)(2,1)S(1)}, bf16[96,384]{1,0:T(8,128)(2,1)S(1)}, u32[]{:S(2)}, u32[]{:S(2)}) collective-permute-start(bf16[96,384]{1,0:T(8,128)(2,1)S(1)} %get-tuple-element.71), channel_id=1, source_target_pairs={{0,1},{1,0},{2,3},{3,2},{4,5},{5,4},{6,7},{7,6},{8,9},{9,8},{10,11... | collective-permute-start | bytes 221192 | tf_op jit(solution)/shard_map/ppermute | solution.py:29
  120.3 11.0 %collective-permute-start.45 = (bf16[96,384]{1,0:T(8,128)(2,1)S(1)}, bf16[96,384]{1,0:T(8,128)(2,1)S(1)}, u32[]{:S(2)}, u32[]{:S(2)}) collective-permute-start(bf16[96,384]{1,0:T(8,128)(2,1)S(1)} %get-tuple-element.71), channel_id=1, source_target_pairs={{0,2},{1,3},{2,0},{3,1},{4,6},{5,7},{6,4},{7,5},{8,10},{9,11},{10,... | collective-permute-start | bytes 221192 | tf_op jit(solution)/shard_map/ppermute | solution.py:29
  120.6 10.0 %collective-permute-start.47 = (bf16[96,384]{1,0:T(8,128)(2,1)S(1)}, bf16[96,384]{1,0:T(8,128)(2,1)S(1)}, u32[]{:S(2)}, u32[]{:S(2)}) collective-permute-start(bf16[96,384]{1,0:T(8,128)(2,1)S(1)} %get-tuple-element.71), channel_id=1, source_target_pairs={{0,8},{4,12},{8,0},{12,4},{16,24},{20,28},{24,16},{28,20},{1,9},{5... | collective-permute-start | bytes 221192 | tf_op jit(solution)/shard_map/ppermute | solution.py:29
  122.0 8.6 %collective-permute-start.48 = (bf16[96,384]{1,0:T(8,128)(2,1)S(1)}, bf16[96,384]{1,0:T(8,128)(2,1)S(1)}, u32[]{:S(2)}, u32[]{:S(2)}) collective-permute-start(bf16[96,384]{1,0:T(8,128)(2,1)S(1)} %get-tuple-element.71), channel_id=1, source_target_pairs={{0,16},{4,20},{8,24},{12,28},{16,0},{20,4},{24,8},{28,12},{1,17},{... | collective-permute-start | bytes 221192 | tf_op jit(solution)/shard_map/ppermute | solution.py:29
  122.8 5.3 %collective-permute-start.49 = (bf16[96,384]{1,0:T(8,128)(2,1)S(1)}, bf16[96,384]{1,0:T(8,128)(2,1)S(1)}, u32[]{:S(2)}, u32[]{:S(2)}) collective-permute-start(bf16[96,384]{1,0:T(8,128)(2,1)S(1)} %get-tuple-element.71), channel_id=1, source_target_pairs={{0,24},{4,28},{8,16},{12,20},{16,8},{20,12},{24,0},{28,4},{1,25},{... | collective-permute-start | bytes 221192 | tf_op jit(solution)/shard_map/ppermute | solution.py:29
  128.0 6.2 %collective-permute-start.46 = (bf16[96,384]{1,0:T(8,128)(2,1)S(1)}, bf16[96,384]{1,0:T(8,128)(2,1)S(1)}, u32[]{:S(2)}, u32[]{:S(2)}) collective-permute-start(bf16[96,384]{1,0:T(8,128)(2,1)S(1)} %get-tuple-element.71), channel_id=1, source_target_pairs={{0,3},{1,2},{2,1},{3,0},{4,7},{5,6},{6,5},{7,4},{8,11},{9,10},{10,... | collective-permute-start | bytes 221192 | tf_op jit(solution)/shard_map/ppermute | solution.py:29
  130.6 7.4 %collective-permute-start.53 = (bf16[48,384]{1,0:T(8,128)(2,1)S(1)}, bf16[48,384]{1,0:T(8,128)(2,1)S(1)}, u32[]{:S(2)}, u32[]{:S(2)}) collective-permute-start(bf16[48,384]{1,0:T(8,128)(2,1)S(1)} %pad_maximum_fusion.3), channel_id=1, source_target_pairs={{0,1},{1,0},{2,3},{3,2},{4,5},{5,4},{6,7},{7,6},{8,9},{9,8},{10,11... | collective-permute-start | bytes 110600 | tf_op jit(solution)/shard_map/ppermute | solution.py:29
  134.3 15.7 %collective-permute-start.56 = (bf16[672,384]{1,0:T(8,128)(2,1)S(1)}, bf16[672,384]{1,0:T(8,128)(2,1)S(1)}, u32[]{:S(2)}, u32[]{:S(2)}) collective-permute-start(bf16[672,384]{1,0:T(8,128)(2,1)S(1)} %constant_dynamic-update-slice_fusion.20.rest_0_), channel_id=1, source_target_pairs={{0,4},{4,0},{8,12},{12,8},{16,20},{20,16},{24,28},{28,24},{1,5},{5... | collective-permute-start | bytes 1548296 | tf_op jit(solution)/shard_map/ppermute | solution.py:29
  134.5 10.9 %collective-permute-start.50 = (bf16[240,384]{1,0:T(8,128)(2,1)S(1)}, bf16[240,384]{1,0:T(8,128)(2,1)S(1)}, u32[]{:S(2)}, u32[]{:S(2)}) collective-permute-start(bf16[240,384]{1,0:T(8,128)(2,1)S(1)} %pad_maximum_fusion.1), channel_id=1, source_target_pairs={{0,8},{4,12},{8,0},{12,4},{16,24},{20,28},{24,16},{28,20},{1,9},{5... | collective-permute-start | bytes 552968 | tf_op jit(solution)/shard_map/ppermute | solution.py:29
  136.0 10.7 %collective-permute-start.51 = (bf16[240,384]{1,0:T(8,128)(2,1)S(1)}, bf16[240,384]{1,0:T(8,128)(2,1)S(1)}, u32[]{:S(2)}, u32[]{:S(2)}) collective-permute-start(bf16[240,384]{1,0:T(8,128)(2,1)S(1)} %pad_maximum_fusion.1), channel_id=1, source_target_pairs={{0,16},{4,20},{8,24},{12,28},{16,0},{20,4},{24,8},{28,12},{1,17},{... | collective-permute-start | bytes 552968 | tf_op jit(solution)/shard_map/ppermute | solution.py:29
  136.5 10.2 %collective-permute-start.52 = (bf16[240,384]{1,0:T(8,128)(2,1)S(1)}, bf16[240,384]{1,0:T(8,128)(2,1)S(1)}, u32[]{:S(2)}, u32[]{:S(2)}) collective-permute-start(bf16[240,384]{1,0:T(8,128)(2,1)S(1)} %pad_maximum_fusion.1), channel_id=1, source_target_pairs={{0,24},{4,28},{8,16},{12,20},{16,8},{20,12},{24,0},{28,4},{1,25},{... | collective-permute-start | bytes 552968 | tf_op jit(solution)/shard_map/ppermute | solution.py:29
  142.9 5.8 %collective-permute-start.55 = (bf16[48,384]{1,0:T(8,128)(2,1)S(1)}, bf16[48,384]{1,0:T(8,128)(2,1)S(1)}, u32[]{:S(2)}, u32[]{:S(2)}) collective-permute-start(bf16[48,384]{1,0:T(8,128)(2,1)S(1)} %pad_maximum_fusion.3), channel_id=1, source_target_pairs={{0,3},{1,2},{2,1},{3,0},{4,7},{5,6},{6,5},{7,4},{8,11},{9,10},{10,... | collective-permute-start | bytes 110600 | tf_op jit(solution)/shard_map/ppermute | solution.py:29
  157.9 5.7 %collective-permute-start.61 = (bf16[304,128]{1,0:T(8,128)(2,1)S(1)}, bf16[304,128]{1,0:T(8,128)(2,1)S(1)}, u32[]{:S(2)}, u32[]{:S(2)}) collective-permute-start(bf16[304,128]{1,0:T(8,128)(2,1)S(1)} %get-tuple-element.73), channel_id=1, source_target_pairs={{0,1},{1,0},{2,3},{3,2},{4,5},{5,4},{6,7},{7,6},{8,9},{9,8},{10,11... | collective-permute-start | bytes 233480 | tf_op jit(solution)/shard_map/ppermute | solution.py:29
  158.0 9.4 %collective-permute-start.62 = (bf16[304,128]{1,0:T(8,128)(2,1)S(1)}, bf16[304,128]{1,0:T(8,128)(2,1)S(1)}, u32[]{:S(2)}, u32[]{:S(2)}) collective-permute-start(bf16[304,128]{1,0:T(8,128)(2,1)S(1)} %get-tuple-element.74), channel_id=1, source_target_pairs={{0,2},{1,3},{2,0},{3,1},{4,6},{5,7},{6,4},{7,5},{8,10},{9,11},{10,... | collective-permute-start | bytes 233480 | tf_op jit(solution)/shard_map/ppermute | solution.py:29
  161.0 6.3 %collective-permute-start.63 = (bf16[304,128]{1,0:T(8,128)(2,1)S(1)}, bf16[304,128]{1,0:T(8,128)(2,1)S(1)}, u32[]{:S(2)}, u32[]{:S(2)}) collective-permute-start(bf16[304,128]{1,0:T(8,128)(2,1)S(1)} %get-tuple-element.75), channel_id=1, source_target_pairs={{0,3},{1,2},{2,1},{3,0},{4,7},{5,6},{6,5},{7,4},{8,11},{9,10},{10,... | collective-permute-start | bytes 233480 | tf_op jit(solution)/shard_map/ppermute | solution.py:29
  177.1 5.4 %collective-permute-start.68 = (f32[8,128]{1,0:T(8,128)S(1)}, f32[8,128]{1,0:T(8,128)S(1)}, u32[]{:S(2)}, u32[]{:S(2)}) collective-permute-start(f32[8,128]{1,0:T(8,128)S(1)} %add_add_fusion.1), channel_id=1, source_target_pairs={{0,3},{1,2},{2,1},{3,0},{4,7},{5,6},{6,5},{7,4},{8,11},{9,10},{10,... | collective-permute-start | bytes 12296 | tf_op jit(solution)/shard_map/ppermute | solution.py:29
  (33 other events, 182.8 us)
